TPU v7x, 32 devices: a whole 2x2x4 slice. The times are simulated.
32 devices in a mesh: shard: 2 (over core), ctx: 4 (over y, x), tp: 4 (over z).
Axes of the slice: x: 2, y: 2, z: 4, core: 2. Of those that a mesh axis runs over, the one named last changes fastest.
Arguments:
- hidden_in: bfloat16 [2, 1024, 640], P('shard', ('ctx', 'tp')), may hold values from -6 to 6
- positions: int32 [2, 1024], P('shard', 'ctx'), may hold values from 0 to 1023, as said below
- cotangent: bfloat16 [2, 1024, 640], P('shard', ('ctx', 'tp')), may hold values from -6 to 6
- input_gain: bfloat16 [640], P('shard'), may hold values from 0.5 to 1.5
- query_weight: bfloat16 [640, 1024], P('shard', 'tp'), may hold values from -0.25 to 0.25
- key_weight: bfloat16 [640, 256], P('shard'), may hold values from -0.25 to 0.25
- value_weight: bfloat16 [640, 256], P('shard'), may hold values from -0.25 to 0.25
- query_gain: bfloat16 [256], P('shard'), may hold values from 0.5 to 1.5
- key_gain: bfloat16 [256], P('shard'), may hold values from 0.5 to 1.5
- out_weight: bfloat16 [1024, 640], P('tp', 'shard'), may hold values from -0.1875 to 0.1875
- attn_post_gain: bfloat16 [640], P('shard'), may hold values from 0.5 to 1.5
- ffn_pre_gain: bfloat16 [640], P('shard'), may hold values from 0.5 to 1.5
- gate_weight: bfloat16 [640, 2048], P('shard', 'tp'), may hold values from -0.25 to 0.25
- up_weight: bfloat16 [640, 2048], P('shard', 'tp'), may hold values from -0.25 to 0.25
- down_weight: bfloat16 [2048, 640], P('tp', 'shard'), may hold values from -0.125 to 0.125
- ffn_post_gain: bfloat16 [640], P('shard'), may hold values from 0.5 to 1.5
Outputs:
- block_out: float32 [2, 1024, 640], P('shard', ('ctx', 'tp'))
- hidden_grad: float32 [2, 1024, 640], P('shard', ('ctx', 'tp'))
- input_gain_grad: float32 [640], P('shard')
- query_weight_grad: float32 [640, 1024], P('shard', 'tp')
- key_weight_grad: float32 [640, 256], P('shard')
- value_weight_grad: float32 [640, 256], P('shard')
- query_gain_grad: float32 [256], P('shard')
- key_gain_grad: float32 [256], P('shard')
- out_weight_grad: float32 [1024, 640], P('tp', 'shard')
- attn_post_gain_grad: float32 [640], P('shard')
- ffn_pre_gain_grad: float32 [640], P('shard')
- gate_weight_grad: float32 [640, 2048], P('shard', 'tp')
- up_weight_grad: float32 [640, 2048], P('shard', 'tp')
- down_weight_grad: float32 [2048, 640], P('tp', 'shard')
- ffn_post_gain_grad: float32 [640], P('shard')
Inputs may be any that keep to these rules, and one draw needn't show every extreme that they name: Within each sequence the positions are each of 0 to 1023 once, laid out in aligned blocks of 64 tokens that hold 64 consecutive positions in increasing order; the order of the blocks is arbitrary.
All inputs are finite; a program needn't handle non-finite values.
Results may differ from a plain program's by a relative error of at most 0.023.
Values may be sent and summed in bfloat16 or wider, within the bound.
No kernel may reach another device: no remote copies, remote signals or barrier semaphores. Data moves between devices by JAX's collectives and lax.ppermute only.
A program may use at most 64 MiB of HBM per device.

v0:
```python
import math

import jax
import jax.numpy as jnp
from jax import lax
from jax.sharding import PartitionSpec as P

epsilon = 1e-06
rope_base = 1000000.0
gelu_coef = 0.044715


def rms_scale(value):
    return lax.rsqrt(jnp.mean(value * value, axis=-1, keepdims=True) + epsilon)


def norm_back(grad_unit, unit, scale):
    return scale * (grad_unit - unit * jnp.mean(grad_unit * unit, axis=-1, keepdims=True))


def gelu_pair(value):
    root = math.sqrt(2.0 / math.pi)
    tangent = jnp.tanh(root * (value + gelu_coef * value * value * value))
    result = 0.5 * value * (1.0 + tangent)
    slope = 0.5 * (1.0 + tangent) + 0.5 * value * (1.0 - tangent * tangent) * root * (
        1.0 + 3.0 * gelu_coef * value * value
    )
    return (result, slope)


def rope_tables(places, width):
    half = width // 2
    freqs = rope_base ** (-(jnp.arange(half, dtype=jnp.float32) * 2.0 / width))
    angles = places.astype(jnp.float32)[:, None] * freqs[None, :]
    return (jnp.cos(angles)[:, None, :], jnp.sin(angles)[:, None, :])


def rotate(value, cosine, sine):
    half = value.shape[-1] // 2
    first = value[..., :half]
    second = value[..., half:]
    return jnp.concatenate(
        [first * cosine - second * sine, second * cosine + first * sine], axis=-1
    )


def unrotate(value, cosine, sine):
    half = value.shape[-1] // 2
    first = value[..., :half]
    second = value[..., half:]
    return jnp.concatenate(
        [first * cosine + second * sine, second * cosine - first * sine], axis=-1
    )


def fill_rows(stacked):
    return lax.all_gather(stacked, "tp", axis=1, tiled=True)


def head_sums(parts):
    return lax.psum(parts, "tp")


def body(
    hidden_in,
    positions,
    cotangent,
    input_gain,
    query_weight,
    key_weight,
    value_weight,
    query_gain,
    key_gain,
    out_weight,
    attn_post_gain,
    ffn_pre_gain,
    gate_weight,
    up_weight,
    down_weight,
    ffn_post_gain,
):
    width = hidden_in.shape[-1]
    gathered = (
        lax.all_gather(input_gain, "shard", axis=0, tiled=True),
        lax.all_gather(query_weight, "shard", axis=0, tiled=True),
        lax.all_gather(key_weight, "shard", axis=0, tiled=True),
        lax.all_gather(value_weight, "shard", axis=0, tiled=True),
        lax.all_gather(query_gain, "shard", axis=0, tiled=True),
        lax.all_gather(key_gain, "shard", axis=0, tiled=True),
        lax.all_gather(out_weight, "shard", axis=1, tiled=True),
        lax.all_gather(attn_post_gain, "shard", axis=0, tiled=True),
        lax.all_gather(ffn_pre_gain, "shard", axis=0, tiled=True),
        lax.all_gather(gate_weight, "shard", axis=0, tiled=True),
        lax.all_gather(up_weight, "shard", axis=0, tiled=True),
        lax.all_gather(down_weight, "shard", axis=1, tiled=True),
        lax.all_gather(ffn_post_gain, "shard", axis=0, tiled=True),
    )
    (
        in_gain_low,
        query_full,
        key_full,
        value_full,
        qgain_low,
        kgain_low,
        out_full,
        post_low,
        pre_low,
        gate_full,
        up_full,
        down_full,
        last_low,
    ) = gathered
    in_gain = in_gain_low.astype(jnp.float32)
    qgain = qgain_low.astype(jnp.float32)
    kgain = kgain_low.astype(jnp.float32)
    post_gain = post_low.astype(jnp.float32)
    pre_gain = pre_low.astype(jnp.float32)
    last_gain = last_low.astype(jnp.float32)
    head_dim = key_full.shape[1]
    heads = query_full.shape[1] // head_dim
    factor = 1.0 / math.sqrt(head_dim)
    own_in = hidden_in.reshape(-1, width)
    own_cot = cotangent.reshape(-1, width)
    part_rows = own_in.shape[0]
    row_start = lax.axis_index("tp") * part_rows
    own_places = positions.reshape(-1)
    both = fill_rows(jnp.stack([own_in, own_cot]))
    rows = both[0].astype(jnp.float32)
    grad_out = both[1].astype(jnp.float32)
    scale_in = rms_scale(rows)
    unit_in = rows * scale_in
    normed_in = (unit_in * in_gain).astype(jnp.bfloat16)
    count = normed_in.shape[0]
    query_raw = jnp.dot(normed_in, query_full, preferred_element_type=jnp.float32).reshape(
        count, heads, head_dim
    )
    query_scale = rms_scale(query_raw)
    query_unit = query_raw * query_scale
    key_raw = jnp.dot(normed_in, key_full, preferred_element_type=jnp.float32)
    key_scale = rms_scale(key_raw)
    key_unit = key_raw * key_scale
    values = jnp.dot(normed_in, value_full, preferred_element_type=jnp.float32).astype(jnp.bfloat16)
    cosine, sine = rope_tables(own_places, head_dim)
    query_rot = rotate(query_unit * qgain, cosine, sine).astype(jnp.bfloat16)
    key_rot = rotate((key_unit * kgain)[:, None, :], cosine, sine)[:, 0].astype(jnp.bfloat16)
    key_all, value_all, places_all = (
        lax.all_gather(key_rot, "ctx", axis=0, tiled=True),
        lax.all_gather(values, "ctx", axis=0, tiled=True),
        lax.all_gather(own_places, "ctx", axis=0, tiled=True),
    )
    visible = places_all[None, None, :] <= own_places[None, :, None]
    scores = (
        jnp.einsum("qhd,kd->hqk", query_rot, key_all, preferred_element_type=jnp.float32) * factor
    )
    scores = jnp.where(visible, scores, -1e30)
    logsum = jnp.log(jnp.sum(jnp.exp(scores), axis=-1, keepdims=True))
    probs = jnp.exp(scores - logsum).astype(jnp.bfloat16)
    context3 = jnp.einsum(
        "hqk,kd->qhd", probs, value_all, preferred_element_type=jnp.float32
    ).astype(jnp.bfloat16)
    context = context3.reshape(count, heads * head_dim)
    attn_part = jnp.dot(context, out_full, preferred_element_type=jnp.float32)
    attn_proj = head_sums((attn_part,))[0]
    attn_scale = rms_scale(attn_proj)
    attn_unit = attn_proj * attn_scale
    resid = rows + attn_unit * post_gain
    ffn_scale = rms_scale(resid)
    ffn_unit = resid * ffn_scale
    ffn_rows = (ffn_unit * pre_gain).astype(jnp.bfloat16)
    gate = jnp.dot(ffn_rows, gate_full, preferred_element_type=jnp.float32)
    upper = jnp.dot(ffn_rows, up_full, preferred_element_type=jnp.float32)
    gelu_val, gelu_slope = gelu_pair(gate)
    hidden_act = (gelu_val * upper).astype(jnp.bfloat16)
    down_part = jnp.dot(hidden_act, down_full, preferred_element_type=jnp.float32)
    ffn_proj = head_sums((down_part,))[0]
    out_scale = rms_scale(ffn_proj)
    out_unit = ffn_proj * out_scale
    block_out = resid + out_unit * last_gain
    last_gain_grad = jnp.sum(grad_out * out_unit, axis=0)
    grad_proj_rows = norm_back(grad_out * last_gain, out_unit, out_scale).astype(jnp.bfloat16)
    down_grad = jnp.dot(hidden_act.T, grad_proj_rows, preferred_element_type=jnp.float32)
    grad_hidden = jnp.dot(grad_proj_rows, down_full.T, preferred_element_type=jnp.float32)
    grad_up = (grad_hidden * gelu_val).astype(jnp.bfloat16)
    grad_gate = (grad_hidden * upper * gelu_slope).astype(jnp.bfloat16)
    gate_grad = jnp.dot(ffn_rows.T, grad_gate, preferred_element_type=jnp.float32)
    up_grad = jnp.dot(ffn_rows.T, grad_up, preferred_element_type=jnp.float32)
    grad_ffn_part = jnp.dot(grad_gate, gate_full.T, preferred_element_type=jnp.float32) + jnp.dot(
        grad_up, up_full.T, preferred_element_type=jnp.float32
    )
    grad_ffn_in = head_sums((grad_ffn_part,))[0]
    pre_gain_grad = jnp.sum(grad_ffn_in * ffn_unit, axis=0)
    grad_resid = grad_out + norm_back(grad_ffn_in * pre_gain, ffn_unit, ffn_scale)
    post_gain_grad = jnp.sum(grad_resid * attn_unit, axis=0)
    grad_attn_rows = norm_back(grad_resid * post_gain, attn_unit, attn_scale).astype(jnp.bfloat16)
    out_grad = jnp.dot(context.T, grad_attn_rows, preferred_element_type=jnp.float32)
    grad_context = (
        jnp.dot(grad_attn_rows, out_full.T, preferred_element_type=jnp.float32)
        .astype(jnp.bfloat16)
        .reshape(count, heads, head_dim)
    )
    delta = jnp.sum(grad_context.astype(jnp.float32) * context3.astype(jnp.float32), axis=-1)
    again = (
        jnp.einsum("qhd,kd->hqk", query_rot, key_all, preferred_element_type=jnp.float32) * factor
    )
    probs_full = jnp.exp(jnp.where(visible, again, -1e30) - logsum)
    grad_probs = jnp.einsum(
        "qhd,kd->hqk", grad_context, value_all, preferred_element_type=jnp.float32
    )
    grad_scores = (probs_full * (grad_probs - delta.T[:, :, None]) * factor).astype(jnp.bfloat16)
    grad_query_rot = jnp.einsum(
        "hqk,kd->qhd", grad_scores, key_all, preferred_element_type=jnp.float32
    )
    grad_key_part = jnp.einsum(
        "hqk,qhd->kd", grad_scores, query_rot, preferred_element_type=jnp.float32
    )
    grad_value_part = jnp.einsum(
        "hqk,qhd->kd", probs, grad_context, preferred_element_type=jnp.float32
    )
    grad_key_own, grad_value_own = (
        lax.psum_scatter(
            grad_key_part.astype(jnp.bfloat16), "ctx", scatter_dimension=0, tiled=True
        ).astype(jnp.float32),
        lax.psum_scatter(
            grad_value_part.astype(jnp.bfloat16), "ctx", scatter_dimension=0, tiled=True
        ).astype(jnp.float32),
    )
    grad_key_rot, grad_values = (
        lax.psum(grad_key_own.astype(jnp.bfloat16), "tp").astype(jnp.float32),
        lax.psum(grad_value_own.astype(jnp.bfloat16), "tp").astype(jnp.float32),
    )
    grad_query_gained = unrotate(grad_query_rot, cosine, sine)
    grad_key_gained = unrotate(grad_key_rot[:, None, :], cosine, sine)[:, 0]
    qgain_part = jnp.sum(grad_query_gained * query_unit, axis=(0, 1))
    kgain_grad = jnp.sum(grad_key_gained * key_unit, axis=0)
    grad_query = (
        norm_back(grad_query_gained * qgain, query_unit, query_scale)
        .astype(jnp.bfloat16)
        .reshape(count, heads * head_dim)
    )
    grad_key = norm_back(grad_key_gained * kgain, key_unit, key_scale).astype(jnp.bfloat16)
    grad_value_low = grad_values.astype(jnp.bfloat16)
    query_grad = jnp.dot(normed_in.T, grad_query, preferred_element_type=jnp.float32)
    key_grad = jnp.dot(normed_in.T, grad_key, preferred_element_type=jnp.float32)
    value_grad = jnp.dot(normed_in.T, grad_value_low, preferred_element_type=jnp.float32)
    query_part = jnp.dot(grad_query, query_full.T, preferred_element_type=jnp.float32)
    query_sum, qgain_grad = head_sums((query_part, qgain_part))
    grad_normed = (
        query_sum
        + jnp.dot(grad_key, key_full.T, preferred_element_type=jnp.float32)
        + jnp.dot(grad_value_low, value_full.T, preferred_element_type=jnp.float32)
    )
    in_gain_grad = jnp.sum(grad_normed * unit_in, axis=0)
    hidden_grad = grad_resid + norm_back(grad_normed * in_gain, unit_in, scale_in)
    block_out = lax.dynamic_slice_in_dim(block_out, row_start, part_rows, 0)
    hidden_grad = lax.dynamic_slice_in_dim(hidden_grad, row_start, part_rows, 0)
    local_grads = (
        in_gain_grad,
        query_grad,
        key_grad,
        value_grad,
        qgain_grad,
        kgain_grad,
        out_grad,
        post_gain_grad,
        pre_gain_grad,
        gate_grad,
        up_grad,
        down_grad,
        last_gain_grad,
    )
    owned = (
        lax.psum_scatter(
            local_grads[0].astype(jnp.bfloat16), "shard", scatter_dimension=0, tiled=True
        ).astype(jnp.float32),
        lax.psum_scatter(
            local_grads[1].astype(jnp.bfloat16), "shard", scatter_dimension=0, tiled=True
        ).astype(jnp.float32),
        lax.psum_scatter(
            local_grads[2].astype(jnp.bfloat16), "shard", scatter_dimension=0, tiled=True
        ).astype(jnp.float32),
        lax.psum_scatter(
            local_grads[3].astype(jnp.bfloat16), "shard", scatter_dimension=0, tiled=True
        ).astype(jnp.float32),
        lax.psum_scatter(
            local_grads[4].astype(jnp.bfloat16), "shard", scatter_dimension=0, tiled=True
        ).astype(jnp.float32),
        lax.psum_scatter(
            local_grads[5].astype(jnp.bfloat16), "shard", scatter_dimension=0, tiled=True
        ).astype(jnp.float32),
        lax.psum_scatter(
            local_grads[6].astype(jnp.bfloat16), "shard", scatter_dimension=1, tiled=True
        ).astype(jnp.float32),
        lax.psum_scatter(
            local_grads[7].astype(jnp.bfloat16), "shard", scatter_dimension=0, tiled=True
        ).astype(jnp.float32),
        lax.psum_scatter(
            local_grads[8].astype(jnp.bfloat16), "shard", scatter_dimension=0, tiled=True
        ).astype(jnp.float32),
        lax.psum_scatter(
            local_grads[9].astype(jnp.bfloat16), "shard", scatter_dimension=0, tiled=True
        ).astype(jnp.float32),
        lax.psum_scatter(
            local_grads[10].astype(jnp.bfloat16), "shard", scatter_dimension=0, tiled=True
        ).astype(jnp.float32),
        lax.psum_scatter(
            local_grads[11].astype(jnp.bfloat16), "shard", scatter_dimension=1, tiled=True
        ).astype(jnp.float32),
        lax.psum_scatter(
            local_grads[12].astype(jnp.bfloat16), "shard", scatter_dimension=0, tiled=True
        ).astype(jnp.float32),
    )
    totals = (
        lax.psum(owned[0].astype(jnp.bfloat16), "ctx").astype(jnp.float32),
        lax.psum(owned[1].astype(jnp.bfloat16), "ctx").astype(jnp.float32),
        lax.psum(owned[2].astype(jnp.bfloat16), "ctx").astype(jnp.float32),
        lax.psum(owned[3].astype(jnp.bfloat16), "ctx").astype(jnp.float32),
        lax.psum(owned[4].astype(jnp.bfloat16), "ctx").astype(jnp.float32),
        lax.psum(owned[5].astype(jnp.bfloat16), "ctx").astype(jnp.float32),
        lax.psum(owned[6].astype(jnp.bfloat16), "ctx").astype(jnp.float32),
        lax.psum(owned[7].astype(jnp.bfloat16), "ctx").astype(jnp.float32),
        lax.psum(owned[8].astype(jnp.bfloat16), "ctx").astype(jnp.float32),
        lax.psum(owned[9].astype(jnp.bfloat16), "ctx").astype(jnp.float32),
        lax.psum(owned[10].astype(jnp.bfloat16), "ctx").astype(jnp.float32),
        lax.psum(owned[11].astype(jnp.bfloat16), "ctx").astype(jnp.float32),
        lax.psum(owned[12].astype(jnp.bfloat16), "ctx").astype(jnp.float32),
    )
    return (
        block_out.reshape(hidden_in.shape),
        hidden_grad.reshape(hidden_in.shape),
        totals[0],
        totals[1],
        totals[2],
        totals[3],
        totals[4],
        totals[5],
        totals[6],
        totals[7],
        totals[8],
        totals[9],
        totals[10],
        totals[11],
        totals[12],
    )


def solution(mesh):
    placed = (
        P("shard", ("ctx", "tp"), None),
        P("shard", "ctx"),
        P("shard", ("ctx", "tp"), None),
        P("shard"),
        P("shard", "tp"),
        P("shard", None),
        P("shard", None),
        P("shard"),
        P("shard"),
        P("tp", "shard"),
        P("shard"),
        P("shard"),
        P("shard", "tp"),
        P("shard", "tp"),
        P("tp", "shard"),
        P("shard"),
    )
    return jax.shard_map(
        body,
        mesh=mesh,
        in_specs=placed,
        out_specs=(
            P("shard", ("ctx", "tp"), None),
            P("shard", ("ctx", "tp"), None),
            P("shard"),
            P("shard", "tp"),
            P("shard", None),
            P("shard", None),
            P("shard"),
            P("shard"),
            P("tp", "shard"),
            P("shard"),
            P("shard"),
            P("shard", "tp"),
            P("shard", "tp"),
            P("tp", "shard"),
            P("shard"),
        ),
        check_vma=False,
    )
```

profile of v0, /device:TPU:0, one launch (start us, length us, event | category | flops | bytes accessed | tf_op | source)
XLA Modules:
  0.0 515.2 jit_solution(12396886439261901686)
XLA Ops:
  7.3 2.4 all_gather.61
  9.7 2.2 all_gather.53
  11.9 1.3 fusion.82
  13.9 0.9 dynamic-update-slice
  14.8 0.9 dynamic-update-slice.1
  15.6 0.9 dynamic-update-slice.2
  17.3 3.1 all-reduce.14
  20.5 19.7 %all_gather.51 = bf16[2,256,640]{2,1,0:T(8,128)(2,1)S(1)} all-gather(bf16[2,64,640]{2,1,0:T(8,128)(2,1)S(1)} %pad_maximum_fusion.1), channel_id=1, replica_groups=mesh['shard'=2,'ctx'=4,'tp'=4] {'tp'}, dimensions={1}, use_global_device_ids=true | all-gather | bytes 819200 | tf_op jit(solution)/shard_map/all_gather | solution.py:57
  40.7 10.9 %all_gather.54 = bf16[1024,256]{1,0:T(8,128)(2,1)S(1)} all-gather(bf16[256,256]{1,0:T(8,128)(2,1)S(1)} %convolution_convert_fusion.11), channel_id=1, replica_groups=mesh['shard'=2,'ctx'=4,'tp'=4] {'ctx'}, dimensions={0}, use_global_device_ids=true | all-gather | bytes 655360 | tf_op jit(solution)/shard_map/all_gather | solution.py:148
  51.6 2.0 all_gather.59
  54.1 1.9 all-gather.3
  56.1 1.8 all-gather.2
  57.9 2.0 all_gather.56
  60.4 7.4 %all-gather = s32[1,1024]{1,0:T(1,128)S(1)} all-gather(s32[1,256]{1,0:T(1,128)S(1)} %copy-done.76), channel_id=2, replica_groups=mesh['shard'=2,'ctx'=4,'tp'=4] {'ctx'}, dimensions={1}, use_global_device_ids=true | all-gather | bytes 5120 | tf_op jit(solution)/shard_map/all_gather | solution.py:149
  68.7 11.8 %all-gather.1 = bf16[1024,1,256]{0,2,1:T(8,128)(2,1)S(1)} all-gather(bf16[256,1,256]{0,2,1:T(8,128)(2,1)S(1)} %pad_maximum_fusion.2), channel_id=3, replica_groups=mesh['shard'=2,'ctx'=4,'tp'=4] {'ctx'}, dimensions={0}, use_global_device_ids=true | all-gather | bytes 655360 | tf_op jit(solution)/shard_map/all_gather | solution.py:147
  81.7 1.1 fusion.72
  83.0 2.5 all_gather.64
  85.5 2.4 all_gather.65
  87.9 2.4 all_gather.66
  90.3 31.5 %all-reduce.22.cloned.1.call-done = f32[256,640]{1,0:T(8,128)} async-done(((f32[256,640]{1,0:T(8,128)}), f32[256,640]{1,0:T(8,128)}) %all-reduce.22.cloned.1.call-update) | async-done | bytes 655376 | tf_op jit(solution)/shard_map/psum | solution.py:61
  121.8 1.3 multiply_reduce_fusion.8
  124.6 1.2 multiply_convert_fusion.4
  126.6 1.2 fusion.84
  128.6 39.3 %all-reduce.24.cloned.1.call-done = f32[256,640]{1,0:T(8,128)} async-done(((f32[256,640]{1,0:T(8,128)}), f32[256,640]{1,0:T(8,128)}) %all-reduce.24.cloned.1.call-update) | async-done | bytes 655376 | tf_op jit(solution)/shard_map/psum | solution.py:61
  167.9 1.3 multiply_reduce_fusion.6
  173.6 1.2 convolution_add_fusion
  174.9 40.2 %all-reduce.26.cloned.1.call-done = f32[256,640]{1,0:T(8,128)} async-done(((f32[256,640]{1,0:T(8,128)}), f32[256,640]{1,0:T(8,128)}) %all-reduce.26.cloned.1.call-update) | async-done | bytes 655376 | tf_op jit(solution)/shard_map/psum | solution.py:61
  215.1 2.0 multiply_reduce_fusion
  217.1 1.8 multiply_reduce_fusion.1
  219.1 1.0 copy-done.10
  221.3 1.1 convolution_convert_fusion.4
  222.6 2.1 convolution_convert_fusion.3
  224.7 22.6 %reduce-scatter.10.cloned.1.call-done = bf16[256,256]{0,1:T(8,128)(2,1)} async-done(((bf16[1024,256]{0,1:T(8,128)(2,1)}), bf16[256,256]{0,1:T(8,128)(2,1)}) %reduce-scatter.10.cloned.1.call-update) | async-done | bytes 131088 | tf_op jit(solution)/shard_map/reduce_scatter | solution.py:220
  247.3 27.8 %reduce-scatter.12.cloned.1.call-done = bf16[256,256]{1,0:T(8,128)(2,1)} async-done(((bf16[1024,256]{1,0:T(8,128)(2,1)}), bf16[256,256]{1,0:T(8,128)(2,1)}) %reduce-scatter.12.cloned.1.call-update) | async-done | bytes 131088 | tf_op jit(solution)/shard_map/reduce_scatter | solution.py:223
  275.2 1.9 convolution_convert_fusion.5
  277.2 1.2 convolution_convert_fusion.2
  278.5 1.2 convolution_convert_fusion.1
  279.8 1.2 convolution_convert_fusion
  281.7 31.4 %all-reduce.30.cloned.1.call-done = (bf16[256,1,256]{0,2,1:T(8,128)(2,1)}, bf16[256,256]{1,0:T(8,128)(2,1)}) async-done(((bf16[256,1,256]{0,2,1:T(8,128)(2,1)}, bf16[256,256]{1,0:T(8,128)(2,1)}), (bf16[256,1,256]{0,2,1:T(8,128)(2,1)}, bf16[256,256]{1,0:T(8,128)(2,1)})) %all-reduce.30.cloned.1.call-update) | async-done | bytes 262160 | tf_op jit(solution)/shard_map/psum | solution.py:228
  313.0 0.9 broadcast_in_dim.15
  315.3 1.1 convolution_convert_fusion.8
  316.6 1.1 convolution_convert_fusion.7
  317.8 1.1 convolution_convert_fusion.6
  319.0 1.1 fusion.86
  320.2 2.6 reduce-scatter.20.cloned.1.call-done
  322.8 11.5 %reduce-scatter.22.cloned.1.call-done = bf16[320,512]{1,0:T(8,128)(2,1)} async-done(((bf16[640,512]{1,0:T(8,128)(2,1)}), bf16[320,512]{1,0:T(8,128)(2,1)}) %reduce-scatter.22.cloned.1.call-update) | async-done | bytes 327696 | tf_op jit(solution)/shard_map/reduce_scatter | solution.py:299
  334.3 11.4 %reduce-scatter.24.cloned.1.call-done = bf16[320,512]{1,0:T(8,128)(2,1)} async-done(((bf16[640,512]{1,0:T(8,128)(2,1)}), bf16[320,512]{1,0:T(8,128)(2,1)}) %reduce-scatter.24.cloned.1.call-update) | async-done | bytes 327696 | tf_op jit(solution)/shard_map/reduce_scatter | solution.py:302
  345.7 11.3 %reduce-scatter.26.cloned.1.call-done = bf16[512,320]{0,1:T(8,128)(2,1)} async-done(((bf16[512,640]{0,1:T(8,128)(2,1)}), bf16[512,320]{0,1:T(8,128)(2,1)}) %reduce-scatter.26.cloned.1.call-update) | async-done | bytes 327696 | tf_op jit(solution)/shard_map/reduce_scatter | solution.py:305
  357.0 11.7 %reduce-scatter.14.cloned.1.call-done = bf16[320,256]{1,0:T(8,128)(2,1)} async-done(((bf16[640,256]{1,0:T(8,128)(2,1)}), bf16[320,256]{1,0:T(8,128)(2,1)}) %reduce-scatter.14.cloned.1.call-update) | async-done | bytes 163856 | tf_op jit(solution)/shard_map/reduce_scatter | solution.py:275
  368.8 11.0 %reduce-scatter.16.cloned.1.call-done = bf16[320,256]{1,0:T(8,128)(2,1)} async-done(((bf16[640,256]{1,0:T(8,128)(2,1)}), bf16[320,256]{1,0:T(8,128)(2,1)}) %reduce-scatter.16.cloned.1.call-update) | async-done | bytes 163856 | tf_op jit(solution)/shard_map/reduce_scatter | solution.py:278
  379.8 11.2 %reduce-scatter.18.cloned.1.call-done = bf16[320,256]{1,0:T(8,128)(2,1)} async-done(((bf16[640,256]{1,0:T(8,128)(2,1)}), bf16[320,256]{1,0:T(8,128)(2,1)}) %reduce-scatter.18.cloned.1.call-update) | async-done | bytes 163856 | tf_op jit(solution)/shard_map/reduce_scatter | solution.py:281
  392.4 1.7 fusion.54
  394.0 12.0 %psum.150 = bf16[256]{0:T(256)(128)(2,1)S(1)} all-reduce(f32[256]{0:T(256)S(1)} %get-tuple-element.25), channel_id=1, replica_groups=mesh['shard'=2,'ctx'=4,'tp'=4] {'tp'}, use_global_device_ids=true, to_apply=%region_32.33 | all-reduce | flops 256 | bytes 1536 | tf_op jit(solution)/shard_map/psum | solution.py:61
  406.1 29.2 %all-reduce.28.cloned.1.call-done = f32[256,640]{1,0:T(8,128)} async-done(((f32[256,640]{1,0:T(8,128)}), f32[256,640]{1,0:T(8,128)}) %all-reduce.28.cloned.1.call-update) | async-done | bytes 655376 | tf_op jit(solution)/shard_map/psum | solution.py:61
  435.3 1.4 convolution_add_fusion.2
  437.4 2.5 all-reduce.13
  440.4 10.6 %all-reduce.11 = (bf16[320]{0:T(512)(128)(2,1)S(1)}, bf16[128]{0:T(256)(128)(2,1)S(1)}, bf16[128]{0:T(256)(128)(2,1)S(1)}, bf16[320]{0:T(512)(128)(2,1)S(1)}, bf...) all-reduce(bf16[320]{0:T(512)(128)(2,1)S(1)} %dynamic-slice.5, ...), channel_id=1, replica_groups=mesh['shard'=2,'ctx'=4,'tp'=4] {'ctx'}, use_global_device_ids=true, to_apply=%region_24.25 | all-reduce | flops 1536 | bytes 6144 | tf_op jit(solution)/shard_map/psum | solution.py:313
  454.3 1.7 fusion.52
  456.0 45.1 %all-reduce.32.cloned.1.call-done = (bf16[320,256]{1,0:T(8,128)(2,1)}, bf16[320,256]{1,0:T(8,128)(2,1)}, bf16[320,256]{1,0:T(8,128)(2,1)}, bf16[256,320]{0,1:T(8...) async-done(((bf16[320,256]{1,0:T(8,128)(2,1)}, bf16[320,256]{1,0:T(8,128)(2,1)}, bf16[320,256]{1,0:T(8,128)(2,1)}, ...) | async-done | bytes 1638416 | tf_op jit(solution)/shard_map/psum | solution.py:314
  501.0 1.7 convert_element_type.268
  502.8 1.7 convert_element_type.270
  505.9 0.9 convert_element_type.284
  506.9 0.9 convert_element_type.286
  507.8 0.9 convert_element_type.288
  (262 shorter events, 21.6 us)
Async XLA Ops:
  7.2 13.2 %copy-start.54 = (bf16[1,64,640]{2,1,0:T(8,128)(2,1)S(1)}, bf16[1,64,640]{2,1,0:T(8,128)(2,1)}, u32[]{:S(2)}) copy-start(bf16[1,64,640]{2,1,0:T(8,128)(2,1)} %param.18) | copy-start | bytes 245764
  7.2 13.2 %copy-start.55 = (bf16[1,64,640]{2,1,0:T(8,128)(2,1)S(1)}, bf16[1,64,640]{2,1,0:T(8,128)(2,1)}, u32[]{:S(2)}) copy-start(bf16[1,64,640]{2,1,0:T(8,128)(2,1)} %param.16) | copy-start | bytes 245764
  7.2 114.6 %all-reduce.22.cloned.1.call-start = ((), (), s32[]{:S(2)}) async-start(), calls=%async_computation.9 | async-start | bytes 1310720 | tf_op jit(solution)/shard_map/psum | solution.py:61
  7.3 60.7 %copy-start.77 = (f32[128]{0:T(128)}, f32[128]{0:T(128)S(1)}, u32[]{:S(2)}) copy-start(f32[128]{0:T(128)S(1)} %negate_power_fusion) | copy-start | bytes 1540
  9.7 72.0 %copy-start.9 = (bf16[256,640]{0,1:T(8,128)(2,1)}, bf16[256,640]{0,1:T(8,128)(2,1)S(1)}, u32[]{:S(2)}) copy-start(bf16[256,640]{0,1:T(8,128)(2,1)S(1)} %all_gather.61) | copy-start | bytes 983044
  11.9 28.4 %copy-start.30 = (bf16[640,256]{1,0:T(8,128)(2,1)}, bf16[640,256]{1,0:T(8,128)(2,1)S(1)}, u32[]{:S(2)}) copy-start(bf16[640,256]{1,0:T(8,128)(2,1)S(1)} %all_gather.53) | copy-start | bytes 983044
  20.4 39.5 %copy-start.59 = (f32[640]{0:T(1024)}, f32[640]{0:T(1024)S(1)}, u32[]{:S(2)}) copy-start(f32[640]{0:T(1024)S(1)} %convert_element_type.231) | copy-start | bytes 7684
  40.2 11.4 %copy-start.49 = (bf16[320,256]{1,0:T(8,128)(2,1)S(1)}, bf16[320,256]{1,0:T(8,128)(2,1)}, u32[]{:S(2)}) copy-start(bf16[320,256]{1,0:T(8,128)(2,1)} %param.20) | copy-start | bytes 491524
  40.3 19.6 %copy-start.74 = (f32[256]{0:T(256)}, f32[256]{0:T(256)S(1)}, u32[]{:S(2)}) copy-start(f32[256]{0:T(256)S(1)} %add_rsqrt_fusion.5) | copy-start | bytes 3076
  40.7 13.4 %copy-start.79 = (bf16[128]{0:T(256)(128)(2,1)S(1)}, bf16[128]{0:T(256)(128)(2,1)}, u32[]{:S(2)}) copy-start(bf16[128]{0:T(256)(128)(2,1)} %param.23) | copy-start | bytes 772
  40.7 15.4 %copy-start.80 = (bf16[128]{0:T(256)(128)(2,1)S(1)}, bf16[128]{0:T(256)(128)(2,1)}, u32[]{:S(2)}) copy-start(bf16[128]{0:T(256)(128)(2,1)} %param.24) | copy-start | bytes 772
  40.7 17.2 %copy-start.50 = (bf16[320,256]{1,0:T(8,128)(2,1)S(1)}, bf16[320,256]{1,0:T(8,128)(2,1)}, u32[]{:S(2)}) copy-start(bf16[320,256]{1,0:T(8,128)(2,1)} %param.21) | copy-start | bytes 491524
  51.6 29.7 %copy-start.3 = (bf16[1024,256]{1,0:T(8,128)(2,1)}, bf16[1024,256]{1,0:T(8,128)(2,1)S(1)}, u32[]{:S(2)}) copy-start(bf16[1024,256]{1,0:T(8,128)(2,1)S(1)} %all_gather.54) | copy-start | bytes 1572868
  53.6 4.2 copy-start.28
  54.1 13.9 %copy-start.19 = (f32[256,256]{0,1:T(8,128)}, f32[256,256]{0,1:T(8,128)S(1)}, u32[]{:S(2)}) copy-start(f32[256,256]{0,1:T(8,128)S(1)} %get-tuple-element.75) | copy-start | bytes 786436
  54.1 6.3 %copy-start.76 = (s32[1,256]{1,0:T(1,128)S(1)}, s32[1,256]{1,0:T(1,128)}, u32[]{:S(2)}) copy-start(s32[1,256]{1,0:T(1,128)} %param.17) | copy-start | bytes 3076
  56.0 11.9 %copy-start.65 = (f32[2,1,128]{2,1,0:T(1,128)}, f32[2,1,128]{2,1,0:T(1,128)S(1)}, u32[]{:S(2)}) copy-start(f32[2,1,128]{2,1,0:T(1,128)S(1)} %convert_element_type.295) | copy-start | bytes 3076
  56.0 11.9 %copy-start.67 = (f32[256]{0:T(256)}, f32[256]{0:T(256)S(1)}, u32[]{:S(2)}) copy-start(f32[256]{0:T(256)S(1)} %add_rsqrt_fusion.3) | copy-start | bytes 3076
  57.9 10.1 %copy-start.61 = (f32[2,1,128]{2,1,0:T(1,128)}, f32[2,1,128]{2,1,0:T(1,128)S(1)}, u32[]{:S(2)}) copy-start(f32[2,1,128]{2,1,0:T(1,128)S(1)} %convert_element_type.294) | copy-start | bytes 3076
  59.9 8.1 %copy-start.24 = (bf16[640,256]{1,0:T(8,128)(2,1)}, bf16[640,256]{1,0:T(8,128)(2,1)S(1)}, u32[]{:S(2)}) copy-start(bf16[640,256]{1,0:T(8,128)(2,1)S(1)} %all_gather.56) | copy-start | bytes 983044
  60.4 8.3 %copy-start.17 = (f32[256,256]{0,1:T(8,128)}, f32[256,256]{0,1:T(8,128)S(1)}, u32[]{:S(2)}) copy-start(f32[256,256]{0,1:T(8,128)S(1)} %get-tuple-element.77) | copy-start | bytes 786436
  60.4 8.2 %copy-start.63 = (f32[256]{0:T(256)}, f32[256]{0:T(256)S(1)}, u32[]{:S(2)}) copy-start(f32[256]{0:T(256)S(1)} %add_rsqrt_fusion.4) | copy-start | bytes 3076
  68.6 12.3 %copy-start.47 = (bf16[256,128]{0,1:T(8,128)(2,1)}, bf16[256,128]{0,1:T(8,128)(2,1)S(1)}, u32[]{:S(2)}) copy-start(bf16[256,128]{0,1:T(8,128)(2,1)S(1)} %get-tuple-element.65) | copy-start | bytes 196612
  81.7 137.4 %copy-start.23 = (bf16[256,256]{1,0:T(8,128)(2,1)}, bf16[256,256]{1,0:T(8,128)(2,1)S(1)}, u32[]{:S(2)}) copy-start(bf16[256,256]{1,0:T(8,128)(2,1)S(1)} %convolution_convert_fusion.10) | copy-start | bytes 393220
  82.9 2.7 copy-start.42
  82.9 5.0 copy-start.43
  82.9 85.0 %all-reduce.24.cloned.1.call-start = ((), (), s32[]{:S(2)}) async-start(), calls=%async_computation.10 | async-start | bytes 1310720 | tf_op jit(solution)/shard_map/psum | solution.py:61
  124.6 1.9 copy-start.13
  127.8 87.3 %all-reduce.26.cloned.1.call-start = ((), (), s32[]{:S(2)}) async-start(), calls=%async_computation.11 | async-start | bytes 1310720 | tf_op jit(solution)/shard_map/psum | solution.py:61
  169.2 2.4 copy-start.81
  170.1 1.6 copy-start.14
  170.1 1.6 copy-start.40
  174.9 72.4 %reduce-scatter.10.cloned.1.call-start = ((), (), s32[]{:S(2)}) async-start(), calls=%async_computation.13 | async-start | bytes 655360 | tf_op jit(solution)/shard_map/reduce_scatter | solution.py:220
  215.1 2.0 copy-start.11
  217.1 1.8 copy-start.57
  222.5 52.7 %copy-start.8 = (bf16[256,640]{1,0:T(8,128)(2,1)S(1)}, bf16[256,640]{1,0:T(8,128)(2,1)}, u32[]{:S(2)}) copy-start(bf16[256,640]{1,0:T(8,128)(2,1)} %copy-done.7) | copy-start | bytes 983044
  222.5 52.6 %reduce-scatter.12.cloned.1.call-start = ((), (), s32[]{:S(2)}) async-start(), calls=%async_computation.14 | async-start | bytes 655360 | tf_op jit(solution)/shard_map/reduce_scatter | solution.py:223
  224.7 52.5 %copy-start.38 = (bf16[256,512]{1,0:T(8,128)(2,1)S(1)}, bf16[256,512]{1,0:T(8,128)(2,1)}, u32[]{:S(2)}) copy-start(bf16[256,512]{1,0:T(8,128)(2,1)} %copy-done.37) | copy-start | bytes 786436
  224.7 88.4 %all-reduce.30.cloned.1.call-start = ((), (), s32[]{:S(2)}) async-start(), calls=%async_computation.22 | async-start | bytes 524288 | tf_op jit(solution)/shard_map/psum | solution.py:228
  275.1 47.7 %reduce-scatter.20.cloned.1.call-start = ((), (), s32[]{:S(2)}) async-start(), calls=%async_computation.18 | async-start | bytes 491520 | tf_op jit(solution)/shard_map/reduce_scatter | solution.py:290
  277.1 57.2 %reduce-scatter.22.cloned.1.call-start = ((), (), s32[]{:S(2)}) async-start(), calls=%async_computation.19 | async-start | bytes 983040 | tf_op jit(solution)/shard_map/reduce_scatter | solution.py:299
  278.4 67.3 %reduce-scatter.24.cloned.1.call-start = ((), (), s32[]{:S(2)}) async-start(), calls=%async_computation.20 | async-start | bytes 983040 | tf_op jit(solution)/shard_map/reduce_scatter | solution.py:302
  279.7 1.6 copy-start.22
  279.7 77.3 %reduce-scatter.26.cloned.1.call-start = ((), (), s32[]{:S(2)}) async-start(), calls=%async_computation.21 | async-start | bytes 983040 | tf_op jit(solution)/shard_map/reduce_scatter | solution.py:305
  281.0 33.0 %copy-start.70 = (f32[256]{0:T(256)S(1)}, f32[256]{0:T(256)}, u32[]{:S(2)}) copy-start(f32[256]{0:T(256)} %copy-done.69) | copy-start | bytes 3076
  281.0 33.0 %copy-start.78 = (f32[128]{0:T(128)S(1)}, f32[128]{0:T(128)}, u32[]{:S(2)}) copy-start(f32[128]{0:T(128)} %copy-done.77) | copy-start | bytes 1540
  281.0 87.7 %reduce-scatter.14.cloned.1.call-start = ((), (), s32[]{:S(2)}) async-start(), calls=%async_computation.15 | async-start | bytes 491520 | tf_op jit(solution)/shard_map/reduce_scatter | solution.py:275
  281.6 33.0 %copy-start.20 = (f32[256,256]{0,1:T(8,128)S(1)}, f32[256,256]{0,1:T(8,128)}, u32[]{:S(2)}) copy-start(f32[256,256]{0,1:T(8,128)} %copy-done.19) | copy-start | bytes 786436
  281.6 33.0 %copy-start.66 = (f32[2,1,128]{2,1,0:T(1,128)S(1)}, f32[2,1,128]{2,1,0:T(1,128)}, u32[]{:S(2)}) copy-start(f32[2,1,128]{2,1,0:T(1,128)} %copy-done.65) | copy-start | bytes 3076
  281.6 33.0 %copy-start.68 = (f32[256]{0:T(256)S(1)}, f32[256]{0:T(256)}, u32[]{:S(2)}) copy-start(f32[256]{0:T(256)} %copy-done.67) | copy-start | bytes 3076
  281.6 33.2 %copy-start.18 = (f32[256,256]{0,1:T(8,128)S(1)}, f32[256,256]{0,1:T(8,128)}, u32[]{:S(2)}) copy-start(f32[256,256]{0,1:T(8,128)} %copy-done.17) | copy-start | bytes 786436
  281.6 33.2 %copy-start.62 = (f32[2,1,128]{2,1,0:T(1,128)S(1)}, f32[2,1,128]{2,1,0:T(1,128)}, u32[]{:S(2)}) copy-start(f32[2,1,128]{2,1,0:T(1,128)} %copy-done.61) | copy-start | bytes 3076
  281.6 33.2 %copy-start.64 = (f32[256]{0:T(256)S(1)}, f32[256]{0:T(256)}, u32[]{:S(2)}) copy-start(f32[256]{0:T(256)} %copy-done.63) | copy-start | bytes 3076
  316.4 63.4 %reduce-scatter.16.cloned.1.call-start = ((), (), s32[]{:S(2)}) async-start(), calls=%async_computation.16 | async-start | bytes 491520 | tf_op jit(solution)/shard_map/reduce_scatter | solution.py:278
  317.7 73.2 %reduce-scatter.18.cloned.1.call-start = ((), (), s32[]{:S(2)}) async-start(), calls=%async_computation.17 | async-start | bytes 491520 | tf_op jit(solution)/shard_map/reduce_scatter | solution.py:281
  318.9 116.4 %all-reduce.28.cloned.1.call-start = ((), (), s32[]{:S(2)}) async-start(), calls=%async_computation.12 | async-start | bytes 1310720 | tf_op jit(solution)/shard_map/psum | solution.py:61
  320.2 180.9 %all-reduce.32.cloned.1.call-start = ((), (), s32[]{:S(2)}) async-start(), calls=%async_computation.23 | async-start | bytes 3276800 | tf_op jit(solution)/shard_map/psum | solution.py:314
  391.0 44.3 %copy-start.25 = (bf16[640,256]{1,0:T(8,128)(2,1)S(1)}, bf16[640,256]{1,0:T(8,128)(2,1)}, u32[]{:S(2)}) copy-start(bf16[640,256]{1,0:T(8,128)(2,1)} %copy-done.24) | copy-start | bytes 983044
  392.4 44.3 %copy-start.31 = (bf16[640,256]{1,0:T(8,128)(2,1)S(1)}, bf16[640,256]{1,0:T(8,128)(2,1)}, u32[]{:S(2)}) copy-start(bf16[640,256]{1,0:T(8,128)(2,1)} %copy-done.30) | copy-start | bytes 983044
  501.0 3.4 copy-start.52
  501.0 4.1 copy-start.51
  501.0 4.9 copy-start.46
  504.4 2.4 copy-start.45
  505.9 1.8 copy-start.44
  (33 other events, 33.2 us)
Sparse Core Ops, SparseCore 0:
  83.0 38.7 all-reduce.21
  127.9 39.9 all-reduce.23
  175.0 40.0 all-reduce.25
  222.6 24.6 reduce-scatter.9
  250.0 25.0 reduce-scatter.11
  277.3 35.6 all-reduce.29
  315.3 7.5 reduce-scatter.19
  325.1 9.1 reduce-scatter.21
  336.5 9.1 reduce-scatter.23
  347.8 9.1 reduce-scatter.25
  359.8 8.8 reduce-scatter.13
  370.9 8.8 reduce-scatter.15
  382.0 8.8 reduce-scatter.17
  393.7 41.5 all-reduce.27
  439.0 61.9 all-reduce.31
where the time goes:
time: 516 us; the launch traced here: 515 us
  waiting for transfers between devices  338 us (66%)
  blocking collectives  97.7 us (19%)
  other arithmetic  26 us (5%)
  matrix products  24.2 us (5%)
  between operations  16.9 us (3%)
  local copies, waits for them, and re-layouts  11.4 us (2%)
    psum x4, waiting for transfers between devices, head_sums(): return lax.psum(parts, 'tp')  140 us
    psum x1, waiting for transfers between devices, body(): lax.psum(owned[1].astype(jnp.bfloat16), 'ctx').astype(jnp.float32)  45.1 us
    psum x1, waiting for transfers between devices, body(): lax.psum(grad_key_own.astype(jnp.bfloat16), 'tp').astype(jnp.float32)  31.4 us
    reduce_scatter x1, waiting for transfers between devices, body(): lax.psum_scatter(grad_value_part.astype(jnp.bfloat16), 'ctx', scatter_dim...  27.8 us
    reduce_scatter x1, waiting for transfers between devices, body(): lax.psum_scatter(grad_key_part.astype(jnp.bfloat16), 'ctx', scatter_dimen...  22.6 us
    all_gather x1, blocking collectives, fill_rows(): return lax.all_gather(stacked, 'tp', axis=1, tiled=True)  19.7 us
    psum x1, blocking collectives, head_sums(): return lax.psum(parts, 'tp')  12 us
    all_gather x1, blocking collectives, body(): lax.all_gather(key_rot, 'ctx', axis=0, tiled=True)  11.8 us
  transfers between devices with their start and end apart: 15, of which 15 were waited for; matrix products, arithmetic and copies ran while one was open for 5% of the time, Pallas kernels for 0%

commit v1 on v0

v1 whole, which is shorter than its diff:
```python
import math

import jax
import jax.numpy as jnp
from jax import lax
from jax.sharding import PartitionSpec as P

epsilon = 1e-06
rope_base = 1000000.0
gelu_coef = 0.044715
low = jnp.bfloat16
full = jnp.float32


def rms_scale(value):
    return lax.rsqrt(jnp.mean(value * value, axis=-1, keepdims=True) + epsilon)


def norm_back(grad_unit, unit, scale):
    return scale * (grad_unit - unit * jnp.mean(grad_unit * unit, axis=-1, keepdims=True))


def gelu_pair(value):
    root = math.sqrt(2.0 / math.pi)
    tangent = jnp.tanh(root * (value + gelu_coef * value * value * value))
    result = 0.5 * value * (1.0 + tangent)
    slope = 0.5 * (1.0 + tangent) + 0.5 * value * (1.0 - tangent * tangent) * root * (
        1.0 + 3.0 * gelu_coef * value * value
    )
    return (result, slope)


def rope_tables(places, width):
    half = width // 2
    freqs = rope_base ** (-(jnp.arange(half, dtype=full) * 2.0 / width))
    angles = places.astype(full)[:, None] * freqs[None, :]
    return (jnp.cos(angles), jnp.sin(angles))


def rotate(value, cosine, sine):
    half = value.shape[-1] // 2
    first = value[..., :half]
    second = value[..., half:]
    return jnp.concatenate(
        [first * cosine - second * sine, second * cosine + first * sine], axis=-1
    )


def unrotate(value, cosine, sine):
    return rotate(value, cosine, -sine)


def dot(left, right):
    return jnp.dot(left, right, preferred_element_type=full)


def dot_tn(left, right):
    return lax.dot_general(left, right, (((0,), (0,)), ((), ())), preferred_element_type=full)


def dot_nt(left, right):
    return lax.dot_general(left, right, (((1,), (1,)), ((), ())), preferred_element_type=full)


def pieces(value, axis):
    count = lax.axis_size(axis)
    return [value] + [
        lax.ppermute(value, axis, [(i, (i + o) % count) for i in range(count)])
        for o in range(1, count)
    ]


def gather_rows(value, axis):
    return jnp.concatenate(pieces(value, axis), axis=0)


def scatter_rows(value, axis):
    count = lax.axis_size(axis)
    rows = value.shape[0] // count
    total = value[:rows].astype(full)
    sent = value.astype(low)
    for o in range(1, count):
        block = sent[o * rows : (o + 1) * rows]
        total = total + lax.ppermute(
            block, axis, [(i, (i - o) % count) for i in range(count)]
        ).astype(full)
    return total


def shard_gather(value, dim):
    count = lax.axis_size("shard")
    if count != 2:
        return lax.all_gather(value, "shard", axis=dim, tiled=True)
    other = lax.ppermute(value, "shard", [(0, 1), (1, 0)])
    first = lax.axis_index("shard") == 0
    return jnp.concatenate(
        [jnp.where(first, value, other), jnp.where(first, other, value)], axis=dim
    )


def shard_scatter(value):
    count = lax.axis_size("shard")
    if count != 2:
        return lax.psum_scatter(value.astype(low), "shard", scatter_dimension=0, tiled=True)
    rows = value.shape[0] // 2
    me = lax.axis_index("shard")
    theirs = lax.dynamic_slice_in_dim(value, (1 - me) * rows, rows, 0).astype(low)
    mine = lax.dynamic_slice_in_dim(value, me * rows, rows, 0)
    return (
        mine.astype(full) + lax.ppermute(theirs, "shard", [(0, 1), (1, 0)]).astype(full)
    ).astype(low)


def axis_total(value, axis):
    count = lax.axis_size(axis)
    rows = value.shape[0] // count
    me = lax.axis_index(axis)
    total = None
    for o in range(count):
        block = lax.dynamic_slice_in_dim(value, ((me + o) % count) * rows, rows, 0)
        if o == 0:
            total = block.astype(full)
        else:
            total = total + lax.ppermute(
                block, axis, [(i, (i + o) % count) for i in range(count)]
            ).astype(full)
    return total.astype(low)


def axis_fill(chunk, axis):
    count = lax.axis_size(axis)
    rows = chunk.shape[0]
    me = lax.axis_index(axis)
    held = [chunk] + [
        lax.ppermute(chunk, axis, [(i, (i - o) % count) for i in range(count)])
        for o in range(1, count)
    ]
    twice = jnp.concatenate(held + held, axis=0)
    start = ((count - me) % count) * rows
    return lax.dynamic_slice_in_dim(twice, start, rows * count, 0)


def axis_sum(value, axis):
    total = None
    for piece in pieces(value, axis):
        total = piece.astype(full) if total is None else total + piece.astype(full)
    return total


def body(
    hidden_in,
    positions,
    cotangent,
    input_gain,
    query_weight,
    key_weight,
    value_weight,
    query_gain,
    key_gain,
    out_weight,
    attn_post_gain,
    ffn_pre_gain,
    gate_weight,
    up_weight,
    down_weight,
    ffn_post_gain,
):
    width = hidden_in.shape[-1]
    head_dim = key_weight.shape[1]
    head_cols = query_weight.shape[1]
    hidden_cols = gate_weight.shape[1]
    heads = head_cols // head_dim
    factor = 1.0 / math.sqrt(head_dim)
    shards = lax.axis_size("shard")
    tps = lax.axis_size("tp")
    ctxs = lax.axis_size("ctx")
    own_in = hidden_in.reshape(-1, width)
    own_cot = cotangent.reshape(-1, width)
    part_rows = own_in.shape[0]
    me_tp = lax.axis_index("tp")

    rows_low = gather_rows(own_in, "tp")
    count = rows_low.shape[0]
    natural = positions.reshape(tps, part_rows)
    places = jnp.concatenate(
        [
            lax.dynamic_slice_in_dim(natural, (me_tp - o) % tps, 1, 0).reshape(-1)
            for o in range(tps)
        ]
    )
    places_all = gather_rows(places, "ctx")

    wide = width // shards
    slim = head_dim // shards
    packed = jnp.concatenate(
        [input_gain, attn_post_gain, ffn_pre_gain, ffn_post_gain, query_gain, key_gain]
    ).reshape(1, -1)
    gains = shard_gather(packed, 0).astype(full)

    def gain_at(start, size):
        return gains[:, start : start + size].reshape(-1)

    in_gain = gain_at(0, wide)
    post_gain = gain_at(wide, wide)
    pre_gain = gain_at(2 * wide, wide)
    last_gain = gain_at(3 * wide, wide)
    qgain = gain_at(4 * wide, slim)
    kgain = gain_at(4 * wide + slim, slim)
    qkv_full = shard_gather(jnp.concatenate([query_weight, key_weight, value_weight], axis=1), 0)
    query_full = qkv_full[:, :head_cols]
    key_full = qkv_full[:, head_cols : head_cols + head_dim]
    value_full = qkv_full[:, head_cols + head_dim :]
    out_full = shard_gather(out_weight, 1)
    gate_full = shard_gather(gate_weight, 0)
    up_full = shard_gather(up_weight, 0)
    down_full = shard_gather(down_weight, 1)

    rows = rows_low.astype(full)
    scale_in = rms_scale(rows)
    unit_in = rows * scale_in
    normed_in = (unit_in * in_gain).astype(low)
    cosine, sine = rope_tables(places, head_dim)
    key_raw = dot(normed_in, key_full)
    key_scale = rms_scale(key_raw)
    key_unit = key_raw * key_scale
    key_rot = rotate(key_unit * kgain, cosine, sine).astype(low)
    key_all = gather_rows(key_rot, "ctx")
    values = dot(normed_in, value_full).astype(low)
    value_all = gather_rows(values, "ctx")
    query_raw = dot(normed_in, query_full).reshape(count, heads, head_dim)
    query_scale = rms_scale(query_raw)
    query_unit = query_raw * query_scale
    query_rot = rotate(query_unit * qgain, cosine[:, None, :], sine[:, None, :]).astype(low)
    visible = places_all[None, None, :] <= places[None, :, None]
    scores = (
        jnp.einsum("qhd,kd->hqk", query_rot, key_all, preferred_element_type=full) * factor
    )
    weight = jnp.exp(jnp.where(visible, scores, -1e30))
    probs_full = weight * (1.0 / jnp.sum(weight, axis=-1, keepdims=True))
    probs = probs_full.astype(low)
    context3 = jnp.einsum(
        "hqk,kd->qhd", probs, value_all, preferred_element_type=full
    ).astype(low)
    context = context3.reshape(count, head_cols)
    attn_proj = scatter_rows(dot(context, out_full), "tp")

    own_rows = own_in.astype(full)
    grad_out = own_cot.astype(full)
    attn_scale = rms_scale(attn_proj)
    attn_unit = attn_proj * attn_scale
    resid = own_rows + attn_unit * post_gain
    ffn_scale = rms_scale(resid)
    ffn_unit = resid * ffn_scale
    ffn_rows = gather_rows((ffn_unit * pre_gain).astype(low), "tp")

    gate = dot(ffn_rows, gate_full)
    upper = dot(ffn_rows, up_full)
    gelu_val, gelu_slope = gelu_pair(gate)
    hidden_act = (gelu_val * upper).astype(low)
    ffn_proj = scatter_rows(dot(hidden_act, down_full), "tp")

    out_scale = rms_scale(ffn_proj)
    out_unit = ffn_proj * out_scale
    block_out = resid + out_unit * last_gain
    last_gain_grad = jnp.sum(grad_out * out_unit, axis=0)
    grad_proj_own = norm_back(grad_out * last_gain, out_unit, out_scale).astype(low)
    grad_proj_rows = gather_rows(grad_proj_own, "tp")

    grad_hidden = dot_nt(grad_proj_rows, down_full)
    grad_up = (grad_hidden * gelu_val).astype(low)
    grad_gate = (grad_hidden * upper * gelu_slope).astype(low)
    grad_ffn_in = scatter_rows(dot_nt(grad_gate, gate_full) + dot_nt(grad_up, up_full), "tp")

    pre_gain_grad = jnp.sum(grad_ffn_in * ffn_unit, axis=0)
    grad_resid = grad_out + norm_back(grad_ffn_in * pre_gain, ffn_unit, ffn_scale)
    post_gain_grad = jnp.sum(grad_resid * attn_unit, axis=0)
    grad_attn_own = norm_back(grad_resid * post_gain, attn_unit, attn_scale).astype(low)
    grad_attn_rows = gather_rows(grad_attn_own, "tp")

    early = shard_scatter(
        jnp.concatenate(
            [
                dot_tn(ffn_rows, grad_gate).astype(low),
                dot_tn(ffn_rows, grad_up).astype(low),
                dot_tn(grad_proj_rows, hidden_act).astype(low),
            ],
            axis=1,
        )
    )
    early_all = axis_fill(axis_total(early, "ctx"), "ctx")

    grad_context_flat = dot_nt(grad_attn_rows, out_full).astype(low)
    grad_context = grad_context_flat.reshape(count, heads, head_dim)
    delta = jnp.sum(grad_context.astype(full) * context3.astype(full), axis=-1)
    grad_probs = jnp.einsum("qhd,kd->hqk", grad_context, value_all, preferred_element_type=full)
    grad_scores = (probs_full * (grad_probs - delta.T[:, :, None]) * factor).astype(low)
    grad_key_part = jnp.einsum(
        "hqk,qhd->kd", grad_scores, query_rot, preferred_element_type=full
    ).astype(low)
    grad_value_part = jnp.einsum(
        "hqk,qhd->kd", probs, grad_context, preferred_element_type=full
    ).astype(low)
    grad_query_rot = jnp.einsum("hqk,kd->qhd", grad_scores, key_all, preferred_element_type=full)
    both = scatter_rows(jnp.concatenate([grad_key_part, grad_value_part], axis=1), "ctx")
    grad_key_rot = both[:, :head_dim]
    grad_value_low = both[:, head_dim:].astype(low)

    grad_query_gained = unrotate(grad_query_rot, cosine[:, None, :], sine[:, None, :])
    qgain_grad = jnp.sum(grad_query_gained * query_unit, axis=(0, 1))
    grad_query = (
        norm_back(grad_query_gained * qgain, query_unit, query_scale)
        .astype(low)
        .reshape(count, head_cols)
    )
    query_part = dot_nt(grad_query, query_full)

    grad_key_gained = unrotate(grad_key_rot, cosine, sine)
    kgain_grad = jnp.sum(grad_key_gained * key_unit, axis=0)
    grad_key = norm_back(grad_key_gained * kgain, key_unit, key_scale).astype(low)
    grad_normed_part = (
        query_part + dot_nt(grad_key, key_full) + dot_nt(grad_value_low, value_full)
    )
    in_gain_grad = jnp.sum(grad_normed_part * unit_in, axis=0)
    grad_normed = scatter_rows(grad_normed_part, "tp")
    own_scale = rms_scale(own_rows)
    hidden_grad = grad_resid + norm_back(grad_normed * in_gain, own_rows * own_scale, own_scale)

    small_width = 2 * head_dim
    late_q = jnp.concatenate(
        [
            dot_tn(normed_in, grad_query).astype(low),
            dot_tn(grad_attn_rows, context).astype(low),
        ],
        axis=1,
    )
    late_kv = jnp.concatenate(
        [
            dot_tn(normed_in, grad_key).astype(low),
            dot_tn(normed_in, grad_value_low).astype(low),
        ],
        axis=1,
    )
    vectors = jnp.concatenate(
        [
            item.reshape(shards, -1)
            for item in (
                in_gain_grad,
                post_gain_grad,
                pre_gain_grad,
                last_gain_grad,
                qgain_grad,
                kgain_grad,
            )
        ],
        axis=1,
    ).astype(low)
    length = vectors.shape[1]
    late_q_own = axis_total(shard_scatter(late_q), "ctx")
    late_kv_own = axis_total(shard_scatter(late_kv), "ctx")
    late_kv_own = axis_sum(late_kv_own, "tp").astype(low)
    late_all = axis_fill(jnp.concatenate([late_q_own, late_kv_own], axis=1), "ctx").astype(full)
    vector_own = shard_scatter(vectors.reshape(shards, 1, length)).reshape(1, length)
    vector_own = axis_sum(axis_sum(vector_own, "ctx").astype(low), "tp").reshape(length)

    def vector_at(start, size):
        return vector_own[start : start + size]

    early_all = early_all.astype(full)
    gate_grad = early_all[:, :hidden_cols]
    up_grad = early_all[:, hidden_cols : 2 * hidden_cols]
    down_grad = early_all[:, 2 * hidden_cols :].T
    query_grad = late_all[:, :head_cols]
    out_grad = late_all[:, head_cols : 2 * head_cols].T
    key_grad = late_all[:, 2 * head_cols : 2 * head_cols + head_dim]
    value_grad = late_all[:, 2 * head_cols + head_dim :]
    return (
        block_out.reshape(hidden_in.shape),
        hidden_grad.reshape(hidden_in.shape),
        vector_at(0, wide),
        query_grad,
        key_grad,
        value_grad,
        vector_at(4 * wide, slim),
        vector_at(4 * wide + slim, slim),
        out_grad,
        vector_at(wide, wide),
        vector_at(2 * wide, wide),
        gate_grad,
        up_grad,
        down_grad,
        vector_at(3 * wide, wide),
    )


def solution(mesh):
    placed = (
        P("shard", ("ctx", "tp"), None),
        P("shard", "ctx"),
        P("shard", ("ctx", "tp"), None),
        P("shard"),
        P("shard", "tp"),
        P("shard", None),
        P("shard", None),
        P("shard"),
        P("shard"),
        P("tp", "shard"),
        P("shard"),
        P("shard"),
        P("shard", "tp"),
        P("shard", "tp"),
        P("tp", "shard"),
        P("shard"),
    )
    return jax.shard_map(
        body,
        mesh=mesh,
        in_specs=placed,
        out_specs=(
            P("shard", ("ctx", "tp"), None),
            P("shard", ("ctx", "tp"), None),
            P("shard"),
            P("shard", "tp"),
            P("shard", None),
            P("shard", None),
            P("shard"),
            P("shard"),
            P("tp", "shard"),
            P("shard"),
            P("shard"),
            P("shard", "tp"),
            P("shard", "tp"),
            P("tp", "shard"),
            P("shard"),
        ),
        check_vma=False,
    )
```

time: 516 us -> 245 us (0.47)
  waiting for transfers between devices: 338 us -> 78.1 us
  blocking collectives: 97.7 us -> 0 us
  starting transfers between devices: 0.8 us -> 82.8 us
  local copies, waits for them, and re-layouts: 11.4 us -> 39.5 us
  between operations: 16.9 us -> 2.54 us
    psum x6 -> x0, waiting for transfers between devices: 217 us -> none  [the longest x4 140 us: head_sums(): return lax.psum(parts, 'tp')]
    reduce_scatter x9 -> x0, waiting for transfers between devices: 121 us -> none  [the longest x1 27.8 us: body(): lax.psum_scatter(grad_value_part.astype(jnp.bfloat16), 'ctx', scatter_dim...]
    ppermute x0 -> x70, starting transfers between devices: none -> 82.8 us  [the longest x30 37.6 us: pieces(): lax.ppermute(value, axis, [(i, (i + o) % count) for i in range(count)])]
    ppermute x0 -> x70, waiting for transfers between devices: none -> 78.1 us  [the longest x30 35.8 us: pieces(): lax.ppermute(value, axis, [(i, (i + o) % count) for i in range(count)])]
    all_gather x13 -> x0, blocking collectives: 69.6 us -> none  [the longest x1 19.7 us: fill_rows(): return lax.all_gather(stacked, 'tp', axis=1, tiled=True)]
    psum x2 -> x0, blocking collectives: 22.6 us -> none  [the longest x1 12 us: head_sums(): return lax.psum(parts, 'tp')]
    concatenate x0 -> x6, local copies, waits for them, and re-layouts: none -> 13.9 us  [the longest x2 8.01 us: axis_fill(): twice = jnp.concatenate(held + held, axis=0)]
    unnamed x2 -> x0, blocking collectives: 5.56 us -> none
  transfers between devices with their start and end apart: 15 -> 70, of which waited for: 15 -> 31; matrix products, arithmetic and copies ran while one was open for 5% -> 23% of each run, Pallas kernels for 0% -> 0%
where the time goes in v1:
time: 245 us; the launch traced here: 244 us
  starting transfers between devices  82.8 us (34%)
  waiting for transfers between devices  78.1 us (32%)
  local copies, waits for them, and re-layouts  39.5 us (16%)
  other arithmetic  20.9 us (9%)
  matrix products  20.5 us (8%)
  between operations  2.54 us (1%)
    ppermute x30, starting transfers between devices, pieces(): lax.ppermute(value, axis, [(i, (i + o) % count) for i in range(count)])  37.6 us
    ppermute x30, waiting for transfers between devices, pieces(): lax.ppermute(value, axis, [(i, (i + o) % count) for i in range(count)])  35.8 us
    ppermute x15, starting transfers between devices, scatter_rows(): lax.ppermute(block, axis, [(i, (i - o) % count) for i in range(count)])  23 us
    ppermute x15, waiting for transfers between devices, scatter_rows(): lax.ppermute(block, axis, [(i, (i - o) % count) for i in range(count)])  18.9 us
    ppermute x9, starting transfers between devices, axis_total(): lax.ppermute(block, axis, [(i, (i + o) % count) for i in range(count)])  14 us
    ppermute x9, waiting for transfers between devices, axis_total(): lax.ppermute(block, axis, [(i, (i + o) % count) for i in range(count)])  12.6 us
    unnamed x238, local copies, waits for them, and re-layouts  11 us
    ppermute x6, waiting for transfers between devices, axis_fill(): lax.ppermute(chunk, axis, [(i, (i - o) % count) for i in range(count)])  10.8 us
  transfers between devices with their start and end apart: 70, of which 31 were waited for; matrix products, arithmetic and copies ran while one was open for 23% of the time, Pallas kernels for 0%

profile of v1, /device:TPU:0, one launch (start us, length us, event | category | flops | bytes accessed | tf_op | source)
XLA Modules:
  0.0 244.4 jit_solution(15085410978928422613)
XLA Ops:
  1.3 1.3 reduce.19
  2.8 3.0 %collective-permute-start.8 = (s32[256]{0:T(256)S(1)}, s32[256]{0:T(256)S(1)}, u32[]{:S(2)}, u32[]{:S(2)}) collective-permute-start(s32[256]{0:T(256)S(1)} %get-tuple-element.68), channel_id=1, source_target_pairs={{0,4},{4,8},{8,12},{12,0},{1,5},{5,9},{9,13},{13,1},{2,6},{6,10},{... | collective-permute-start | bytes 3080 | tf_op jit(solution)/shard_map/ppermute | solution.py:68
  5.8 1.5 collective-permute-start.9
  7.3 1.4 collective-permute-start.10
  8.7 4.2 %concatenate.107 = bf16[1536]{0:T(1024)(128)(2,1)S(1)} concatenate(bf16[320]{0:T(512)(128)(2,1)} %param.19, bf16[320]{0:T(512)(128)(2,1)} %param.26, bf16[320]{0:T(512)(128)(2,1)} %param.27, bf16[320]{0:T(512)(128)(2,1)} %param.31, bf16[128]{0:T(256)(128)(2,1)} %param.23, bf16[128]{0:T(256)(128)(2,1)} %param.24), dimensions={0} | concatenate | bytes 6144 | tf_op jit(solution)/shard_map/concatenate | solution.py:195
  13.0 3.7 %collective-permute-start.2 = (bf16[64,640]{1,0:T(8,128)(2,1)}, bf16[64,640]{1,0:T(8,128)(2,1)S(1)}, u32[]{:S(2)}, u32[]{:S(2)}) collective-permute-start(bf16[64,640]{1,0:T(8,128)(2,1)} %bitcast.133), channel_id=1, source_target_pairs={{0,3},{1,0},{2,1},{3,2},{4,7},{5,4},{6,5},{7,6},{8,11},{9,8},{10,9... | collective-permute-start | bytes 245768 | tf_op jit(solution)/shard_map/ppermute | solution.py:68
  22.8 4.1 %collective-permute-done.1 = bf16[64,640]{1,0:T(8,128)(2,1)S(1)} collective-permute-done((bf16[64,640]{1,0:T(8,128)(2,1)}, bf16[64,640]{1,0:T(8,128)(2,1)S(1)}, u32[]{:S(2)}, u32[]{:S(2)}) %collective-permute-start.1) | collective-permute-done | bytes 81952 | tf_op jit(solution)/shard_map/ppermute | solution.py:68
  29.6 1.5 collective-permute-start.12
  34.1 1.4 collective-permute-done.13
  35.5 1.5 collective-permute-start.7
  40.5 4.8 %collective-permute-done.6 = bf16[256,256]{1,0:T(8,128)(2,1)S(1)} collective-permute-done((bf16[256,256]{1,0:T(8,128)(2,1)S(1)}, bf16[256,256]{1,0:T(8,128)(2,1)S(1)}, u32[]{:S(2)}, u32[]{:S(2)}) %collective-permute-start.6) | collective-permute-done | bytes 131104 | tf_op jit(solution)/shard_map/ppermute | solution.py:68
  46.4 1.8 collective-permute-start.16
  48.2 2.2 collective-permute-start.15
  50.5 2.2 collective-permute-done.17
  52.7 1.4 collective-permute-done.15
  55.0 2.6 %collective-permute-start.20 = (bf16[64,640]{1,0:T(8,128)(2,1)S(1)}, bf16[64,640]{1,0:T(8,128)(2,1)S(1)}, u32[]{:S(2)}, u32[]{:S(2)}) collective-permute-start(bf16[64,640]{1,0:T(8,128)(2,1)S(1)} %multiply_convert_fusion.6), channel_id=1, source_target_pairs={{0,3},{1,0},{2,1},{3,2},{4,7},{5,4},{6,5},{7,6},{8,11},{9,8},{10,9... | collective-permute-start | bytes 245768 | tf_op jit(solution)/shard_map/ppermute | solution.py:68
  58.3 1.4 collective-permute-done.20
  59.7 3.3 %collective-permute-done.19 = bf16[64,640]{1,0:T(8,128)(2,1)S(1)} collective-permute-done((bf16[64,640]{1,0:T(8,128)(2,1)S(1)}, bf16[64,640]{1,0:T(8,128)(2,1)S(1)}, u32[]{:S(2)}, u32[]{:S(2)}) %collective-permute-start.19) | collective-permute-done | bytes 81952 | tf_op jit(solution)/shard_map/ppermute | solution.py:68
  63.0 1.4 collective-permute-done.18
  68.9 2.8 %collective-permute-start.24 = (bf16[64,640]{1,0:T(8,128)(2,1)S(1)}, bf16[64,640]{1,0:T(8,128)(2,1)S(1)}, u32[]{:S(2)}, u32[]{:S(2)}) collective-permute-start(bf16[64,640]{1,0:T(8,128)(2,1)S(1)} %get-tuple-element.108), channel_id=1, source_target_pairs={{0,3},{1,0},{2,1},{3,2},{4,7},{5,4},{6,5},{7,6},{8,11},{9,8},{10,9... | collective-permute-start | bytes 245768 | tf_op jit(solution)/shard_map/ppermute | solution.py:84
  72.5 2.4 collective-permute-done.26
  78.2 4.6 %collective-permute-start.29 = (bf16[64,640]{1,0:T(8,128)(2,1)S(1)}, bf16[64,640]{1,0:T(8,128)(2,1)S(1)}, u32[]{:S(2)}, u32[]{:S(2)}) collective-permute-start(bf16[64,640]{1,0:T(8,128)(2,1)S(1)} %get-tuple-element.122), channel_id=1, source_target_pairs={{0,3},{1,0},{2,1},{3,2},{4,7},{5,4},{6,5},{7,6},{8,11},{9,8},{10,9... | collective-permute-start | bytes 245768 | tf_op jit(solution)/shard_map/ppermute | solution.py:68
  85.4 5.9 %collective-permute-done.28 = bf16[64,640]{1,0:T(8,128)(2,1)S(1)} collective-permute-done((bf16[64,640]{1,0:T(8,128)(2,1)S(1)}, bf16[64,640]{1,0:T(8,128)(2,1)S(1)}, u32[]{:S(2)}, u32[]{:S(2)}) %collective-permute-start.28) | collective-permute-done | bytes 81952 | tf_op jit(solution)/shard_map/ppermute | solution.py:68
  91.4 1.9 fusion.20
  94.3 1.7 collective-permute-start.31
  96.1 2.8 %collective-permute-start.30 = (bf16[64,640]{1,0:T(8,128)(2,1)S(1)}, bf16[64,640]{1,0:T(8,128)(2,1)S(1)}, u32[]{:S(2)}, u32[]{:S(2)}) collective-permute-start(bf16[64,640]{1,0:T(8,128)(2,1)S(1)} %get-tuple-element.105), channel_id=1, source_target_pairs={{0,3},{1,0},{2,1},{3,2},{4,7},{5,4},{6,5},{7,6},{8,11},{9,8},{10,9... | collective-permute-start | bytes 245768 | tf_op jit(solution)/shard_map/ppermute | solution.py:84
  101.1 2.5 %collective-permute-done.31 = bf16[64,640]{1,0:T(8,128)(2,1)S(1)} collective-permute-done((bf16[64,640]{1,0:T(8,128)(2,1)S(1)}, bf16[64,640]{1,0:T(8,128)(2,1)S(1)}, u32[]{:S(2)}, u32[]{:S(2)}) %collective-permute-start.31) | collective-permute-done | bytes 81952 | tf_op jit(solution)/shard_map/ppermute | solution.py:84
  105.7 3.0 %collective-permute-start.35 = (bf16[64,640]{1,0:T(8,128)(2,1)}, bf16[64,640]{1,0:T(8,128)(2,1)}, u32[]{:S(2)}, u32[]{:S(2)}) collective-permute-start(bf16[64,640]{1,0:T(8,128)(2,1)} %multiply_convert_fusion.5), channel_id=1, source_target_pairs={{0,3},{1,0},{2,1},{3,2},{4,7},{5,4},{6,5},{7,6},{8,11},{9,8},{10,9... | collective-permute-start | bytes 245768 | tf_op jit(solution)/shard_map/ppermute | solution.py:68
  109.3 1.5 constant_dynamic-slice_fusion.3
  110.8 2.4 copy.38
  115.3 1.4 fusion.36
  119.4 2.7 %collective-permute-start.38 = (bf16[256,512]{0,1:T(8,128)(2,1)S(1)}, bf16[256,512]{0,1:T(8,128)(2,1)S(1)}, u32[]{:S(2)}, u32[]{:S(2)}) collective-permute-start(bf16[256,512]{0,1:T(8,128)(2,1)S(1)} %get-tuple-element.80), channel_id=1, source_target_pairs={{0,4},{4,8},{8,12},{12,0},{1,5},{5,9},{9,13},{13,1},{2,6},{6,10},{... | collective-permute-start | bytes 786440 | tf_op jit(solution)/shard_map/ppermute | solution.py:84
  124.6 2.0 convolution_convert_fusion.7
  126.6 3.0 %collective-permute-done.38 = bf16[256,512]{0,1:T(8,128)(2,1)S(1)} collective-permute-done((bf16[256,512]{0,1:T(8,128)(2,1)S(1)}, bf16[256,512]{0,1:T(8,128)(2,1)S(1)}, u32[]{:S(2)}, u32[]{:S(2)}) %collective-permute-start.38) | collective-permute-done | bytes 262176 | tf_op jit(solution)/shard_map/ppermute | solution.py:84
  129.6 4.5 %collective-permute-done.37 = bf16[256,512]{0,1:T(8,128)(2,1)S(1)} collective-permute-done((bf16[256,512]{0,1:T(8,128)(2,1)S(1)}, bf16[256,512]{0,1:T(8,128)(2,1)S(1)}, u32[]{:S(2)}, u32[]{:S(2)}) %collective-permute-start.37) | collective-permute-done | bytes 262176 | tf_op jit(solution)/shard_map/ppermute | solution.py:84
  139.2 2.8 %collective-permute-start.41 = (bf16[64,640]{1,0:T(8,128)(2,1)}, bf16[64,640]{1,0:T(8,128)(2,1)}, u32[]{:S(2)}, u32[]{:S(2)}) collective-permute-start(bf16[64,640]{1,0:T(8,128)(2,1)} %get-tuple-element.103), channel_id=1, source_target_pairs={{0,1},{1,2},{2,3},{3,0},{4,5},{5,6},{6,7},{7,4},{8,9},{9,10},{10,1... | collective-permute-start | bytes 245768 | tf_op jit(solution)/shard_map/ppermute | solution.py:84
  142.4 1.4 convolution_convert_fusion.6
  145.6 1.9 collective-permute-start.45
  149.3 1.8 collective-permute-done.44
  151.1 1.7 collective-permute-done.43
  152.8 1.4 collective-permute-start.48
  154.3 1.6 collective-permute-start.46
  156.5 1.7 collective-permute-start.40
  158.9 1.6 collective-permute-start.39
  165.1 1.5 collective-permute-start.55
  166.6 1.9 collective-permute-start.54
  170.1 1.4 collective-permute-done.56
  171.5 1.4 collective-permute-start.51
  172.9 4.2 %collective-permute-start.50 = (bf16[80,512]{0,1:T(8,128)(2,1)S(1)}, bf16[80,512]{0,1:T(8,128)(2,1)S(1)}, u32[]{:S(2)}, u32[]{:S(2)}) collective-permute-start(bf16[80,512]{0,1:T(8,128)(2,1)S(1)} %get-tuple-element.96), channel_id=1, source_target_pairs={{0,4},{4,8},{8,12},{12,0},{1,5},{5,9},{9,13},{13,1},{2,6},{6,10},{... | collective-permute-start | bytes 245768 | tf_op jit(solution)/shard_map/ppermute | solution.py:124
  180.4 2.1 collective-permute-done.59
  182.5 4.5 %collective-permute-done.58 = bf16[80,512]{0,1:T(8,128)(2,1)S(1)} collective-permute-done((bf16[80,512]{0,1:T(8,128)(2,1)S(1)}, bf16[80,512]{0,1:T(8,128)(2,1)S(1)}, u32[]{:S(2)}, u32[]{:S(2)}) %collective-permute-start.58) | collective-permute-done | bytes 81952 | tf_op jit(solution)/shard_map/ppermute | solution.py:68
  187.2 2.0 collective-permute-start.60
  190.4 2.3 copy.39
  192.7 2.0 add_convert_fusion
  196.0 2.9 %collective-permute-start.66 = (bf16[80,1536]{0,1:T(8,128)(2,1)}, bf16[80,1536]{0,1:T(8,128)(2,1)}, u32[]{:S(2)}, u32[]{:S(2)}) collective-permute-start(bf16[80,1536]{0,1:T(8,128)(2,1)} %get-tuple-element.77), channel_id=1, source_target_pairs={{0,12},{4,0},{8,4},{12,8},{1,13},{5,1},{9,5},{13,9},{2,14},{6,2},{... | collective-permute-start | bytes 737288 | tf_op jit(solution)/shard_map/ppermute | solution.py:124
  199.9 1.7 fusion.67
  201.7 2.9 %concatenate.135 = bf16[640,1024]{0,1:T(8,128)(2,1)S(1)} concatenate(bf16[80,1024]{0,1:T(8,128)(2,1)S(1)} %pad_maximum_fusion.21, bf16[80,1024]{0,1:T(8,128)(2,1)} %collective-permute-done.60, bf16[80,1024]{0,1:T(8,128)(2,1)} %collective-permute-done.61, bf16[80,1024]{0,1:T(8,128)(2,1)} %collective-permute-done.62, bf16[80,1024]{0,1:T(8,128)(2,1)S(1)} %pad_maximum_fusion.21, ...), dimensions={0} | concatenate | bytes 2621440 | tf_op jit(solution)/shard_map/concatenate | solution.py:138
  204.9 3.9 %collective-permute-done.66 = bf16[80,1536]{0,1:T(8,128)(2,1)} collective-permute-done((bf16[80,1536]{0,1:T(8,128)(2,1)}, bf16[80,1536]{0,1:T(8,128)(2,1)}, u32[]{:S(2)}, u32[]{:S(2)}) %collective-permute-start.66) | collective-permute-done | bytes 245792 | tf_op jit(solution)/shard_map/ppermute | solution.py:124
  208.9 7.3 %collective-permute-done.65 = bf16[80,1536]{0,1:T(8,128)(2,1)} collective-permute-done((bf16[80,1536]{0,1:T(8,128)(2,1)}, bf16[80,1536]{0,1:T(8,128)(2,1)}, u32[]{:S(2)}, u32[]{:S(2)}) %collective-permute-start.65) | collective-permute-done | bytes 245792 | tf_op jit(solution)/shard_map/ppermute | solution.py:124
  216.2 1.5 add_convert_fusion.1
  219.6 1.6 collective-permute-start.69
  224.7 5.0 %collective-permute-done.67 = bf16[80,1536]{0,1:T(8,128)(2,1)S(1)} collective-permute-done((bf16[80,1536]{0,1:T(8,128)(2,1)S(1)}, bf16[80,1536]{0,1:T(8,128)(2,1)S(1)}, u32[]{:S(2)}, u32[]{:S(2)}) %collective-permute-start.67) | collective-permute-done | bytes 245792 | tf_op jit(solution)/shard_map/ppermute | solution.py:135
  229.7 5.7 %collective-permute-done.68 = bf16[80,1536]{0,1:T(8,128)(2,1)S(1)} collective-permute-done((bf16[80,1536]{0,1:T(8,128)(2,1)S(1)}, bf16[80,1536]{0,1:T(8,128)(2,1)S(1)}, u32[]{:S(2)}, u32[]{:S(2)}) %collective-permute-start.68) | collective-permute-done | bytes 245792 | tf_op jit(solution)/shard_map/ppermute | solution.py:135
  235.5 5.1 %concatenate.137 = bf16[640,1536]{0,1:T(8,128)(2,1)S(1)} concatenate(bf16[80,1536]{0,1:T(8,128)(2,1)S(1)} %add_convert_fusion.1, bf16[80,1536]{0,1:T(8,128)(2,1)S(1)} %collective-permute-done.67, bf16[80,1536]{0,1:T(8,128)(2,1)S(1)} %collective-permute-done.68, bf16[80,1536]{0,1:T(8,128)(2,1)S(1)} %collective-permute-done.69, bf16[80,1536]{0,1:T(8,128)(2,1)S(1)} %add_convert_fusion.1, ...), dimensions={0} | concatenate | bytes 3932160 | tf_op jit(solution)/shard_map/concatenate | solution.py:138
  (439 shorter events, 75.0 us)
Async XLA Ops:
  2.8 16.7 %collective-permute-start.8 = (s32[256]{0:T(256)S(1)}, s32[256]{0:T(256)S(1)}, u32[]{:S(2)}, u32[]{:S(2)}) collective-permute-start(s32[256]{0:T(256)S(1)} %get-tuple-element.68), channel_id=1, source_target_pairs={{0,4},{4,8},{8,12},{12,0},{1,5},{5,9},{9,13},{13,1},{2,6},{6,10},{... | collective-permute-start | bytes 3080 | tf_op jit(solution)/shard_map/ppermute | solution.py:68
  5.8 13.8 %collective-permute-start.9 = (s32[256]{0:T(256)S(1)}, s32[256]{0:T(256)S(1)}, u32[]{:S(2)}, u32[]{:S(2)}) collective-permute-start(s32[256]{0:T(256)S(1)} %get-tuple-element.68), channel_id=1, source_target_pairs={{0,8},{4,12},{8,0},{12,4},{1,9},{5,13},{9,1},{13,5},{2,10},{6,14},... | collective-permute-start | bytes 3080 | tf_op jit(solution)/shard_map/ppermute | solution.py:68
  7.3 13.3 %collective-permute-start.10 = (s32[256]{0:T(256)S(1)}, s32[256]{0:T(256)S(1)}, u32[]{:S(2)}, u32[]{:S(2)}) collective-permute-start(s32[256]{0:T(256)S(1)} %get-tuple-element.68), channel_id=1, source_target_pairs={{0,12},{4,0},{8,4},{12,8},{1,13},{5,1},{9,5},{13,9},{2,14},{6,2},{... | collective-permute-start | bytes 3080 | tf_op jit(solution)/shard_map/ppermute | solution.py:68
  12.9 8.3 %collective-permute-start.3 = (bf16[1,1536]{1,0:T(2,128)(2,1)S(1)}, bf16[1,1536]{1,0:T(2,128)(2,1)S(1)}, u32[]{:S(2)}, u32[]{:S(2)}) collective-permute-start(bf16[1,1536]{1,0:T(2,128)(2,1)S(1)} %reshape.504), channel_id=1, source_target_pairs={{0,16},{16,0},{1,17},{17,1},{2,18},{18,2},{3,19},{19,3},{4,20},{20... | collective-permute-start | bytes 9224 | tf_op jit(solution)/shard_map/ppermute | solution.py:94
  13.0 9.7 %collective-permute-start.2 = (bf16[64,640]{1,0:T(8,128)(2,1)}, bf16[64,640]{1,0:T(8,128)(2,1)S(1)}, u32[]{:S(2)}, u32[]{:S(2)}) collective-permute-start(bf16[64,640]{1,0:T(8,128)(2,1)} %bitcast.133), channel_id=1, source_target_pairs={{0,3},{1,0},{2,1},{3,2},{4,7},{5,4},{6,5},{7,6},{8,11},{9,8},{10,9... | collective-permute-start | bytes 245768 | tf_op jit(solution)/shard_map/ppermute | solution.py:68
  19.5 7.4 %collective-permute-start.1 = (bf16[64,640]{1,0:T(8,128)(2,1)}, bf16[64,640]{1,0:T(8,128)(2,1)S(1)}, u32[]{:S(2)}, u32[]{:S(2)}) collective-permute-start(bf16[64,640]{1,0:T(8,128)(2,1)} %bitcast.134), channel_id=1, source_target_pairs={{0,2},{1,3},{2,0},{3,1},{4,6},{5,7},{6,4},{7,5},{8,10},{9,11},{10,... | collective-permute-start | bytes 245768 | tf_op jit(solution)/shard_map/ppermute | solution.py:68
  19.5 7.4 %collective-permute-start = (bf16[64,640]{1,0:T(8,128)(2,1)}, bf16[64,640]{1,0:T(8,128)(2,1)S(1)}, u32[]{:S(2)}, u32[]{:S(2)}) collective-permute-start(bf16[64,640]{1,0:T(8,128)(2,1)} %bitcast.135), channel_id=1, source_target_pairs={{0,1},{1,2},{2,3},{3,0},{4,5},{5,6},{6,7},{7,4},{8,9},{9,10},{10,1... | collective-permute-start | bytes 245768 | tf_op jit(solution)/shard_map/ppermute | solution.py:68
  20.5 7.1 %collective-permute-start.21 = (bf16[320,512]{1,0:T(8,128)(2,1)}, bf16[320,512]{1,0:T(8,128)(2,1)S(1)}, u32[]{:S(2)}, u32[]{:S(2)}) collective-permute-start(bf16[320,512]{1,0:T(8,128)(2,1)} %param.28), channel_id=1, source_target_pairs={{0,16},{16,0},{1,17},{17,1},{2,18},{18,2},{3,19},{19,3},{4,20},{20... | collective-permute-start | bytes 983048 | tf_op jit(solution)/shard_map/ppermute | solution.py:94
  21.2 6.4 %collective-permute-start.14 = (bf16[256,320]{0,1:T(8,128)(2,1)}, bf16[256,320]{0,1:T(8,128)(2,1)S(1)}, u32[]{:S(2)}, u32[]{:S(2)}) collective-permute-start(bf16[256,320]{0,1:T(8,128)(2,1)} %param.25), channel_id=1, source_target_pairs={{0,16},{16,0},{1,17},{17,1},{2,18},{18,2},{3,19},{19,3},{4,20},{20... | collective-permute-start | bytes 491528 | tf_op jit(solution)/shard_map/ppermute | solution.py:94
  22.7 5.0 %collective-permute-start.4 = (bf16[320,768]{1,0:T(8,128)(2,1)S(1)}, bf16[320,768]{1,0:T(8,128)(2,1)S(1)}, u32[]{:S(2)}, u32[]{:S(2)}) collective-permute-start(bf16[320,768]{1,0:T(8,128)(2,1)S(1)} %constant_dynamic-update-slice_fusion), channel_id=1, source_target_pairs={{0,16},{16,0},{1,17},{17,1},{2,18},{18,2},{3,19},{19,3},{4,20},{20... | collective-permute-start | bytes 1474568 | tf_op jit(solution)/shard_map/ppermute | solution.py:94
  26.9 23.5 %collective-permute-start.22 = (bf16[320,512]{1,0:T(8,128)(2,1)}, bf16[320,512]{1,0:T(8,128)(2,1)S(1)}, u32[]{:S(2)}, u32[]{:S(2)}) collective-permute-start(bf16[320,512]{1,0:T(8,128)(2,1)} %param.29), channel_id=1, source_target_pairs={{0,16},{16,0},{1,17},{17,1},{2,18},{18,2},{3,19},{19,3},{4,20},{20... | collective-permute-start | bytes 983048 | tf_op jit(solution)/shard_map/ppermute | solution.py:94
  26.9 31.4 %collective-permute-start.23 = (bf16[512,320]{0,1:T(8,128)(2,1)}, bf16[512,320]{0,1:T(8,128)(2,1)S(1)}, u32[]{:S(2)}, u32[]{:S(2)}) collective-permute-start(bf16[512,320]{0,1:T(8,128)(2,1)} %param.30), channel_id=1, source_target_pairs={{0,16},{16,0},{1,17},{17,1},{2,18},{18,2},{3,19},{19,3},{4,20},{20... | collective-permute-start | bytes 983048 | tf_op jit(solution)/shard_map/ppermute | solution.py:94
  29.0 6.4 %collective-permute-start.13 = (bf16[256,256]{0,1:T(8,128)(2,1)S(1)}, bf16[256,256]{0,1:T(8,128)(2,1)S(1)}, u32[]{:S(2)}, u32[]{:S(2)}) collective-permute-start(bf16[256,256]{0,1:T(8,128)(2,1)S(1)} %pad_maximum_fusion.24), channel_id=1, source_target_pairs={{0,12},{4,0},{8,4},{12,8},{1,13},{5,1},{9,5},{13,9},{2,14},{6,2},{... | collective-permute-start | bytes 393224 | tf_op jit(solution)/shard_map/ppermute | solution.py:68
  29.6 8.0 %collective-permute-start.12 = (bf16[256,256]{0,1:T(8,128)(2,1)S(1)}, bf16[256,256]{0,1:T(8,128)(2,1)S(1)}, u32[]{:S(2)}, u32[]{:S(2)}) collective-permute-start(bf16[256,256]{0,1:T(8,128)(2,1)S(1)} %pad_maximum_fusion.24), channel_id=1, source_target_pairs={{0,8},{4,12},{8,0},{12,4},{1,9},{5,13},{9,1},{13,5},{2,10},{6,14},... | collective-permute-start | bytes 393224 | tf_op jit(solution)/shard_map/ppermute | solution.py:68
  31.1 7.6 %collective-permute-start.11 = (bf16[256,256]{0,1:T(8,128)(2,1)S(1)}, bf16[256,256]{0,1:T(8,128)(2,1)S(1)}, u32[]{:S(2)}, u32[]{:S(2)}) collective-permute-start(bf16[256,256]{0,1:T(8,128)(2,1)S(1)} %pad_maximum_fusion.24), channel_id=1, source_target_pairs={{0,4},{4,8},{8,12},{12,0},{1,5},{5,9},{9,13},{13,1},{2,6},{6,10},{... | collective-permute-start | bytes 393224 | tf_op jit(solution)/shard_map/ppermute | solution.py:68
  35.5 5.0 %collective-permute-start.7 = (bf16[256,256]{1,0:T(8,128)(2,1)S(1)}, bf16[256,256]{1,0:T(8,128)(2,1)S(1)}, u32[]{:S(2)}, u32[]{:S(2)}) collective-permute-start(bf16[256,256]{1,0:T(8,128)(2,1)S(1)} %convolution_convert_fusion.11), channel_id=1, source_target_pairs={{0,12},{4,0},{8,4},{12,8},{1,13},{5,1},{9,5},{13,9},{2,14},{6,2},{... | collective-permute-start | bytes 393224 | tf_op jit(solution)/shard_map/ppermute | solution.py:68
  37.6 7.6 %collective-permute-start.6 = (bf16[256,256]{1,0:T(8,128)(2,1)S(1)}, bf16[256,256]{1,0:T(8,128)(2,1)S(1)}, u32[]{:S(2)}, u32[]{:S(2)}) collective-permute-start(bf16[256,256]{1,0:T(8,128)(2,1)S(1)} %convolution_convert_fusion.11), channel_id=1, source_target_pairs={{0,8},{4,12},{8,0},{12,4},{1,9},{5,13},{9,1},{13,5},{2,10},{6,14},... | collective-permute-start | bytes 393224 | tf_op jit(solution)/shard_map/ppermute | solution.py:68
  38.8 6.5 %collective-permute-start.5 = (bf16[256,256]{1,0:T(8,128)(2,1)S(1)}, bf16[256,256]{1,0:T(8,128)(2,1)S(1)}, u32[]{:S(2)}, u32[]{:S(2)}) collective-permute-start(bf16[256,256]{1,0:T(8,128)(2,1)S(1)} %convolution_convert_fusion.11), channel_id=1, source_target_pairs={{0,4},{4,8},{8,12},{12,0},{1,5},{5,9},{9,13},{13,1},{2,6},{6,10},{... | collective-permute-start | bytes 393224 | tf_op jit(solution)/shard_map/ppermute | solution.py:68
  46.3 6.4 %collective-permute-start.17 = (bf16[64,640]{1,0:T(8,128)(2,1)S(1)}, bf16[64,640]{1,0:T(8,128)(2,1)S(1)}, u32[]{:S(2)}, u32[]{:S(2)}) collective-permute-start(bf16[64,640]{1,0:T(8,128)(2,1)S(1)} %get-tuple-element.112), channel_id=1, source_target_pairs={{0,1},{1,2},{2,3},{3,0},{4,5},{5,6},{6,7},{7,4},{8,9},{9,10},{10,1... | collective-permute-start | bytes 245768 | tf_op jit(solution)/shard_map/ppermute | solution.py:84
  46.4 6.3 %collective-permute-start.16 = (bf16[64,640]{1,0:T(8,128)(2,1)S(1)}, bf16[64,640]{1,0:T(8,128)(2,1)S(1)}, u32[]{:S(2)}, u32[]{:S(2)}) collective-permute-start(bf16[64,640]{1,0:T(8,128)(2,1)S(1)} %get-tuple-element.113), channel_id=1, source_target_pairs={{0,2},{1,3},{2,0},{3,1},{4,6},{5,7},{6,4},{7,5},{8,10},{9,11},{10,... | collective-permute-start | bytes 245768 | tf_op jit(solution)/shard_map/ppermute | solution.py:84
  48.2 5.9 %collective-permute-start.15 = (bf16[64,640]{1,0:T(8,128)(2,1)S(1)}, bf16[64,640]{1,0:T(8,128)(2,1)S(1)}, u32[]{:S(2)}, u32[]{:S(2)}) collective-permute-start(bf16[64,640]{1,0:T(8,128)(2,1)S(1)} %get-tuple-element.111), channel_id=1, source_target_pairs={{0,3},{1,0},{2,1},{3,2},{4,7},{5,4},{6,5},{7,6},{8,11},{9,8},{10,9... | collective-permute-start | bytes 245768 | tf_op jit(solution)/shard_map/ppermute | solution.py:84
  55.0 4.7 %collective-permute-start.20 = (bf16[64,640]{1,0:T(8,128)(2,1)S(1)}, bf16[64,640]{1,0:T(8,128)(2,1)S(1)}, u32[]{:S(2)}, u32[]{:S(2)}) collective-permute-start(bf16[64,640]{1,0:T(8,128)(2,1)S(1)} %multiply_convert_fusion.6), channel_id=1, source_target_pairs={{0,3},{1,0},{2,1},{3,2},{4,7},{5,4},{6,5},{7,6},{8,11},{9,8},{10,9... | collective-permute-start | bytes 245768 | tf_op jit(solution)/shard_map/ppermute | solution.py:68
  57.6 5.3 %collective-permute-start.19 = (bf16[64,640]{1,0:T(8,128)(2,1)S(1)}, bf16[64,640]{1,0:T(8,128)(2,1)S(1)}, u32[]{:S(2)}, u32[]{:S(2)}) collective-permute-start(bf16[64,640]{1,0:T(8,128)(2,1)S(1)} %multiply_convert_fusion.6), channel_id=1, source_target_pairs={{0,2},{1,3},{2,0},{3,1},{4,6},{5,7},{6,4},{7,5},{8,10},{9,11},{10,... | collective-permute-start | bytes 245768 | tf_op jit(solution)/shard_map/ppermute | solution.py:68
  58.1 6.2 %collective-permute-start.18 = (bf16[64,640]{1,0:T(8,128)(2,1)S(1)}, bf16[64,640]{1,0:T(8,128)(2,1)S(1)}, u32[]{:S(2)}, u32[]{:S(2)}) collective-permute-start(bf16[64,640]{1,0:T(8,128)(2,1)S(1)} %multiply_convert_fusion.6), channel_id=1, source_target_pairs={{0,1},{1,2},{2,3},{3,0},{4,5},{5,6},{6,7},{7,4},{8,9},{9,10},{10,1... | collective-permute-start | bytes 245768 | tf_op jit(solution)/shard_map/ppermute | solution.py:68
  67.9 7.0 %collective-permute-start.26 = (bf16[64,640]{1,0:T(8,128)(2,1)}, bf16[64,640]{1,0:T(8,128)(2,1)S(1)}, u32[]{:S(2)}, u32[]{:S(2)}) collective-permute-start(bf16[64,640]{1,0:T(8,128)(2,1)} %get-tuple-element.109), channel_id=1, source_target_pairs={{0,1},{1,2},{2,3},{3,0},{4,5},{5,6},{6,7},{7,4},{8,9},{9,10},{10,1... | collective-permute-start | bytes 245768 | tf_op jit(solution)/shard_map/ppermute | solution.py:84
  67.9 7.0 %collective-permute-start.25 = (bf16[64,640]{1,0:T(8,128)(2,1)}, bf16[64,640]{1,0:T(8,128)(2,1)S(1)}, u32[]{:S(2)}, u32[]{:S(2)}) collective-permute-start(bf16[64,640]{1,0:T(8,128)(2,1)} %get-tuple-element.110), channel_id=1, source_target_pairs={{0,2},{1,3},{2,0},{3,1},{4,6},{5,7},{6,4},{7,5},{8,10},{9,11},{10,... | collective-permute-start | bytes 245768 | tf_op jit(solution)/shard_map/ppermute | solution.py:84
  68.9 7.2 %collective-permute-start.24 = (bf16[64,640]{1,0:T(8,128)(2,1)S(1)}, bf16[64,640]{1,0:T(8,128)(2,1)S(1)}, u32[]{:S(2)}, u32[]{:S(2)}) collective-permute-start(bf16[64,640]{1,0:T(8,128)(2,1)S(1)} %get-tuple-element.108), channel_id=1, source_target_pairs={{0,3},{1,0},{2,1},{3,2},{4,7},{5,4},{6,5},{7,6},{8,11},{9,8},{10,9... | collective-permute-start | bytes 245768 | tf_op jit(solution)/shard_map/ppermute | solution.py:84
  78.2 7.3 %collective-permute-start.29 = (bf16[64,640]{1,0:T(8,128)(2,1)S(1)}, bf16[64,640]{1,0:T(8,128)(2,1)S(1)}, u32[]{:S(2)}, u32[]{:S(2)}) collective-permute-start(bf16[64,640]{1,0:T(8,128)(2,1)S(1)} %get-tuple-element.122), channel_id=1, source_target_pairs={{0,3},{1,0},{2,1},{3,2},{4,7},{5,4},{6,5},{7,6},{8,11},{9,8},{10,9... | collective-permute-start | bytes 245768 | tf_op jit(solution)/shard_map/ppermute | solution.py:68
  82.8 8.6 %collective-permute-start.28 = (bf16[64,640]{1,0:T(8,128)(2,1)S(1)}, bf16[64,640]{1,0:T(8,128)(2,1)S(1)}, u32[]{:S(2)}, u32[]{:S(2)}) collective-permute-start(bf16[64,640]{1,0:T(8,128)(2,1)S(1)} %get-tuple-element.122), channel_id=1, source_target_pairs={{0,2},{1,3},{2,0},{3,1},{4,6},{5,7},{6,4},{7,5},{8,10},{9,11},{10,... | collective-permute-start | bytes 245768 | tf_op jit(solution)/shard_map/ppermute | solution.py:68
  83.6 7.8 %collective-permute-start.27 = (bf16[64,640]{1,0:T(8,128)(2,1)S(1)}, bf16[64,640]{1,0:T(8,128)(2,1)S(1)}, u32[]{:S(2)}, u32[]{:S(2)}) collective-permute-start(bf16[64,640]{1,0:T(8,128)(2,1)S(1)} %get-tuple-element.122), channel_id=1, source_target_pairs={{0,1},{1,2},{2,3},{3,0},{4,5},{5,6},{6,7},{7,4},{8,9},{9,10},{10,1... | collective-permute-start | bytes 245768 | tf_op jit(solution)/shard_map/ppermute | solution.py:68
  94.3 6.8 %collective-permute-start.32 = (bf16[64,640]{1,0:T(8,128)(2,1)S(1)}, bf16[64,640]{1,0:T(8,128)(2,1)S(1)}, u32[]{:S(2)}, u32[]{:S(2)}) collective-permute-start(bf16[64,640]{1,0:T(8,128)(2,1)S(1)} %get-tuple-element.106), channel_id=1, source_target_pairs={{0,1},{1,2},{2,3},{3,0},{4,5},{5,6},{6,7},{7,4},{8,9},{9,10},{10,1... | collective-permute-start | bytes 245768 | tf_op jit(solution)/shard_map/ppermute | solution.py:84
  94.3 9.2 %collective-permute-start.31 = (bf16[64,640]{1,0:T(8,128)(2,1)S(1)}, bf16[64,640]{1,0:T(8,128)(2,1)S(1)}, u32[]{:S(2)}, u32[]{:S(2)}) collective-permute-start(bf16[64,640]{1,0:T(8,128)(2,1)S(1)} %get-tuple-element.107), channel_id=1, source_target_pairs={{0,2},{1,3},{2,0},{3,1},{4,6},{5,7},{6,4},{7,5},{8,10},{9,11},{10,... | collective-permute-start | bytes 245768 | tf_op jit(solution)/shard_map/ppermute | solution.py:84
  96.1 7.5 %collective-permute-start.30 = (bf16[64,640]{1,0:T(8,128)(2,1)S(1)}, bf16[64,640]{1,0:T(8,128)(2,1)S(1)}, u32[]{:S(2)}, u32[]{:S(2)}) collective-permute-start(bf16[64,640]{1,0:T(8,128)(2,1)S(1)} %get-tuple-element.105), channel_id=1, source_target_pairs={{0,3},{1,0},{2,1},{3,2},{4,7},{5,4},{6,5},{7,6},{8,11},{9,8},{10,9... | collective-permute-start | bytes 245768 | tf_op jit(solution)/shard_map/ppermute | solution.py:84
  105.7 8.8 %collective-permute-start.35 = (bf16[64,640]{1,0:T(8,128)(2,1)}, bf16[64,640]{1,0:T(8,128)(2,1)}, u32[]{:S(2)}, u32[]{:S(2)}) collective-permute-start(bf16[64,640]{1,0:T(8,128)(2,1)} %multiply_convert_fusion.5), channel_id=1, source_target_pairs={{0,3},{1,0},{2,1},{3,2},{4,7},{5,4},{6,5},{7,6},{8,11},{9,8},{10,9... | collective-permute-start | bytes 245768 | tf_op jit(solution)/shard_map/ppermute | solution.py:68
  108.7 5.8 %collective-permute-start.34 = (bf16[64,640]{1,0:T(8,128)(2,1)}, bf16[64,640]{1,0:T(8,128)(2,1)}, u32[]{:S(2)}, u32[]{:S(2)}) collective-permute-start(bf16[64,640]{1,0:T(8,128)(2,1)} %multiply_convert_fusion.5), channel_id=1, source_target_pairs={{0,2},{1,3},{2,0},{3,1},{4,6},{5,7},{6,4},{7,5},{8,10},{9,11},{10,... | collective-permute-start | bytes 245768 | tf_op jit(solution)/shard_map/ppermute | solution.py:68
  108.7 6.6 %collective-permute-start.33 = (bf16[64,640]{1,0:T(8,128)(2,1)}, bf16[64,640]{1,0:T(8,128)(2,1)}, u32[]{:S(2)}, u32[]{:S(2)}) collective-permute-start(bf16[64,640]{1,0:T(8,128)(2,1)} %multiply_convert_fusion.5), channel_id=1, source_target_pairs={{0,1},{1,2},{2,3},{3,0},{4,5},{5,6},{6,7},{7,4},{8,9},{9,10},{10,1... | collective-permute-start | bytes 245768 | tf_op jit(solution)/shard_map/ppermute | solution.py:68
  113.2 77.1 %collective-permute-start.63 = (bf16[320,1536]{1,0:T(8,128)(2,1)}, bf16[320,1536]{1,0:T(8,128)(2,1)}, u32[]{:S(2)}, u32[]{:S(2)}) collective-permute-start(bf16[320,1536]{1,0:T(8,128)(2,1)} %copy.38), channel_id=1, source_target_pairs={{0,16},{16,0},{1,17},{17,1},{2,18},{18,2},{3,19},{19,3},{4,20},{20... | collective-permute-start | bytes 2949128 | tf_op jit(solution)/shard_map/ppermute | solution.py:110
  119.4 10.2 %collective-permute-start.38 = (bf16[256,512]{0,1:T(8,128)(2,1)S(1)}, bf16[256,512]{0,1:T(8,128)(2,1)S(1)}, u32[]{:S(2)}, u32[]{:S(2)}) collective-permute-start(bf16[256,512]{0,1:T(8,128)(2,1)S(1)} %get-tuple-element.80), channel_id=1, source_target_pairs={{0,4},{4,8},{8,12},{12,0},{1,5},{5,9},{9,13},{13,1},{2,6},{6,10},{... | collective-permute-start | bytes 786440 | tf_op jit(solution)/shard_map/ppermute | solution.py:84
  122.1 12.0 %collective-permute-start.37 = (bf16[256,512]{0,1:T(8,128)(2,1)S(1)}, bf16[256,512]{0,1:T(8,128)(2,1)S(1)}, u32[]{:S(2)}, u32[]{:S(2)}) collective-permute-start(bf16[256,512]{0,1:T(8,128)(2,1)S(1)} %get-tuple-element.81), channel_id=1, source_target_pairs={{0,8},{4,12},{8,0},{12,4},{1,9},{5,13},{9,1},{13,5},{2,10},{6,14},... | collective-permute-start | bytes 786440 | tf_op jit(solution)/shard_map/ppermute | solution.py:84
  122.6 11.5 %collective-permute-start.36 = (bf16[256,512]{0,1:T(8,128)(2,1)S(1)}, bf16[256,512]{0,1:T(8,128)(2,1)S(1)}, u32[]{:S(2)}, u32[]{:S(2)}) collective-permute-start(bf16[256,512]{0,1:T(8,128)(2,1)S(1)} %get-tuple-element.79), channel_id=1, source_target_pairs={{0,12},{4,0},{8,4},{12,8},{1,13},{5,1},{9,5},{13,9},{2,14},{6,2},{... | collective-permute-start | bytes 786440 | tf_op jit(solution)/shard_map/ppermute | solution.py:84
  139.2 22.5 %collective-permute-start.41 = (bf16[64,640]{1,0:T(8,128)(2,1)}, bf16[64,640]{1,0:T(8,128)(2,1)}, u32[]{:S(2)}, u32[]{:S(2)}) collective-permute-start(bf16[64,640]{1,0:T(8,128)(2,1)} %get-tuple-element.103), channel_id=1, source_target_pairs={{0,1},{1,2},{2,3},{3,0},{4,5},{5,6},{6,7},{7,4},{8,9},{9,10},{10,1... | collective-permute-start | bytes 245768 | tf_op jit(solution)/shard_map/ppermute | solution.py:84
  148.2 4.5 %collective-permute-start.43 = (bf16[1,1536]{1,0:T(2,128)(2,1)S(1)}, bf16[1,1536]{1,0:T(2,128)(2,1)S(1)}, u32[]{:S(2)}, u32[]{:S(2)}) collective-permute-start(bf16[1,1536]{1,0:T(2,128)(2,1)S(1)} %convert_bitcast_fusion), channel_id=1, source_target_pairs={{0,4},{4,8},{8,12},{12,0},{1,5},{5,9},{9,13},{13,1},{2,6},{6,10},{... | collective-permute-start | bytes 9224 | tf_op jit(solution)/shard_map/ppermute | solution.py:68
  154.2 4.6 %collective-permute-start.47 = (bf16[1,1536]{1,0:T(2,128)(2,1)S(1)}, bf16[1,1536]{1,0:T(2,128)(2,1)S(1)}, u32[]{:S(2)}, u32[]{:S(2)}) collective-permute-start(bf16[1,1536]{1,0:T(2,128)(2,1)S(1)} %add_convert_fusion.7), channel_id=1, source_target_pairs={{0,2},{1,3},{2,0},{3,1},{4,6},{5,7},{6,4},{7,5},{8,10},{9,11},{10,... | collective-permute-start | bytes 9224 | tf_op jit(solution)/shard_map/ppermute | solution.py:68
  154.3 6.2 %collective-permute-start.46 = (bf16[1,1536]{1,0:T(2,128)(2,1)S(1)}, bf16[1,1536]{1,0:T(2,128)(2,1)S(1)}, u32[]{:S(2)}, u32[]{:S(2)}) collective-permute-start(bf16[1,1536]{1,0:T(2,128)(2,1)S(1)} %add_convert_fusion.7), channel_id=1, source_target_pairs={{0,1},{1,2},{2,3},{3,0},{4,5},{5,6},{6,7},{7,4},{8,9},{9,10},{10,1... | collective-permute-start | bytes 9224 | tf_op jit(solution)/shard_map/ppermute | solution.py:68
  156.5 5.8 %collective-permute-start.40 = (bf16[64,640]{1,0:T(8,128)(2,1)S(1)}, bf16[64,640]{1,0:T(8,128)(2,1)S(1)}, u32[]{:S(2)}, u32[]{:S(2)}) collective-permute-start(bf16[64,640]{1,0:T(8,128)(2,1)S(1)} %copy-done.55), channel_id=1, source_target_pairs={{0,2},{1,3},{2,0},{3,1},{4,6},{5,7},{6,4},{7,5},{8,10},{9,11},{10,... | collective-permute-start | bytes 245768 | tf_op jit(solution)/shard_map/ppermute | solution.py:84
  161.7 6.8 %collective-permute-start.49 = (bf16[320,512]{0,1:T(8,128)(2,1)S(1)}, bf16[320,512]{0,1:T(8,128)(2,1)S(1)}, u32[]{:S(2)}, u32[]{:S(2)}) collective-permute-start(bf16[320,512]{0,1:T(8,128)(2,1)S(1)} %fusion.29), channel_id=1, source_target_pairs={{0,16},{16,0},{1,17},{17,1},{2,18},{18,2},{3,19},{19,3},{4,20},{20... | collective-permute-start | bytes 983048 | tf_op jit(solution)/shard_map/ppermute | solution.py:110
  165.1 6.4 %collective-permute-start.56 = (bf16[80,512]{0,1:T(8,128)(2,1)S(1)}, bf16[80,512]{0,1:T(8,128)(2,1)S(1)}, u32[]{:S(2)}, u32[]{:S(2)}) collective-permute-start(bf16[80,512]{0,1:T(8,128)(2,1)S(1)} %get-tuple-element.100), channel_id=1, source_target_pairs={{0,12},{4,0},{8,4},{12,8},{1,13},{5,1},{9,5},{13,9},{2,14},{6,2},{... | collective-permute-start | bytes 245768 | tf_op jit(solution)/shard_map/ppermute | solution.py:124
  165.1 7.8 %collective-permute-start.55 = (bf16[80,512]{0,1:T(8,128)(2,1)S(1)}, bf16[80,512]{0,1:T(8,128)(2,1)S(1)}, u32[]{:S(2)}, u32[]{:S(2)}) collective-permute-start(bf16[80,512]{0,1:T(8,128)(2,1)S(1)} %get-tuple-element.101), channel_id=1, source_target_pairs={{0,8},{4,12},{8,0},{12,4},{1,9},{5,13},{9,1},{13,5},{2,10},{6,14},... | collective-permute-start | bytes 245768 | tf_op jit(solution)/shard_map/ppermute | solution.py:124
  166.6 10.5 %collective-permute-start.54 = (bf16[80,512]{0,1:T(8,128)(2,1)S(1)}, bf16[80,512]{0,1:T(8,128)(2,1)S(1)}, u32[]{:S(2)}, u32[]{:S(2)}) collective-permute-start(bf16[80,512]{0,1:T(8,128)(2,1)S(1)} %get-tuple-element.99), channel_id=1, source_target_pairs={{0,4},{4,8},{8,12},{12,0},{1,5},{5,9},{9,13},{13,1},{2,6},{6,10},{... | collective-permute-start | bytes 245768 | tf_op jit(solution)/shard_map/ppermute | solution.py:124
  169.1 9.3 %collective-permute-start.52 = (bf16[80,512]{0,1:T(8,128)(2,1)S(1)}, bf16[80,512]{0,1:T(8,128)(2,1)S(1)}, u32[]{:S(2)}, u32[]{:S(2)}) collective-permute-start(bf16[80,512]{0,1:T(8,128)(2,1)S(1)} %get-tuple-element.97), channel_id=1, source_target_pairs={{0,12},{4,0},{8,4},{12,8},{1,13},{5,1},{9,5},{13,9},{2,14},{6,2},{... | collective-permute-start | bytes 245768 | tf_op jit(solution)/shard_map/ppermute | solution.py:124
  171.5 7.7 %collective-permute-start.51 = (bf16[80,512]{0,1:T(8,128)(2,1)S(1)}, bf16[80,512]{0,1:T(8,128)(2,1)S(1)}, u32[]{:S(2)}, u32[]{:S(2)}) collective-permute-start(bf16[80,512]{0,1:T(8,128)(2,1)S(1)} %get-tuple-element.98), channel_id=1, source_target_pairs={{0,8},{4,12},{8,0},{12,4},{1,9},{5,13},{9,1},{13,5},{2,10},{6,14},... | collective-permute-start | bytes 245768 | tf_op jit(solution)/shard_map/ppermute | solution.py:124
  172.9 7.4 %collective-permute-start.50 = (bf16[80,512]{0,1:T(8,128)(2,1)S(1)}, bf16[80,512]{0,1:T(8,128)(2,1)S(1)}, u32[]{:S(2)}, u32[]{:S(2)}) collective-permute-start(bf16[80,512]{0,1:T(8,128)(2,1)S(1)} %get-tuple-element.96), channel_id=1, source_target_pairs={{0,4},{4,8},{8,12},{12,0},{1,5},{5,9},{9,13},{13,1},{2,6},{6,10},{... | collective-permute-start | bytes 245768 | tf_op jit(solution)/shard_map/ppermute | solution.py:124
  177.2 5.3 %collective-permute-start.59 = (bf16[80,512]{0,1:T(8,128)(2,1)S(1)}, bf16[80,512]{0,1:T(8,128)(2,1)S(1)}, u32[]{:S(2)}, u32[]{:S(2)}) collective-permute-start(bf16[80,512]{0,1:T(8,128)(2,1)S(1)} %add_convert_fusion.5), channel_id=1, source_target_pairs={{0,3},{1,0},{2,1},{3,2},{4,7},{5,4},{6,5},{7,6},{8,11},{9,8},{10,9... | collective-permute-start | bytes 245768 | tf_op jit(solution)/shard_map/ppermute | solution.py:68
  178.4 8.7 %collective-permute-start.58 = (bf16[80,512]{0,1:T(8,128)(2,1)S(1)}, bf16[80,512]{0,1:T(8,128)(2,1)S(1)}, u32[]{:S(2)}, u32[]{:S(2)}) collective-permute-start(bf16[80,512]{0,1:T(8,128)(2,1)S(1)} %add_convert_fusion.5), channel_id=1, source_target_pairs={{0,2},{1,3},{2,0},{3,1},{4,6},{5,7},{6,4},{7,5},{8,10},{9,11},{10,... | collective-permute-start | bytes 245768 | tf_op jit(solution)/shard_map/ppermute | solution.py:68
  179.2 7.9 %collective-permute-start.57 = (bf16[80,512]{0,1:T(8,128)(2,1)S(1)}, bf16[80,512]{0,1:T(8,128)(2,1)S(1)}, u32[]{:S(2)}, u32[]{:S(2)}) collective-permute-start(bf16[80,512]{0,1:T(8,128)(2,1)S(1)} %add_convert_fusion.5), channel_id=1, source_target_pairs={{0,1},{1,2},{2,3},{3,0},{4,5},{5,6},{6,7},{7,4},{8,9},{9,10},{10,1... | collective-permute-start | bytes 245768 | tf_op jit(solution)/shard_map/ppermute | solution.py:68
  187.2 12.7 %collective-permute-start.60 = (bf16[80,1024]{0,1:T(8,128)(2,1)S(1)}, bf16[80,1024]{0,1:T(8,128)(2,1)}, u32[]{:S(2)}, u32[]{:S(2)}) collective-permute-start(bf16[80,1024]{0,1:T(8,128)(2,1)S(1)} %pad_maximum_fusion.21), channel_id=1, source_target_pairs={{0,12},{4,0},{8,4},{12,8},{1,13},{5,1},{9,5},{13,9},{2,14},{6,2},{... | collective-permute-start | bytes 491528 | tf_op jit(solution)/shard_map/ppermute | solution.py:135
  189.2 12.4 %collective-permute-start.61 = (bf16[80,1024]{0,1:T(8,128)(2,1)S(1)}, bf16[80,1024]{0,1:T(8,128)(2,1)}, u32[]{:S(2)}, u32[]{:S(2)}) collective-permute-start(bf16[80,1024]{0,1:T(8,128)(2,1)S(1)} %pad_maximum_fusion.21), channel_id=1, source_target_pairs={{0,8},{4,12},{8,0},{12,4},{1,9},{5,13},{9,1},{13,5},{2,10},{6,14},... | collective-permute-start | bytes 491528 | tf_op jit(solution)/shard_map/ppermute | solution.py:135
  190.3 11.3 %collective-permute-start.62 = (bf16[80,1024]{0,1:T(8,128)(2,1)S(1)}, bf16[80,1024]{0,1:T(8,128)(2,1)}, u32[]{:S(2)}, u32[]{:S(2)}) collective-permute-start(bf16[80,1024]{0,1:T(8,128)(2,1)S(1)} %pad_maximum_fusion.21), channel_id=1, source_target_pairs={{0,4},{4,8},{8,12},{12,0},{1,5},{5,9},{9,13},{13,1},{2,6},{6,10},{... | collective-permute-start | bytes 491528 | tf_op jit(solution)/shard_map/ppermute | solution.py:135
  196.0 12.8 %collective-permute-start.66 = (bf16[80,1536]{0,1:T(8,128)(2,1)}, bf16[80,1536]{0,1:T(8,128)(2,1)}, u32[]{:S(2)}, u32[]{:S(2)}) collective-permute-start(bf16[80,1536]{0,1:T(8,128)(2,1)} %get-tuple-element.77), channel_id=1, source_target_pairs={{0,12},{4,0},{8,4},{12,8},{1,13},{5,1},{9,5},{13,9},{2,14},{6,2},{... | collective-permute-start | bytes 737288 | tf_op jit(solution)/shard_map/ppermute | solution.py:124
  199.0 17.2 %collective-permute-start.65 = (bf16[80,1536]{0,1:T(8,128)(2,1)}, bf16[80,1536]{0,1:T(8,128)(2,1)}, u32[]{:S(2)}, u32[]{:S(2)}) collective-permute-start(bf16[80,1536]{0,1:T(8,128)(2,1)} %get-tuple-element.78), channel_id=1, source_target_pairs={{0,8},{4,12},{8,0},{12,4},{1,9},{5,13},{9,1},{13,5},{2,10},{6,14},... | collective-permute-start | bytes 737288 | tf_op jit(solution)/shard_map/ppermute | solution.py:124
  199.9 16.3 %collective-permute-start.64 = (bf16[80,1536]{0,1:T(8,128)(2,1)S(1)}, bf16[80,1536]{0,1:T(8,128)(2,1)}, u32[]{:S(2)}, u32[]{:S(2)}) collective-permute-start(bf16[80,1536]{0,1:T(8,128)(2,1)S(1)} %get-tuple-element.76), channel_id=1, source_target_pairs={{0,4},{4,8},{8,12},{12,0},{1,5},{5,9},{9,13},{13,1},{2,6},{6,10},{... | collective-permute-start | bytes 737288 | tf_op jit(solution)/shard_map/ppermute | solution.py:124
  217.7 12.0 %collective-permute-start.67 = (bf16[80,1536]{0,1:T(8,128)(2,1)S(1)}, bf16[80,1536]{0,1:T(8,128)(2,1)S(1)}, u32[]{:S(2)}, u32[]{:S(2)}) collective-permute-start(bf16[80,1536]{0,1:T(8,128)(2,1)S(1)} %add_convert_fusion.1), channel_id=1, source_target_pairs={{0,12},{4,0},{8,4},{12,8},{1,13},{5,1},{9,5},{13,9},{2,14},{6,2},{... | collective-permute-start | bytes 737288 | tf_op jit(solution)/shard_map/ppermute | solution.py:135
  218.9 16.6 %collective-permute-start.68 = (bf16[80,1536]{0,1:T(8,128)(2,1)S(1)}, bf16[80,1536]{0,1:T(8,128)(2,1)S(1)}, u32[]{:S(2)}, u32[]{:S(2)}) collective-permute-start(bf16[80,1536]{0,1:T(8,128)(2,1)S(1)} %add_convert_fusion.1), channel_id=1, source_target_pairs={{0,8},{4,12},{8,0},{12,4},{1,9},{5,13},{9,1},{13,5},{2,10},{6,14},... | collective-permute-start | bytes 737288 | tf_op jit(solution)/shard_map/ppermute | solution.py:135
  219.6 15.9 %collective-permute-start.69 = (bf16[80,1536]{0,1:T(8,128)(2,1)S(1)}, bf16[80,1536]{0,1:T(8,128)(2,1)S(1)}, u32[]{:S(2)}, u32[]{:S(2)}) collective-permute-start(bf16[80,1536]{0,1:T(8,128)(2,1)S(1)} %add_convert_fusion.1), channel_id=1, source_target_pairs={{0,4},{4,8},{8,12},{12,0},{1,5},{5,9},{9,13},{13,1},{2,6},{6,10},{... | collective-permute-start | bytes 737288 | tf_op jit(solution)/shard_map/ppermute | solution.py:135
  (120 other events, 639.4 us)

commit v2 on v1

--- a/solution.py
+++ b/solution.py
@@ -1,8 +1,11 @@
+import functools
 import math
 
 import jax
 import jax.numpy as jnp
 from jax import lax
+from jax.experimental import pallas as pl
+from jax.experimental.pallas import tpu as pltpu
 from jax.sharding import PartitionSpec as P
 
 epsilon = 1e-06
@@ -147,7 +150,7 @@
     return total
 
 
-def body(
+def plain_body(
     hidden_in,
     positions,
     cotangent,
@@ -392,6 +395,568 @@
     )
 
 
+def run(kernel, outs, *args, scalars=None, scratch=()):
+    vmem = pl.BlockSpec(memory_space=pltpu.VMEM)
+    specs = [vmem] * len(args)
+    if scalars is not None:
+        specs = [pl.BlockSpec(memory_space=pltpu.SMEM)] + specs
+        args = (scalars,) + args
+    return pl.pallas_call(
+        kernel,
+        out_shape=[jax.ShapeDtypeStruct(shape, kind) for shape, kind in outs],
+        in_specs=specs,
+        out_specs=[vmem] * len(outs),
+        scratch_shapes=list(scratch),
+        compiler_params=pltpu.CompilerParams(vmem_limit_bytes=24 * 1024 * 1024),
+    )(*args)
+
+
+def store_blocks(value, refs):
+    rows = refs[0].shape[0]
+    for o, ref in enumerate(refs):
+        ref[...] = value[o * rows : (o + 1) * rows].astype(ref.dtype)
+
+
+def total_of(refs):
+    total = refs[0][...].astype(full)
+    for ref in refs[1:]:
+        total = total + ref[...].astype(full)
+    return total
+
+
+def unit_of(value):
+    scale = rms_scale(value)
+    return value * scale, scale
+
+
+def query_kernel(rows, gd, gh, cos, sin, wq, wk, wv, q_rot, q_unit, q_scale, k_rot, val):
+    unit, _ = unit_of(rows[...].astype(full))
+    normed = (unit * gd[0:1, :]).astype(low)
+    key_unit, _ = unit_of(dot(normed, wk[...]))
+    k_rot[...] = rotate(key_unit * gh[1:2, :], cos[...], sin[...]).astype(low)
+    val[...] = dot(normed, wv[...]).astype(low)
+    query_unit, query_scale = unit_of(dot(normed, wq[...]))
+    q_unit[...] = query_unit
+    q_scale[...] = query_scale
+    q_rot[...] = rotate(query_unit * gh[0:1, :], cos[...], sin[...]).astype(low)
+
+
+def attend_kernel(n, *refs):
+    q_rot, k_own, v_own = refs[:3]
+    others = refs[3 : 2 + n]
+    gd, gh, cos, sin, wk, wv, wot, at_query, at_key = refs[2 + n : 11 + n]
+    k_all, v_all, context, probs = refs[11 + n : 15 + n]
+    blocks = refs[15 + n :]
+    rows = k_own.shape[0]
+    k_all[0:rows, :] = k_own[...]
+    v_all[0:rows, :] = v_own[...]
+    for o, other in enumerate(others, 1):
+        at = slice(o * rows, (o + 1) * rows)
+        unit, _ = unit_of(other[...].astype(full))
+        normed = (unit * gd[0:1, :]).astype(low)
+        key_unit, _ = unit_of(dot(normed, wk[...]))
+        k_all[at, :] = rotate(key_unit * gh[1:2, :], cos[at, :], sin[at, :]).astype(low)
+        v_all[at, :] = dot(normed, wv[...]).astype(low)
+    factor = 1.0 / math.sqrt(q_rot.shape[1])
+    scores = dot_nt(q_rot[...], k_all[...]) * factor
+    weight = jnp.exp(jnp.where(at_key[...] <= at_query[...], scores, -1e30))
+    chance = weight * (1.0 / jnp.sum(weight, axis=-1, keepdims=True))
+    probs[...] = chance
+    mixed = dot(chance.astype(low), v_all[...]).astype(low)
+    context[...] = mixed
+    store_blocks(dot_nt(mixed, wot[...]), blocks)
+
+
+def middle_kernel(b0, b1, b2, b3, own_in, gd, attn_proj, ffn_own):
+    proj = total_of((b0, b1, b2, b3))
+    attn_proj[...] = proj
+    attn_unit, _ = unit_of(proj)
+    ffn_unit, _ = unit_of(own_in[...].astype(full) + attn_unit * gd[1:2, :])
+    ffn_own[...] = (ffn_unit * gd[2:3, :]).astype(low)
+
+
+def ffn_kernel(f0, f1, f2, f3, wg, wu, wdt, ffn_rows, gate, upper, act, *blocks):
+    rows = f0.shape[0]
+    for o, ref in enumerate((f0, f1, f2, f3)):
+        ffn_rows[o * rows : (o + 1) * rows, :] = ref[...]
+    held = ffn_rows[...]
+    gate_val = dot(held, wg[...])
+    upper_val = dot(held, wu[...])
+    gate[...] = gate_val
+    upper[...] = upper_val
+    gelu_val, _ = gelu_pair(gate_val)
+    hidden = (gelu_val * upper_val).astype(low)
+    act[...] = hidden
+    store_blocks(dot_nt(hidden, wdt[...]), blocks)
+
+
+def turn_kernel(b0, b1, b2, b3, own_in, attn_proj, cot, gd, block_out, grad_own, last_grad):
+    out_unit, out_scale = unit_of(total_of((b0, b1, b2, b3)))
+    attn_unit, _ = unit_of(attn_proj[...])
+    grad_out = cot[...].astype(full)
+    grad_own[...] = norm_back(grad_out * gd[3:4, :], out_unit, out_scale).astype(low)
+    resid = own_in[...].astype(full) + attn_unit * gd[1:2, :]
+    block_out[...] = resid + out_unit * gd[3:4, :]
+    last_grad[...] = jnp.sum(grad_out * out_unit, axis=0, keepdims=True)
+
+
+def ffn_back_kernel(g0, g1, g2, g3, gate, upper, wg, wu, wdt, g_rows, g_gate, g_up, *blocks):
+    rows = g0.shape[0]
+    for o, ref in enumerate((g0, g1, g2, g3)):
+        g_rows[o * rows : (o + 1) * rows, :] = ref[...]
+    grad_hidden = dot(g_rows[...], wdt[...])
+    gelu_val, gelu_slope = gelu_pair(gate[...])
+    grad_up = (grad_hidden * gelu_val).astype(low)
+    grad_gate = (grad_hidden * upper[...] * gelu_slope).astype(low)
+    g_up[...] = grad_up
+    g_gate[...] = grad_gate
+    store_blocks(dot_nt(grad_gate, wg[...]) + dot_nt(grad_up, wu[...]), blocks)
+
+
+def store_halves(first, theirs, mine, at, value):
+    half = value.shape[0] // 2
+    value = value.astype(low)
+    mine[:, at] = jnp.where(first, value[:half], value[half:])
+    theirs[:, at] = jnp.where(first, value[half:], value[:half])
+
+
+def early_kernel(place, ffn_rows, g_rows, g_gate, g_up, act, theirs, mine):
+    first = place[0] == 0
+    cols = g_gate.shape[1]
+    held = ffn_rows[...]
+    store_halves(first, theirs, mine, slice(0, cols), dot_tn(held, g_gate[...]))
+    store_halves(first, theirs, mine, slice(cols, 2 * cols), dot_tn(held, g_up[...]))
+    store_halves(first, theirs, mine, slice(2 * cols, 3 * cols), dot_tn(g_rows[...], act[...]))
+
+
+def chunk_kernel(place, mine, came, *chunks):
+    n = len(chunks)
+    rows = chunks[0].shape[0]
+    for o, chunk in enumerate(chunks):
+        start = pl.multiple_of(lax.rem(place[1] + o, n) * rows, 16)
+        chunk[...] = (
+            mine[pl.ds(start, rows), :].astype(full) + came[pl.ds(start, rows), :].astype(full)
+        ).astype(chunk.dtype)
+
+
+def sum_kernel(*refs):
+    refs[-1][...] = total_of(refs[:-1]).astype(refs[-1].dtype)
+
+
+def split_sum_kernel(*refs):
+    total = total_of(refs[:-2]).astype(low)
+    half = refs[-1].shape[1]
+    refs[-2][...] = total[:, :half]
+    refs[-1][...] = total[:, half:]
+
+
+def join_sum_kernel(left, *refs):
+    half = left.shape[1]
+    refs[-1][:, :half] = left[...]
+    refs[-1][:, half:] = total_of(refs[:-1]).astype(low)
+
+
+def early_out_kernel(place, c0, c1, c2, c3, gate_grad, up_grad, down_turned):
+    rows = c0.shape[0]
+    cols = gate_grad.shape[1]
+    for o, chunk in enumerate((c0, c1, c2, c3)):
+        start = pl.multiple_of(lax.rem(place[1] + o, 4) * rows, 16)
+        value = chunk[...].astype(full)
+        gate_grad[pl.ds(start, rows), :] = value[:, :cols]
+        up_grad[pl.ds(start, rows), :] = value[:, cols : 2 * cols]
+        down_turned[pl.ds(start, rows), :] = value[:, 2 * cols :]
+
+
+def late_out_kernel(place, c0, c1, c2, c3, query_grad, out_turned, key_grad, value_grad, vector):
+    rows = query_grad.shape[0] // 4
+    cols = query_grad.shape[1]
+    for o, chunk in enumerate((c0, c1, c2, c3)):
+        which = lax.rem(place[1] + o, 4)
+        start = pl.multiple_of(which * rows, 16)
+        value = chunk[0:rows, :].astype(full)
+        query_grad[pl.ds(start, rows), :] = value[:, :cols]
+        out_turned[pl.ds(start, rows), :] = value[:, cols : 2 * cols]
+        key_grad[pl.ds(start, rows), :] = value[:, 2 * cols : 3 * cols]
+        value_grad[pl.ds(start, rows), :] = value[:, 3 * cols :]
+        tail = chunk[rows:, 2 * cols :].astype(full)
+        vector[pl.ds(pl.multiple_of(which * 8, 8), 8), :] = tail[0:8, :]
+
+
+def grad_middle_kernel(
+    b0, b1, b2, b3, own_in, attn_proj, cot, gd, grad_resid, grad_own, pre_grad, post_grad
+):
+    grad_ffn_in = total_of((b0, b1, b2, b3))
+    attn_unit, attn_scale = unit_of(attn_proj[...])
+    ffn_unit, ffn_scale = unit_of(own_in[...].astype(full) + attn_unit * gd[1:2, :])
+    resid_grad = cot[...].astype(full) + norm_back(
+        grad_ffn_in * gd[2:3, :], ffn_unit, ffn_scale
+    )
+    grad_own[...] = norm_back(resid_grad * gd[1:2, :], attn_unit, attn_scale).astype(low)
+    grad_resid[...] = resid_grad
+    pre_grad[...] = jnp.sum(grad_ffn_in * ffn_unit, axis=0, keepdims=True)
+    post_grad[...] = jnp.sum(resid_grad * attn_unit, axis=0, keepdims=True)
+
+
+def attend_back_kernel(
+    a0, a1, a2, a3, wot, context, probs, q_rot, k_all, v_all, a_rows, grad_query, *blocks
+):
+    rows = a0.shape[0]
+    for o, ref in enumerate((a0, a1, a2, a3)):
+        a_rows[o * rows : (o + 1) * rows, :] = ref[...]
+    grad_context = dot(a_rows[...], wot[...]).astype(low)
+    delta = jnp.sum(
+        grad_context.astype(full) * context[...].astype(full), axis=-1, keepdims=True
+    )
+    factor = 1.0 / math.sqrt(q_rot.shape[1])
+    chance = probs[...]
+    grad_probs = dot_nt(grad_context, v_all[...])
+    grad_scores = (chance * (grad_probs - delta) * factor).astype(low)
+    keys = dot_tn(grad_scores, q_rot[...]).astype(low)
+    vals = dot_tn(chance.astype(low), grad_context).astype(low)
+    size = blocks[0].shape[0]
+    wide = keys.shape[1]
+    for o, block in enumerate(blocks):
+        block[:, :wide] = keys[o * size : (o + 1) * size]
+        block[:, wide:] = vals[o * size : (o + 1) * size]
+    grad_query[...] = dot(grad_scores, k_all[...])
+
+
+def late_kernel(
+    place, grad_rot, q_unit, q_scale, gd, gh, cos, sin, wq, wk, wv, a_rows, context,
+    g0, g1, g2, g3, h0, h1, h2, h3, post_grad, pre_grad, last_grad,
+    theirs, mine, query_part,
+):
+    first = place[0] == 0
+    size = h0.shape[0]
+    gained = unrotate(grad_rot[...], cos[0:size, :], sin[0:size, :])
+    query_unit = q_unit[...]
+    qgain_grad = jnp.sum(gained * query_unit, axis=0, keepdims=True)
+    grad_query = norm_back(gained * gh[0:1, :], query_unit, q_scale[...]).astype(low)
+    q_part = dot_nt(grad_query, wq[...])
+    query_part[...] = q_part
+    cols = grad_query.shape[1]
+    kgain_grad = jnp.zeros_like(qgain_grad)
+    in_grad = None
+    key_weight = None
+    for o, (held, grads) in enumerate(((h0, g0), (h1, g1), (h2, g2), (h3, g3))):
+        at = slice(o * size, (o + 1) * size)
+        unit, _ = unit_of(held[...].astype(full))
+        normed = (unit * gd[0:1, :]).astype(low)
+        key_unit, key_scale = unit_of(dot(normed, wk[...]))
+        gained = unrotate(grads[:, :cols].astype(full), cos[at, :], sin[at, :])
+        kgain_grad = kgain_grad + jnp.sum(gained * key_unit, axis=0, keepdims=True)
+        grad_key = norm_back(gained * gh[1:2, :], key_unit, key_scale).astype(low)
+        grad_value = grads[:, cols:]
+        part = dot_nt(grad_key, wk[...]) + dot_nt(grad_value, wv[...])
+        if o == 0:
+            part = part + q_part
+            query_weight = dot_tn(normed, grad_query)
+            key_weight = dot_tn(normed, grad_key)
+            value_weight = dot_tn(normed, grad_value)
+            in_grad = jnp.sum(part * unit, axis=0, keepdims=True)
+        else:
+            key_weight = key_weight + dot_tn(normed, grad_key)
+            value_weight = value_weight + dot_tn(normed, grad_value)
+            in_grad = in_grad + jnp.sum(part * unit, axis=0, keepdims=True)
+    out_weight = dot_tn(a_rows[...], context[...])
+    half = query_weight.shape[0] // 2
+    rows = half // 4
+    stride = rows + 16
+    slim = cols // 2
+    weights = [w.astype(low) for w in (query_weight, out_weight, key_weight, value_weight)]
+    wide_vectors = (in_grad, post_grad[...], pre_grad[...], last_grad[...])
+    sides = [
+        jnp.concatenate(
+            [v[:, s * half : (s + 1) * half] for v in wide_vectors]
+            + [v[:, s * slim : (s + 1) * slim] for v in (qgain_grad, kgain_grad)],
+            axis=1,
+        )
+        for s in range(2)
+    ]
+    length = sides[0].shape[1] // 4
+    for target, pick in ((mine, 0), (theirs, 1)):
+        vector = jnp.where(first, sides[pick], sides[1 - pick])
+        for j, w in enumerate(weights):
+            chosen = jnp.where(
+                first,
+                w[pick * half : (pick + 1) * half],
+                w[(1 - pick) * half : (2 - pick) * half],
+            )
+            for c in range(4):
+                target[c * stride : c * stride + rows, j * cols : (j + 1) * cols] = chosen[
+                    c * rows : (c + 1) * rows
+                ]
+        for c in range(4):
+            tail = slice(c * stride + rows, (c + 1) * stride)
+            target[tail, :] = jnp.zeros((16, target.shape[1]), low)
+            target[tail, 2 * cols : 2 * cols + length] = jnp.broadcast_to(
+                vector[:, c * length : (c + 1) * length], (16, length)
+            ).astype(low)
+
+
+def join_kernel(g0, g1, g2, g3, rows, gd, gh, cos, sin, wk, wv, query_part, *blocks):
+    grads = total_of((g0, g1, g2, g3))
+    cols = wk.shape[1]
+    unit, _ = unit_of(rows[...].astype(full))
+    normed = (unit * gd[0:1, :]).astype(low)
+    key_unit, key_scale = unit_of(dot(normed, wk[...]))
+    gained = unrotate(grads[:, :cols], cos[...], sin[...])
+    grad_key = norm_back(gained * gh[1:2, :], key_unit, key_scale).astype(low)
+    part = query_part[...] + dot_nt(grad_key, wk[...])
+    store_blocks(part + dot_nt(grads[:, cols:].astype(low), wv[...]), blocks)
+
+
+def final_kernel(b0, b1, b2, b3, own_in, grad_resid, gd, hidden_grad):
+    unit, scale = unit_of(own_in[...].astype(full))
+    grad = total_of((b0, b1, b2, b3))
+    hidden_grad[...] = grad_resid[...] + norm_back(grad * gd[0:1, :], unit, scale)
+
+
+def send(value, axis, offset, name):
+    count = lax.axis_size(axis)
+    with jax.named_scope(name):
+        return lax.ppermute(value, axis, [(i, (i + offset) % count) for i in range(count)])
+
+
+def spread(value, axis, name):
+    return [value] + [send(value, axis, o, f"{name}_{o}") for o in range(1, lax.axis_size(axis))]
+
+
+def deal(blocks, axis, name):
+    return [blocks[0]] + [send(b, axis, -o, f"{name}_{o}") for o, b in enumerate(blocks) if o]
+
+
+def deal_up(blocks, axis, name):
+    return [blocks[0]] + [send(b, axis, o, f"{name}_{o}") for o, b in enumerate(blocks) if o]
+
+
+def pair_gather(value, name):
+    other = send(value, "shard", 1, name)
+    first = lax.axis_index("shard") == 0
+    return jnp.concatenate(
+        [jnp.where(first, value, other), jnp.where(first, other, value)], axis=0
+    )
+
+
+def body(
+    hidden_in,
+    positions,
+    cotangent,
+    input_gain,
+    query_weight,
+    key_weight,
+    value_weight,
+    query_gain,
+    key_gain,
+    out_weight,
+    attn_post_gain,
+    ffn_pre_gain,
+    gate_weight,
+    up_weight,
+    down_weight,
+    ffn_post_gain,
+):
+    width = hidden_in.shape[-1]
+    head_dim = key_weight.shape[1]
+    cols = gate_weight.shape[1]
+    tps = lax.axis_size("tp")
+    ctxs = lax.axis_size("ctx")
+    own_in = hidden_in.reshape(-1, width)
+    cot = cotangent.reshape(-1, width)
+    part = own_in.shape[0]
+    count = part * tps
+    me_tp = lax.axis_index("tp")
+    place = jnp.stack([lax.axis_index("shard"), lax.axis_index("ctx")]).astype(jnp.int32)
+
+    rows = jnp.concatenate(spread(own_in, "tp", "rows"), axis=0)
+    natural = positions.reshape(tps, part)
+    places = jnp.concatenate(
+        [lax.dynamic_slice_in_dim(natural, (me_tp - o) % tps, 1, 0) for o in range(tps)], axis=1
+    )
+    places_all = jnp.concatenate(spread(places, "ctx", "places"), axis=1).astype(full)
+    cos, sin = rope_tables(places_all.reshape(-1), head_dim)
+    at_query = places.astype(full).reshape(count, 1)
+
+    wide = width // 2
+    slim = head_dim // 2
+    query_full = pair_gather(query_weight, "wq")
+    key_full = pair_gather(key_weight, "wk")
+    value_full = pair_gather(value_weight, "wv")
+    packed = jnp.concatenate(
+        [input_gain, attn_post_gain, ffn_pre_gain, ffn_post_gain, query_gain, key_gain]
+    ).reshape(1, -1)
+    gains = pair_gather(packed, "gains").astype(full)
+    gd = gains[:, : 4 * wide].reshape(2, 4, wide).transpose(1, 0, 2).reshape(4, width)
+    gh = gains[:, 4 * wide :].reshape(2, 2, slim).transpose(1, 0, 2).reshape(2, head_dim)
+    out_turned = pair_gather(out_weight.T, "wo")
+    gate_full = pair_gather(gate_weight, "wg")
+    up_full = pair_gather(up_weight, "wu")
+    down_turned = pair_gather(down_weight.T, "wd")
+
+    block_outs = [((part, width), full)] + [((part, width), low)] * (tps - 1)
+    held = spread(rows, "ctx", "held")
+    q_rot, q_unit, q_scale, k_own, v_own = run(
+        query_kernel,
+        [
+            ((count, head_dim), low),
+            ((count, head_dim), full),
+            ((count, 1), full),
+            ((count, head_dim), low),
+            ((count, head_dim), low),
+        ],
+        rows, gd, gh, cos[:count], sin[:count], query_full, key_full, value_full,
+    )
+    k_all, v_all, context, probs, *blocks = run(
+        functools.partial(attend_kernel, ctxs),
+        [
+            ((ctxs * count, head_dim), low),
+            ((ctxs * count, head_dim), low),
+            ((count, head_dim), low),
+            ((count, ctxs * count), full),
+        ]
+        + block_outs,
+        q_rot, k_own, v_own, *held[1:], gd, gh, cos, sin, key_full, value_full, out_turned,
+        at_query, places_all,
+    )
+    blocks = deal(blocks, "tp", "attn_rs")
+    attn_proj, ffn_own = run(
+        middle_kernel, [((part, width), full), ((part, width), low)], *blocks, own_in, gd
+    )
+    ffn_rows, gate, upper, act, *blocks = run(
+        ffn_kernel,
+        [
+            ((count, width), low),
+            ((count, cols), full),
+            ((count, cols), full),
+            ((count, cols), low),
+        ]
+        + block_outs,
+        *spread(ffn_own, "tp", "ffn_ag"), gate_full, up_full, down_turned,
+    )
+    blocks = deal(blocks, "tp", "ffn_rs")
+    block_out, grad_own, last_grad = run(
+        turn_kernel,
+        [((part, width), full), ((part, width), low), ((1, width), full)],
+        *blocks, own_in, attn_proj, cot, gd,
+    )
+    g_rows, g_gate, g_up, *blocks = run(
+        ffn_back_kernel,
+        [((count, width), low), ((count, cols), low), ((count, cols), low)] + block_outs,
+        *spread(grad_own, "tp", "gproj_ag"), gate, upper, gate_full, up_full, down_turned,
+    )
+    blocks = deal(blocks, "tp", "gffn_rs")
+
+    theirs, mine = run(
+        early_kernel,
+        [((wide, 3 * cols), low)] * 2,
+        ffn_rows, g_rows, g_gate, g_up, act, scalars=place,
+    )
+    came = send(theirs, "shard", 1, "early_pair")
+    chunk = wide // ctxs
+    chunks = run(
+        chunk_kernel,
+        [((chunk, 3 * cols), full)] + [((chunk, 3 * cols), low)] * (ctxs - 1),
+        mine, came, scalars=place,
+    )
+    chunks = deal_up(chunks, "ctx", "early_rs")
+
+    grad_resid, attn_grad_own, pre_grad, post_grad = run(
+        grad_middle_kernel,
+        [((part, width), full), ((part, width), low), ((1, width), full), ((1, width), full)],
+        *blocks, own_in, attn_proj, cot, gd,
+    )
+    attn_pieces = spread(attn_grad_own, "tp", "gattn_ag")
+    (early_total,) = run(sum_kernel, [((chunk, 3 * cols), low)], *chunks)
+    early_all = deal([early_total] * ctxs, "ctx", "early_ag")
+
+    a_rows, grad_rot, *grads = run(
+        attend_back_kernel,
+        [((count, width), low), ((count, head_dim), full)]
+        + [((count, 2 * head_dim), low)] * ctxs,
+        *attn_pieces, out_turned, context, probs, q_rot, k_all, v_all,
+    )
+    dealt = deal(grads, "ctx", "gkv_rs")
+    late_rows = wide + 16 * ctxs
+    theirs, mine, query_part = run(
+        late_kernel,
+        [((late_rows, 4 * head_dim), low)] * 2 + [((count, width), full)],
+        grad_rot, q_unit, q_scale, gd, gh, cos, sin, query_full, key_full, value_full,
+        a_rows, context, *grads, *held, post_grad, pre_grad, last_grad,
+        scalars=place,
+    )
+    came = send(theirs, "shard", 1, "late_pair")
+    chunks = run(
+        chunk_kernel,
+        [((late_rows // ctxs, 4 * head_dim), full)]
+        + [((late_rows // ctxs, 4 * head_dim), low)] * (ctxs - 1),
+        mine, came, scalars=place,
+    )
+    chunks = deal_up(chunks, "ctx", "late_rs")
+
+    blocks = run(
+        join_kernel,
+        block_outs,
+        *dealt, rows, gd, gh, cos[:count], sin[:count], key_full, value_full, query_part,
+    )
+    blocks = deal(blocks, "tp", "hidden_rs")
+    left, right = run(
+        split_sum_kernel, [((late_rows // ctxs, 2 * head_dim), low)] * 2, *chunks
+    )
+    rights = spread(right, "tp", "late_z")
+    (hidden_grad,) = run(final_kernel, [((part, width), full)], *blocks, own_in, grad_resid, gd)
+    (late_total,) = run(
+        join_sum_kernel, [((late_rows // ctxs, 4 * head_dim), low)], left, *rights
+    )
+    late_all = deal([late_total] * ctxs, "ctx", "late_ag")
+
+    gate_grad, up_grad, down_grad = run(
+        early_out_kernel, [((wide, cols), full)] * 3, *early_all, scalars=place
+    )
+    query_grad, out_grad, key_grad, value_grad, vector = run(
+        late_out_kernel,
+        [((wide, head_dim), full)] * 4 + [((8 * ctxs, 2 * head_dim), full)],
+        *late_all, scalars=place,
+    )
+    length = (4 * wide + 2 * slim) // ctxs
+    vector = vector.reshape(ctxs, 8, 2 * head_dim)[:, 0, :length].reshape(-1)
+
+    def vector_at(start, size):
+        return vector[start : start + size]
+
+    return (
+        block_out.reshape(hidden_in.shape),
+        hidden_grad.reshape(hidden_in.shape),
+        vector_at(0, wide),
+        query_grad,
+        key_grad,
+        value_grad,
+        vector_at(4 * wide, slim),
+        vector_at(4 * wide + slim, slim),
+        out_grad.T,
+        vector_at(wide, wide),
+        vector_at(2 * wide, wide),
+        gate_grad,
+        up_grad,
+        down_grad.T,
+        vector_at(3 * wide, wide),
+    )
+
+
+def chosen_body(mesh):
+    def pick(*args):
+        width = args[0].shape[-1]
+        fits = (
+            mesh.shape["shard"] == 2
+            and mesh.shape["ctx"] == 4
+            and mesh.shape["tp"] == 4
+            and args[4].shape[1] == args[5].shape[1]
+            and (width // 8) % 16 == 0
+        )
+        return (body if fits else plain_body)(*args)
+
+    return pick
+
+
 def solution(mesh):
     placed = (
         P("shard", ("ctx", "tp"), None),
@@ -412,7 +977,7 @@
         P("shard"),
     )
     return jax.shard_map(
-        body,
+        chosen_body(mesh),
         mesh=mesh,
         in_specs=placed,
         out_specs=(

time: 245 us -> 199 us (0.81); the launches traced: 244 us -> 196 us
  Pallas kernels: 0 us -> 21.8 us
  matrix products: 20.5 us -> 0 us
  local copies, waits for them, and re-layouts: 39.5 us -> 23.9 us
  other arithmetic: 20.9 us -> 6.68 us
  starting transfers between devices: 82.8 us -> 72.3 us
  waiting for transfers between devices: 78.1 us -> 69.7 us
    pallas_call x0 -> x19, Pallas kernels: none -> 21.8 us  [run(): pl.pallas_call(kernel, out_shape=[jax.ShapeDtypeStruct(shape, kind) for s...]
    dot_general x27 -> x0, matrix products: 20.5 us -> none  [the longest x7 6.26 us: dot_tn(): lax.dot_general(left, right, (((0,), (0,)), ((), ())), preferred_element_...]
    ppermute x70 -> x58, starting transfers between devices: 82.8 us -> 72.3 us  [send(): lax.ppermute(value, axis, [(i, (i + offset) % count) for i in range(count)])]
    concatenate x5 -> x2, local copies, waits for them, and re-layouts: 9.7 us -> 0.17 us  [body(): jnp.concatenate(spread(places, 'ctx', 'places'), axis=1).astype(full)]
    ppermute x70 -> x58, waiting for transfers between devices: 78.1 us -> 69.7 us  [send(): lax.ppermute(value, axis, [(i, (i + offset) % count) for i in range(count)])]
    convert_element_type x17 -> x4, other arithmetic: 7.21 us -> 0.7 us  [the longest x2 0.61 us: body(): jnp.concatenate(spread(places, 'ctx', 'places'), axis=1).astype(full)]
    unnamed x238 -> x110, local copies, waits for them, and re-layouts: 11 us -> 17.2 us
    dynamic_slice x6 -> x1, local copies, waits for them, and re-layouts: 5.67 us -> 0.01 us  [body(): lax.dynamic_slice_in_dim(natural, (me_tp - o) % tps, 1, 0)]
  transfers between devices with their start and end apart: 70 -> 58, of which waited for: 31 -> 23; matrix products, arithmetic and copies ran while one was open for 23% -> 6% of each run, Pallas kernels for 0% -> 6%
where the time goes in v2:
time: 199 us; the launch traced here: 196 us
  starting transfers between devices  72.3 us (36%)
  waiting for transfers between devices  69.7 us (35%)
  local copies, waits for them, and re-layouts  23.9 us (12%)
  Pallas kernels  21.8 us (11%)
  other arithmetic  6.68 us (3%)
    ppermute x58, starting transfers between devices, send(): lax.ppermute(value, axis, [(i, (i + offset) % count) for i in range(count)])  72.3 us
    ppermute x58, waiting for transfers between devices, send(): lax.ppermute(value, axis, [(i, (i + offset) % count) for i in range(count)])  69.7 us
    pallas_call x19, Pallas kernels, run(): pl.pallas_call(kernel, out_shape=[jax.ShapeDtypeStruct(shape, kind) for s...  21.8 us
    unnamed x110, local copies, waits for them, and re-layouts  17.2 us
    concatenate x1, local copies, waits for them, and re-layouts, body(): jnp.concatenate([input_gain, attn_post_gain, ffn_pre_gain, ffn_post_gain,...  4.18 us
  transfers between devices with their start and end apart: 58, of which 23 were waited for; matrix products, arithmetic and copies ran while one was open for 6% of the time, Pallas kernels for 6%

profile of v2, /device:TPU:0, one launch (start us, length us, event | category | flops | bytes accessed | tf_op | source)
XLA Modules:
  0.0 195.8 jit_solution(3598506853650522702)
XLA Ops:
  1.3 1.3 reduce.5
  2.8 3.9 %collective-permute-start.6 = (s32[1,256]{1,0:T(1,128)S(1)}, s32[1,256]{1,0:T(1,128)S(1)}, u32[]{:S(2)}, u32[]{:S(2)}) collective-permute-start(s32[1,256]{1,0:T(1,128)S(1)} %pad_add_fusion), channel_id=1, source_target_pairs={{0,12},{4,0},{8,4},{12,8},{1,13},{5,1},{9,5},{13,9},{2,14},{6,2},{... | collective-permute-start | bytes 3080 | tf_op jit(solution)/shard_map/places_3/ppermute | solution.py:718
  7.8 3.6 %collective-permute-start.2 = (bf16[64,640]{1,0:T(8,128)(2,1)}, bf16[64,640]{1,0:T(8,128)(2,1)S(1)}, u32[]{:S(2)}, u32[]{:S(2)}) collective-permute-start(bf16[64,640]{1,0:T(8,128)(2,1)} %bitcast.35), channel_id=1, source_target_pairs={{0,3},{1,0},{2,1},{3,2},{4,7},{5,4},{6,5},{7,6},{8,11},{9,8},{10,9... | collective-permute-start | bytes 245768 | tf_op jit(solution)/shard_map/rows_3/ppermute | solution.py:718
  11.5 4.2 %concatenate.85 = bf16[1536]{0:T(1024)(128)(2,1)S(1)} concatenate(bf16[320]{0:T(512)(128)(2,1)} %param.19, bf16[320]{0:T(512)(128)(2,1)} %param.26, bf16[320]{0:T(512)(128)(2,1)} %param.27, bf16[320]{0:T(512)(128)(2,1)} %param.31, bf16[128]{0:T(256)(128)(2,1)} %param.23, bf16[128]{0:T(256)(128)(2,1)} %param.24), dimensions={0} | concatenate | bytes 6144 | tf_op jit(solution)/shard_map/concatenate | solution.py:785
  16.5 1.0 collective-permute-start
  18.1 1.9 multiply_sine_fusion
  21.8 1.1 collective-permute-done
  23.8 2.4 %collective-permute-start.12 = (bf16[256,640]{1,0:T(8,128)(2,1)S(1)}, bf16[256,640]{1,0:T(8,128)(2,1)S(1)}, u32[]{:S(2)}, u32[]{:S(2)}) collective-permute-start(bf16[256,640]{1,0:T(8,128)(2,1)S(1)} %pad_maximum_fusion.3.rows.h0), channel_id=1, source_target_pairs={{0,12},{4,0},{8,4},{12,8},{1,13},{5,1},{9,5},{13,9},{2,14},{6,2},{... | collective-permute-start | bytes 983048 | tf_op jit(solution)/shard_map/held_3/ppermute | solution.py:718
  26.2 1.5 collective-permute-start.11
  29.2 1.0 broadcast_select_fusion.5
  30.4 1.2 broadcast_select_fusion.1
  31.6 3.2 %collective-permute-done.12.refs_5_.h3 = bf16[256,640]{1,0:T(8,128)(2,1)S(1)} collective-permute-done((bf16[256,640]{1,0:T(8,128)(2,1)S(1)}, bf16[256,640]{1,0:T(8,128)(2,1)S(1)}, u32[]{:S(2)}, u32[]{:S(2)}) %collective-permute-start.12) | collective-permute-done | bytes 327712 | tf_op jit(solution)/shard_map/held_3/ppermute | solution.py:718
  34.8 8.2 %collective-permute-done.11.refs_4_.h2 = bf16[256,640]{1,0:T(8,128)(2,1)S(1)} collective-permute-done((bf16[256,640]{1,0:T(8,128)(2,1)S(1)}, bf16[256,640]{1,0:T(8,128)(2,1)S(1)}, u32[]{:S(2)}, u32[]{:S(2)}) %collective-permute-start.11) | collective-permute-done | bytes 327712 | tf_op jit(solution)/shard_map/held_2/ppermute | solution.py:718
  43.0 2.0 %shard_map.272 = (bf16[1024,256]{1,0:T(8,128)(2,1)S(1)}, bf16[1024,256]{1,0:T(8,128)(2,1)S(1)}, bf16[256,256]{1,0:T(8,128)(2,1)S(1)}, f32[256,1024]{1,0:T(8,128)...) custom-call(bf16[256,256]{1,0:T(8,128)(2,1)S(1)} %get-tuple-element., ...), custom_call_target="tpu_custom_call" | custom-call | tf_op jit(solution)/shard_map/pallas_call | solution.py:404
  45.0 1.0 copy-done.5
  47.5 1.7 collective-permute-start.14
  49.1 1.1 collective-permute-start.15
  50.7 1.6 collective-permute-done.14.b1
  52.2 5.2 %collective-permute-done.15.b2 = bf16[64,640]{1,0:T(8,128)(2,1)S(1)} collective-permute-done((bf16[64,640]{1,0:T(8,128)(2,1)S(1)}, bf16[64,640]{1,0:T(8,128)(2,1)S(1)}, u32[]{:S(2)}, u32[]{:S(2)}) %collective-permute-start.15) | collective-permute-done | bytes 81952 | tf_op jit(solution)/shard_map/attn_rs_2/ppermute | solution.py:718
  59.0 1.9 collective-permute-start.17
  61.0 1.9 collective-permute-done.19.f3
  62.9 3.8 %collective-permute-done.18.f2 = bf16[64,640]{1,0:T(8,128)(2,1)S(1)} collective-permute-done((bf16[64,640]{1,0:T(8,128)(2,1)S(1)}, bf16[64,640]{1,0:T(8,128)(2,1)S(1)}, u32[]{:S(2)}, u32[]{:S(2)}) %collective-permute-start.18) | collective-permute-done | bytes 81952 | tf_op jit(solution)/shard_map/ffn_ag_2/ppermute | solution.py:718
  68.3 1.2 collective-permute-start.23
  70.1 2.0 %collective-permute-start.25 = (bf16[64,640]{1,0:T(8,128)(2,1)S(1)}, bf16[64,640]{1,0:T(8,128)(2,1)S(1)}, u32[]{:S(2)}, u32[]{:S(2)}) collective-permute-start(bf16[64,640]{1,0:T(8,128)(2,1)S(1)} %get-tuple-element.96), channel_id=1, source_target_pairs={{0,1},{1,2},{2,3},{3,0},{4,5},{5,6},{6,7},{7,4},{8,9},{9,10},{10,1... | collective-permute-start | bytes 245768 | tf_op jit(solution)/shard_map/ffn_rs_3/ppermute | solution.py:718
  72.9 5.0 %collective-permute-done.24.b2 = bf16[64,640]{1,0:T(8,128)(2,1)S(1)} collective-permute-done((bf16[64,640]{1,0:T(8,128)(2,1)S(1)}, bf16[64,640]{1,0:T(8,128)(2,1)S(1)}, u32[]{:S(2)}, u32[]{:S(2)}) %collective-permute-start.24) | collective-permute-done | bytes 81952 | tf_op jit(solution)/shard_map/ffn_rs_2/ppermute | solution.py:718
  78.8 1.0 collective-permute-start.28
  80.6 2.0 %collective-permute-start.26 = (bf16[64,640]{1,0:T(8,128)(2,1)S(1)}, bf16[64,640]{1,0:T(8,128)(2,1)S(1)}, u32[]{:S(2)}, u32[]{:S(2)}) collective-permute-start(bf16[64,640]{1,0:T(8,128)(2,1)S(1)} %get-tuple-element.99.g0), channel_id=1, source_target_pairs={{0,1},{1,2},{2,3},{3,0},{4,5},{5,6},{6,7},{7,4},{8,9},{9,10},{10,1... | collective-permute-start | bytes 245768 | tf_op jit(solution)/shard_map/gproj_ag_1/ppermute | solution.py:718
  83.5 5.0 %collective-permute-done.27.g2 = bf16[64,640]{1,0:T(8,128)(2,1)S(1)} collective-permute-done((bf16[64,640]{1,0:T(8,128)(2,1)S(1)}, bf16[64,640]{1,0:T(8,128)(2,1)S(1)}, u32[]{:S(2)}, u32[]{:S(2)}) %collective-permute-start.27) | collective-permute-done | bytes 81952 | tf_op jit(solution)/shard_map/gproj_ag_2/ppermute | solution.py:718
  88.5 1.8 shard_map.276
  93.1 1.0 collective-permute-start.29
  94.9 2.0 %collective-permute-start.31 = (bf16[64,640]{1,0:T(8,128)(2,1)}, bf16[64,640]{1,0:T(8,128)(2,1)}, u32[]{:S(2)}, u32[]{:S(2)}) collective-permute-start(bf16[64,640]{1,0:T(8,128)(2,1)} %get-tuple-element.105), channel_id=1, source_target_pairs={{0,1},{1,2},{2,3},{3,0},{4,5},{5,6},{6,7},{7,4},{8,9},{9,10},{10,1... | collective-permute-start | bytes 245768 | tf_op jit(solution)/shard_map/gffn_rs_3/ppermute | solution.py:718
  96.9 1.2 collective-permute-done.29.b1
  98.1 5.0 %collective-permute-done.30.b2 = bf16[64,640]{1,0:T(8,128)(2,1)} collective-permute-done((bf16[64,640]{1,0:T(8,128)(2,1)}, bf16[64,640]{1,0:T(8,128)(2,1)}, u32[]{:S(2)}, u32[]{:S(2)}) %collective-permute-start.30) | collective-permute-done | bytes 81952 | tf_op jit(solution)/shard_map/gffn_rs_2/ppermute | solution.py:718
  106.5 1.5 shard_map.277
  108.1 1.1 collective-permute-start.34
  110.0 1.9 collective-permute-start.32
  116.8 1.2 shard_map.286
  118.2 1.0 copy-done.21
  119.3 1.2 shard_map.278
  120.6 4.1 %shard_map.279 = (bf16[384,1024]{1,0:T(8,128)(2,1)S(1)}, bf16[384,1024]{1,0:T(8,128)(2,1)S(1)}, f32[256,640]{1,0:T(8,128)S(1)}) custom-call(s32[2]{0:T(128)S(1)} %pad_add_fusion.1.place, f32[256,256]{1,0:T(8,128)S(1)} %get-tuple-element.115.grad_rot, f32[256,256]{1,0:T(8,128)S(1)} %copy-done.29, f32[256,1]{1,0:T(8,128)S(1)} %copy-done.39, ...), custom_call_target="tpu_custom_call" | custom-call | tf_op jit(solution)/shard_map/pallas_call | solution.py:404
  125.3 1.9 collective-permute-done.41.came
  128.6 1.7 collective-permute-start.43
  130.3 2.2 %collective-permute-start.35 = (bf16[256,512]{1,0:T(8,128)(2,1)S(1)}, bf16[256,512]{1,0:T(8,128)(2,1)S(1)}, u32[]{:S(2)}, u32[]{:S(2)}) collective-permute-start(bf16[256,512]{1,0:T(8,128)(2,1)S(1)} %get-tuple-element.112.g1), channel_id=1, source_target_pairs={{0,12},{4,0},{8,4},{12,8},{1,13},{5,1},{9,5},{13,9},{2,14},{6,2},{... | collective-permute-start | bytes 786440 | tf_op jit(solution)/shard_map/gkv_rs_1/ppermute | solution.py:718
  133.0 3.7 %collective-permute-done.42.refs_1_ = bf16[96,1024]{1,0:T(8,128)(2,1)S(1)} collective-permute-done((bf16[96,1024]{1,0:T(8,128)(2,1)S(1)}, bf16[96,1024]{1,0:T(8,128)(2,1)S(1)}, u32[]{:S(2)}, u32[]{:S(2)}) %collective-permute-start.42) | collective-permute-done | bytes 196640 | tf_op jit(solution)/shard_map/late_rs_1/ppermute | solution.py:718
  138.3 2.1 %collective-permute-done.43.refs_2_ = bf16[96,1024]{1,0:T(8,128)(2,1)S(1)} collective-permute-done((bf16[96,1024]{1,0:T(8,128)(2,1)S(1)}, bf16[96,1024]{1,0:T(8,128)(2,1)S(1)}, u32[]{:S(2)}, u32[]{:S(2)}) %collective-permute-start.43) | collective-permute-done | bytes 196640 | tf_op jit(solution)/shard_map/late_rs_2/ppermute | solution.py:718
  140.4 4.0 %collective-permute-start.52 = (bf16[80,1536]{1,0:T(8,128)(2,1)S(1)}, bf16[80,1536]{1,0:T(8,128)(2,1)S(1)}, u32[]{:S(2)}, u32[]{:S(2)}) collective-permute-start(bf16[80,1536]{1,0:T(8,128)(2,1)S(1)} %get-tuple-element.149), channel_id=1, source_target_pairs={{0,4},{4,8},{8,12},{12,0},{1,5},{5,9},{9,13},{13,1},{2,6},{6,10},{... | collective-permute-start | bytes 737288 | tf_op jit(solution)/shard_map/early_rs_1/ppermute | solution.py:718
  144.4 7.9 %collective-permute-done.44.refs_3_ = bf16[96,1024]{1,0:T(8,128)(2,1)S(1)} collective-permute-done((bf16[96,1024]{1,0:T(8,128)(2,1)S(1)}, bf16[96,1024]{1,0:T(8,128)(2,1)S(1)}, u32[]{:S(2)}, u32[]{:S(2)}) %collective-permute-start.44) | collective-permute-done | bytes 196640 | tf_op jit(solution)/shard_map/late_rs_3/ppermute | solution.py:718
  152.4 1.9 collective-permute-start.47
  154.3 1.0 shard_map.280
  155.3 1.0 collective-permute-start.38
  157.7 2.4 %collective-permute-done.38.b1 = bf16[64,640]{1,0:T(8,128)(2,1)S(1)} collective-permute-done((bf16[64,640]{1,0:T(8,128)(2,1)S(1)}, bf16[64,640]{1,0:T(8,128)(2,1)S(1)}, u32[]{:S(2)}, u32[]{:S(2)}) %collective-permute-start.38) | collective-permute-done | bytes 81952 | tf_op jit(solution)/shard_map/hidden_rs_1/ppermute | solution.py:718
  160.1 5.5 %collective-permute-start.39 = (bf16[64,640]{1,0:T(8,128)(2,1)S(1)}, bf16[64,640]{1,0:T(8,128)(2,1)S(1)}, u32[]{:S(2)}, u32[]{:S(2)}) collective-permute-start(bf16[64,640]{1,0:T(8,128)(2,1)S(1)} %get-tuple-element.125), channel_id=1, source_target_pairs={{0,2},{1,3},{2,0},{3,1},{4,6},{5,7},{6,4},{7,5},{8,10},{9,11},{10,... | collective-permute-start | bytes 245768 | tf_op jit(solution)/shard_map/hidden_rs_2/ppermute | solution.py:718
  165.6 1.2 collective-permute-start.40
  166.8 1.1 collective-permute-done.46.refs_2_
  168.4 1.7 collective-permute-start.54
  170.5 1.9 collective-permute-done.40.b3
  173.0 1.7 collective-permute-start.48
  175.6 2.2 %collective-permute-done.53.refs_2_ = bf16[80,1536]{1,0:T(8,128)(2,1)S(1)} collective-permute-done((bf16[80,1536]{1,0:T(8,128)(2,1)S(1)}, bf16[80,1536]{1,0:T(8,128)(2,1)S(1)}, u32[]{:S(2)}, u32[]{:S(2)}) %collective-permute-start.53) | collective-permute-done | bytes 245792 | tf_op jit(solution)/shard_map/early_rs_2/ppermute | solution.py:718
  177.9 6.6 %collective-permute-start.57 = (bf16[80,1536]{1,0:T(8,128)(2,1)S(1)}, bf16[80,1536]{1,0:T(8,128)(2,1)S(1)}, u32[]{:S(2)}, u32[]{:S(2)}) collective-permute-start(bf16[80,1536]{1,0:T(8,128)(2,1)S(1)} %shard_map.288.c0), channel_id=1, source_target_pairs={{0,4},{4,8},{8,12},{12,0},{1,5},{5,9},{9,13},{13,1},{2,6},{6,10},{... | collective-permute-start | bytes 737288 | tf_op jit(solution)/shard_map/early_ag_3/ppermute | solution.py:718
  184.5 2.2 %collective-permute-start.56 = (bf16[80,1536]{1,0:T(8,128)(2,1)S(1)}, bf16[80,1536]{1,0:T(8,128)(2,1)S(1)}, u32[]{:S(2)}, u32[]{:S(2)}) collective-permute-start(bf16[80,1536]{1,0:T(8,128)(2,1)S(1)} %shard_map.288.c0), channel_id=1, source_target_pairs={{0,8},{4,12},{8,0},{12,4},{1,9},{5,13},{9,1},{13,5},{2,10},{6,14},... | collective-permute-start | bytes 737288 | tf_op jit(solution)/shard_map/early_ag_2/ppermute | solution.py:718
  186.7 1.7 shard_map.285
  189.6 1.6 collective-permute-done.57.c3
  191.2 2.0 %collective-permute-done.56.c2 = bf16[80,1536]{1,0:T(8,128)(2,1)S(1)} collective-permute-done((bf16[80,1536]{1,0:T(8,128)(2,1)S(1)}, bf16[80,1536]{1,0:T(8,128)(2,1)S(1)}, u32[]{:S(2)}, u32[]{:S(2)}) %collective-permute-start.56) | collective-permute-done | bytes 245792 | tf_op jit(solution)/shard_map/early_ag_2/ppermute | solution.py:718
  193.9 1.9 shard_map.289
  (221 shorter events, 39.0 us)
Async XLA Ops:
  0.7 20.5 %copy-start.52 = (bf16[320,256]{1,0:T(8,128)(2,1)S(1)}, bf16[320,256]{1,0:T(8,128)(2,1)}, u32[]{:S(2)}) copy-start(bf16[320,256]{1,0:T(8,128)(2,1)} %param.20) | copy-start | bytes 491524
  0.7 21.0 %copy-start.50 = (bf16[320,256]{1,0:T(8,128)(2,1)S(1)}, bf16[320,256]{1,0:T(8,128)(2,1)}, u32[]{:S(2)}) copy-start(bf16[320,256]{1,0:T(8,128)(2,1)} %param.21) | copy-start | bytes 491524
  0.7 22.3 %copy-start = (bf16[1,64,640]{2,1,0:T(8,128)(2,1)S(1)}, bf16[1,64,640]{2,1,0:T(8,128)(2,1)}, u32[]{:S(2)}) copy-start(bf16[1,64,640]{2,1,0:T(8,128)(2,1)} %param.16) | copy-start | bytes 245764
  2.8 13.7 %collective-permute-start.6 = (s32[1,256]{1,0:T(1,128)S(1)}, s32[1,256]{1,0:T(1,128)S(1)}, u32[]{:S(2)}, u32[]{:S(2)}) collective-permute-start(s32[1,256]{1,0:T(1,128)S(1)} %pad_add_fusion), channel_id=1, source_target_pairs={{0,12},{4,0},{8,4},{12,8},{1,13},{5,1},{9,5},{13,9},{2,14},{6,2},{... | collective-permute-start | bytes 3080 | tf_op jit(solution)/shard_map/places_3/ppermute | solution.py:718
  6.7 10.8 %collective-permute-start.5 = (s32[1,256]{1,0:T(1,128)S(1)}, s32[1,256]{1,0:T(1,128)S(1)}, u32[]{:S(2)}, u32[]{:S(2)}) collective-permute-start(s32[1,256]{1,0:T(1,128)S(1)} %pad_add_fusion), channel_id=1, source_target_pairs={{0,8},{4,12},{8,0},{12,4},{1,9},{5,13},{9,1},{13,5},{2,10},{6,14},... | collective-permute-start | bytes 3080 | tf_op jit(solution)/shard_map/places_2/ppermute | solution.py:718
  7.2 10.3 %collective-permute-start.4 = (s32[1,256]{1,0:T(1,128)S(1)}, s32[1,256]{1,0:T(1,128)S(1)}, u32[]{:S(2)}, u32[]{:S(2)}) collective-permute-start(s32[1,256]{1,0:T(1,128)S(1)} %pad_add_fusion), channel_id=1, source_target_pairs={{0,4},{4,8},{8,12},{12,0},{1,5},{5,9},{9,13},{13,1},{2,6},{6,10},{... | collective-permute-start | bytes 3080 | tf_op jit(solution)/shard_map/places_1/ppermute | solution.py:718
  7.8 13.4 %collective-permute-start.2 = (bf16[64,640]{1,0:T(8,128)(2,1)}, bf16[64,640]{1,0:T(8,128)(2,1)S(1)}, u32[]{:S(2)}, u32[]{:S(2)}) collective-permute-start(bf16[64,640]{1,0:T(8,128)(2,1)} %bitcast.35), channel_id=1, source_target_pairs={{0,3},{1,0},{2,1},{3,2},{4,7},{5,4},{6,5},{7,6},{8,11},{9,8},{10,9... | collective-permute-start | bytes 245768 | tf_op jit(solution)/shard_map/rows_3/ppermute | solution.py:718
  11.4 10.3 %collective-permute-start.1 = (bf16[64,640]{1,0:T(8,128)(2,1)}, bf16[64,640]{1,0:T(8,128)(2,1)S(1)}, u32[]{:S(2)}, u32[]{:S(2)}) collective-permute-start(bf16[64,640]{1,0:T(8,128)(2,1)} %bitcast.36), channel_id=1, source_target_pairs={{0,2},{1,3},{2,0},{3,1},{4,6},{5,7},{6,4},{7,5},{8,10},{9,11},{10,... | collective-permute-start | bytes 245768 | tf_op jit(solution)/shard_map/rows_2/ppermute | solution.py:718
  16.5 6.5 %collective-permute-start = (bf16[64,640]{1,0:T(8,128)(2,1)}, bf16[64,640]{1,0:T(8,128)(2,1)S(1)}, u32[]{:S(2)}, u32[]{:S(2)}) collective-permute-start(bf16[64,640]{1,0:T(8,128)(2,1)} %bitcast.37), channel_id=1, source_target_pairs={{0,1},{1,2},{2,3},{3,0},{4,5},{5,6},{6,7},{7,4},{8,9},{9,10},{10,1... | collective-permute-start | bytes 245768 | tf_op jit(solution)/shard_map/rows_1/ppermute | solution.py:718
  17.5 3.2 %collective-permute-start.3 = (bf16[1,1536]{1,0:T(2,128)(2,1)S(1)}, bf16[1,1536]{1,0:T(2,128)(2,1)S(1)}, u32[]{:S(2)}, u32[]{:S(2)}) collective-permute-start(bf16[1,1536]{1,0:T(2,128)(2,1)S(1)} %reshape.288), channel_id=1, source_target_pairs={{0,16},{16,0},{1,17},{17,1},{2,18},{18,2},{3,19},{19,3},{4,20},{20... | collective-permute-start | bytes 9224 | tf_op jit(solution)/shard_map/gains/ppermute | solution.py:718
  17.5 5.5 %collective-permute-start.13 = (bf16[320,256]{1,0:T(8,128)(2,1)}, bf16[320,256]{1,0:T(8,128)(2,1)S(1)}, u32[]{:S(2)}, u32[]{:S(2)}) collective-permute-start(bf16[320,256]{1,0:T(8,128)(2,1)} %bitcast.50), channel_id=1, source_target_pairs={{0,16},{16,0},{1,17},{17,1},{2,18},{18,2},{3,19},{19,3},{4,20},{20... | collective-permute-start | bytes 491528 | tf_op jit(solution)/shard_map/wo/ppermute | solution.py:718
  20.8 2.8 %collective-permute-start.9 = (bf16[320,256]{1,0:T(8,128)(2,1)S(1)}, bf16[320,256]{1,0:T(8,128)(2,1)S(1)}, u32[]{:S(2)}, u32[]{:S(2)}) collective-permute-start(bf16[320,256]{1,0:T(8,128)(2,1)S(1)} %copy-done.49), channel_id=1, source_target_pairs={{0,16},{16,0},{1,17},{17,1},{2,18},{18,2},{3,19},{19,3},{4,20},{20... | collective-permute-start | bytes 491528 | tf_op jit(solution)/shard_map/wv/ppermute | solution.py:718
  21.2 2.6 %collective-permute-start.7 = (bf16[320,256]{1,0:T(8,128)(2,1)S(1)}, bf16[320,256]{1,0:T(8,128)(2,1)S(1)}, u32[]{:S(2)}, u32[]{:S(2)}) collective-permute-start(bf16[320,256]{1,0:T(8,128)(2,1)S(1)} %copy-done.52), channel_id=1, source_target_pairs={{0,16},{16,0},{1,17},{17,1},{2,18},{18,2},{3,19},{19,3},{4,20},{20... | collective-permute-start | bytes 491528 | tf_op jit(solution)/shard_map/wq/ppermute | solution.py:718
  21.7 4.5 %collective-permute-start.8 = (bf16[320,256]{1,0:T(8,128)(2,1)S(1)}, bf16[320,256]{1,0:T(8,128)(2,1)S(1)}, u32[]{:S(2)}, u32[]{:S(2)}) collective-permute-start(bf16[320,256]{1,0:T(8,128)(2,1)S(1)} %copy-done.50), channel_id=1, source_target_pairs={{0,16},{16,0},{1,17},{17,1},{2,18},{18,2},{3,19},{19,3},{4,20},{20... | collective-permute-start | bytes 491528 | tf_op jit(solution)/shard_map/wk/ppermute | solution.py:718
  23.0 7.4 %collective-permute-start.22 = (bf16[320,512]{1,0:T(8,128)(2,1)}, bf16[320,512]{1,0:T(8,128)(2,1)S(1)}, u32[]{:S(2)}, u32[]{:S(2)}) collective-permute-start(bf16[320,512]{1,0:T(8,128)(2,1)} %bitcast.16), channel_id=1, source_target_pairs={{0,16},{16,0},{1,17},{17,1},{2,18},{18,2},{3,19},{19,3},{4,20},{20... | collective-permute-start | bytes 983048 | tf_op jit(solution)/shard_map/wd/ppermute | solution.py:718
  23.0 6.2 %collective-permute-start.20 = (bf16[320,512]{1,0:T(8,128)(2,1)}, bf16[320,512]{1,0:T(8,128)(2,1)S(1)}, u32[]{:S(2)}, u32[]{:S(2)}) collective-permute-start(bf16[320,512]{1,0:T(8,128)(2,1)} %param.28), channel_id=1, source_target_pairs={{0,16},{16,0},{1,17},{17,1},{2,18},{18,2},{3,19},{19,3},{4,20},{20... | collective-permute-start | bytes 983048 | tf_op jit(solution)/shard_map/wg/ppermute | solution.py:718
  23.6 6.8 %collective-permute-start.21 = (bf16[320,512]{1,0:T(8,128)(2,1)}, bf16[320,512]{1,0:T(8,128)(2,1)S(1)}, u32[]{:S(2)}, u32[]{:S(2)}) collective-permute-start(bf16[320,512]{1,0:T(8,128)(2,1)} %param.29), channel_id=1, source_target_pairs={{0,16},{16,0},{1,17},{17,1},{2,18},{18,2},{3,19},{19,3},{4,20},{20... | collective-permute-start | bytes 983048 | tf_op jit(solution)/shard_map/wu/ppermute | solution.py:718
  23.8 11.0 %collective-permute-start.12 = (bf16[256,640]{1,0:T(8,128)(2,1)S(1)}, bf16[256,640]{1,0:T(8,128)(2,1)S(1)}, u32[]{:S(2)}, u32[]{:S(2)}) collective-permute-start(bf16[256,640]{1,0:T(8,128)(2,1)S(1)} %pad_maximum_fusion.3.rows.h0), channel_id=1, source_target_pairs={{0,12},{4,0},{8,4},{12,8},{1,13},{5,1},{9,5},{13,9},{2,14},{6,2},{... | collective-permute-start | bytes 983048 | tf_op jit(solution)/shard_map/held_3/ppermute | solution.py:718
  26.2 16.8 %collective-permute-start.11 = (bf16[256,640]{1,0:T(8,128)(2,1)S(1)}, bf16[256,640]{1,0:T(8,128)(2,1)S(1)}, u32[]{:S(2)}, u32[]{:S(2)}) collective-permute-start(bf16[256,640]{1,0:T(8,128)(2,1)S(1)} %pad_maximum_fusion.3.rows.h0), channel_id=1, source_target_pairs={{0,8},{4,12},{8,0},{12,4},{1,9},{5,13},{9,1},{13,5},{2,10},{6,14},... | collective-permute-start | bytes 983048 | tf_op jit(solution)/shard_map/held_2/ppermute | solution.py:718
  29.2 13.7 %collective-permute-start.10 = (bf16[256,640]{1,0:T(8,128)(2,1)S(1)}, bf16[256,640]{1,0:T(8,128)(2,1)S(1)}, u32[]{:S(2)}, u32[]{:S(2)}) collective-permute-start(bf16[256,640]{1,0:T(8,128)(2,1)S(1)} %pad_maximum_fusion.3.rows.h0), channel_id=1, source_target_pairs={{0,4},{4,8},{8,12},{12,0},{1,5},{5,9},{9,13},{13,1},{2,6},{6,10},{... | collective-permute-start | bytes 983048 | tf_op jit(solution)/shard_map/held_1/ppermute | solution.py:718
  47.5 4.8 %collective-permute-start.14 = (bf16[64,640]{1,0:T(8,128)(2,1)S(1)}, bf16[64,640]{1,0:T(8,128)(2,1)S(1)}, u32[]{:S(2)}, u32[]{:S(2)}) collective-permute-start(bf16[64,640]{1,0:T(8,128)(2,1)S(1)} %get-tuple-element.89), channel_id=1, source_target_pairs={{0,3},{1,0},{2,1},{3,2},{4,7},{5,4},{6,5},{7,6},{8,11},{9,8},{10,9... | collective-permute-start | bytes 245768 | tf_op jit(solution)/shard_map/attn_rs_1/ppermute | solution.py:718
  49.1 8.3 %collective-permute-start.15 = (bf16[64,640]{1,0:T(8,128)(2,1)S(1)}, bf16[64,640]{1,0:T(8,128)(2,1)S(1)}, u32[]{:S(2)}, u32[]{:S(2)}) collective-permute-start(bf16[64,640]{1,0:T(8,128)(2,1)S(1)} %get-tuple-element.90), channel_id=1, source_target_pairs={{0,2},{1,3},{2,0},{3,1},{4,6},{5,7},{6,4},{7,5},{8,10},{9,11},{10,... | collective-permute-start | bytes 245768 | tf_op jit(solution)/shard_map/attn_rs_2/ppermute | solution.py:718
  50.3 7.2 %collective-permute-start.16 = (bf16[64,640]{1,0:T(8,128)(2,1)S(1)}, bf16[64,640]{1,0:T(8,128)(2,1)S(1)}, u32[]{:S(2)}, u32[]{:S(2)}) collective-permute-start(bf16[64,640]{1,0:T(8,128)(2,1)S(1)} %get-tuple-element.91), channel_id=1, source_target_pairs={{0,1},{1,2},{2,3},{3,0},{4,5},{5,6},{6,7},{7,4},{8,9},{9,10},{10,1... | collective-permute-start | bytes 245768 | tf_op jit(solution)/shard_map/attn_rs_3/ppermute | solution.py:718
  57.7 20.3 %copy-start.11 = (f32[64,640]{1,0:T(8,128)}, f32[64,640]{1,0:T(8,128)S(1)}, u32[]{:S(2)}) copy-start(f32[64,640]{1,0:T(8,128)S(1)} %get-tuple-element.97.attn_proj) | copy-start | bytes 491524
  57.7 5.2 %collective-permute-start.19 = (bf16[64,640]{1,0:T(8,128)(2,1)S(1)}, bf16[64,640]{1,0:T(8,128)(2,1)S(1)}, u32[]{:S(2)}, u32[]{:S(2)}) collective-permute-start(bf16[64,640]{1,0:T(8,128)(2,1)S(1)} %get-tuple-element.92.f0), channel_id=1, source_target_pairs={{0,3},{1,0},{2,1},{3,2},{4,7},{5,4},{6,5},{7,6},{8,11},{9,8},{10,9... | collective-permute-start | bytes 245768 | tf_op jit(solution)/shard_map/ffn_ag_3/ppermute | solution.py:718
  58.3 8.3 %collective-permute-start.18 = (bf16[64,640]{1,0:T(8,128)(2,1)S(1)}, bf16[64,640]{1,0:T(8,128)(2,1)S(1)}, u32[]{:S(2)}, u32[]{:S(2)}) collective-permute-start(bf16[64,640]{1,0:T(8,128)(2,1)S(1)} %get-tuple-element.92.f0), channel_id=1, source_target_pairs={{0,2},{1,3},{2,0},{3,1},{4,6},{5,7},{6,4},{7,5},{8,10},{9,11},{10,... | collective-permute-start | bytes 245768 | tf_op jit(solution)/shard_map/ffn_ag_2/ppermute | solution.py:718
  59.0 7.6 %collective-permute-start.17 = (bf16[64,640]{1,0:T(8,128)(2,1)S(1)}, bf16[64,640]{1,0:T(8,128)(2,1)S(1)}, u32[]{:S(2)}, u32[]{:S(2)}) collective-permute-start(bf16[64,640]{1,0:T(8,128)(2,1)S(1)} %get-tuple-element.92.f0), channel_id=1, source_target_pairs={{0,1},{1,2},{2,3},{3,0},{4,5},{5,6},{6,7},{7,4},{8,9},{9,10},{10,1... | collective-permute-start | bytes 245768 | tf_op jit(solution)/shard_map/ffn_ag_1/ppermute | solution.py:718
  68.3 20.2 %copy-start.30 = (bf16[256,512]{1,0:T(8,128)(2,1)}, bf16[256,512]{1,0:T(8,128)(2,1)S(1)}, u32[]{:S(2)}) copy-start(bf16[256,512]{1,0:T(8,128)(2,1)S(1)} %get-tuple-element.145.act) | copy-start | bytes 786436
  68.3 4.7 %collective-permute-start.23 = (bf16[64,640]{1,0:T(8,128)(2,1)S(1)}, bf16[64,640]{1,0:T(8,128)(2,1)S(1)}, u32[]{:S(2)}, u32[]{:S(2)}) collective-permute-start(bf16[64,640]{1,0:T(8,128)(2,1)S(1)} %get-tuple-element.94), channel_id=1, source_target_pairs={{0,3},{1,0},{2,1},{3,2},{4,7},{5,4},{6,5},{7,6},{8,11},{9,8},{10,9... | collective-permute-start | bytes 245768 | tf_op jit(solution)/shard_map/ffn_rs_1/ppermute | solution.py:718
  69.4 8.5 %collective-permute-start.24 = (bf16[64,640]{1,0:T(8,128)(2,1)S(1)}, bf16[64,640]{1,0:T(8,128)(2,1)S(1)}, u32[]{:S(2)}, u32[]{:S(2)}) collective-permute-start(bf16[64,640]{1,0:T(8,128)(2,1)S(1)} %get-tuple-element.95), channel_id=1, source_target_pairs={{0,2},{1,3},{2,0},{3,1},{4,6},{5,7},{6,4},{7,5},{8,10},{9,11},{10,... | collective-permute-start | bytes 245768 | tf_op jit(solution)/shard_map/ffn_rs_2/ppermute | solution.py:718
  70.1 7.9 %collective-permute-start.25 = (bf16[64,640]{1,0:T(8,128)(2,1)S(1)}, bf16[64,640]{1,0:T(8,128)(2,1)S(1)}, u32[]{:S(2)}, u32[]{:S(2)}) collective-permute-start(bf16[64,640]{1,0:T(8,128)(2,1)S(1)} %get-tuple-element.96), channel_id=1, source_target_pairs={{0,1},{1,2},{2,3},{3,0},{4,5},{5,6},{6,7},{7,4},{8,9},{9,10},{10,1... | collective-permute-start | bytes 245768 | tf_op jit(solution)/shard_map/ffn_rs_3/ppermute | solution.py:718
  78.8 4.7 %collective-permute-start.28 = (bf16[64,640]{1,0:T(8,128)(2,1)S(1)}, bf16[64,640]{1,0:T(8,128)(2,1)S(1)}, u32[]{:S(2)}, u32[]{:S(2)}) collective-permute-start(bf16[64,640]{1,0:T(8,128)(2,1)S(1)} %get-tuple-element.99.g0), channel_id=1, source_target_pairs={{0,3},{1,0},{2,1},{3,2},{4,7},{5,4},{6,5},{7,6},{8,11},{9,8},{10,9... | collective-permute-start | bytes 245768 | tf_op jit(solution)/shard_map/gproj_ag_3/ppermute | solution.py:718
  79.8 8.6 %collective-permute-start.27 = (bf16[64,640]{1,0:T(8,128)(2,1)S(1)}, bf16[64,640]{1,0:T(8,128)(2,1)S(1)}, u32[]{:S(2)}, u32[]{:S(2)}) collective-permute-start(bf16[64,640]{1,0:T(8,128)(2,1)S(1)} %get-tuple-element.99.g0), channel_id=1, source_target_pairs={{0,2},{1,3},{2,0},{3,1},{4,6},{5,7},{6,4},{7,5},{8,10},{9,11},{10,... | collective-permute-start | bytes 245768 | tf_op jit(solution)/shard_map/gproj_ag_2/ppermute | solution.py:718
  80.6 7.9 %collective-permute-start.26 = (bf16[64,640]{1,0:T(8,128)(2,1)S(1)}, bf16[64,640]{1,0:T(8,128)(2,1)S(1)}, u32[]{:S(2)}, u32[]{:S(2)}) collective-permute-start(bf16[64,640]{1,0:T(8,128)(2,1)S(1)} %get-tuple-element.99.g0), channel_id=1, source_target_pairs={{0,1},{1,2},{2,3},{3,0},{4,5},{5,6},{6,7},{7,4},{8,9},{9,10},{10,1... | collective-permute-start | bytes 245768 | tf_op jit(solution)/shard_map/gproj_ag_1/ppermute | solution.py:718
  93.1 5.0 %collective-permute-start.29 = (bf16[64,640]{1,0:T(8,128)(2,1)}, bf16[64,640]{1,0:T(8,128)(2,1)}, u32[]{:S(2)}, u32[]{:S(2)}) collective-permute-start(bf16[64,640]{1,0:T(8,128)(2,1)} %get-tuple-element.103), channel_id=1, source_target_pairs={{0,3},{1,0},{2,1},{3,2},{4,7},{5,4},{6,5},{7,6},{8,11},{9,8},{10,9... | collective-permute-start | bytes 245768 | tf_op jit(solution)/shard_map/gffn_rs_1/ppermute | solution.py:718
  94.1 9.0 %collective-permute-start.30 = (bf16[64,640]{1,0:T(8,128)(2,1)}, bf16[64,640]{1,0:T(8,128)(2,1)}, u32[]{:S(2)}, u32[]{:S(2)}) collective-permute-start(bf16[64,640]{1,0:T(8,128)(2,1)} %get-tuple-element.104), channel_id=1, source_target_pairs={{0,2},{1,3},{2,0},{3,1},{4,6},{5,7},{6,4},{7,5},{8,10},{9,11},{10,... | collective-permute-start | bytes 245768 | tf_op jit(solution)/shard_map/gffn_rs_2/ppermute | solution.py:718
  94.9 8.2 %collective-permute-start.31 = (bf16[64,640]{1,0:T(8,128)(2,1)}, bf16[64,640]{1,0:T(8,128)(2,1)}, u32[]{:S(2)}, u32[]{:S(2)}) collective-permute-start(bf16[64,640]{1,0:T(8,128)(2,1)} %get-tuple-element.105), channel_id=1, source_target_pairs={{0,1},{1,2},{2,3},{3,0},{4,5},{5,6},{6,7},{7,4},{8,9},{9,10},{10,1... | collective-permute-start | bytes 245768 | tf_op jit(solution)/shard_map/gffn_rs_3/ppermute | solution.py:718
  108.1 10.1 %collective-permute-start.34 = (bf16[64,640]{1,0:T(8,128)(2,1)S(1)}, bf16[64,640]{1,0:T(8,128)(2,1)S(1)}, u32[]{:S(2)}, u32[]{:S(2)}) collective-permute-start(bf16[64,640]{1,0:T(8,128)(2,1)S(1)} %get-tuple-element.106.a0), channel_id=1, source_target_pairs={{0,3},{1,0},{2,1},{3,2},{4,7},{5,4},{6,5},{7,6},{8,11},{9,8},{10,9... | collective-permute-start | bytes 245768 | tf_op jit(solution)/shard_map/gattn_ag_3/ppermute | solution.py:718
  109.1 9.0 %collective-permute-start.33 = (bf16[64,640]{1,0:T(8,128)(2,1)S(1)}, bf16[64,640]{1,0:T(8,128)(2,1)S(1)}, u32[]{:S(2)}, u32[]{:S(2)}) collective-permute-start(bf16[64,640]{1,0:T(8,128)(2,1)S(1)} %get-tuple-element.106.a0), channel_id=1, source_target_pairs={{0,2},{1,3},{2,0},{3,1},{4,6},{5,7},{6,4},{7,5},{8,10},{9,11},{10,... | collective-permute-start | bytes 245768 | tf_op jit(solution)/shard_map/gattn_ag_2/ppermute | solution.py:718
  110.0 8.2 %collective-permute-start.32 = (bf16[64,640]{1,0:T(8,128)(2,1)S(1)}, bf16[64,640]{1,0:T(8,128)(2,1)S(1)}, u32[]{:S(2)}, u32[]{:S(2)}) collective-permute-start(bf16[64,640]{1,0:T(8,128)(2,1)S(1)} %get-tuple-element.106.a0), channel_id=1, source_target_pairs={{0,1},{1,2},{2,3},{3,0},{4,5},{5,6},{6,7},{7,4},{8,9},{9,10},{10,1... | collective-permute-start | bytes 245768 | tf_op jit(solution)/shard_map/gattn_ag_1/ppermute | solution.py:718
  112.0 74.7 %copy-start.43 = (s32[2]{0:T(128)}, s32[2]{0:T(128)S(1)}, u32[]{:S(2)}) copy-start(s32[2]{0:T(128)S(1)} %pad_add_fusion.1.place) | copy-start | bytes 28
  118.1 14.9 %collective-permute-start.51 = (bf16[320,1536]{1,0:T(8,128)(2,1)S(1)}, bf16[320,1536]{1,0:T(8,128)(2,1)S(1)}, u32[]{:S(2)}, u32[]{:S(2)}) collective-permute-start(bf16[320,1536]{1,0:T(8,128)(2,1)S(1)} %get-tuple-element.147), channel_id=1, source_target_pairs={{0,16},{16,0},{1,17},{17,1},{2,18},{18,2},{3,19},{19,3},{4,20},{20... | collective-permute-start | bytes 2949128 | tf_op jit(solution)/shard_map/early_pair/ppermute | solution.py:718
  124.7 2.5 %collective-permute-start.41 = (bf16[384,1024]{1,0:T(8,128)(2,1)S(1)}, bf16[384,1024]{1,0:T(8,128)(2,1)S(1)}, u32[]{:S(2)}, u32[]{:S(2)}) collective-permute-start(bf16[384,1024]{1,0:T(8,128)(2,1)S(1)} %get-tuple-element.129), channel_id=1, source_target_pairs={{0,16},{16,0},{1,17},{17,1},{2,18},{18,2},{3,19},{19,3},{4,20},{20... | collective-permute-start | bytes 2359304 | tf_op jit(solution)/shard_map/late_pair/ppermute | solution.py:718
  127.9 8.8 %collective-permute-start.42 = (bf16[96,1024]{1,0:T(8,128)(2,1)S(1)}, bf16[96,1024]{1,0:T(8,128)(2,1)S(1)}, u32[]{:S(2)}, u32[]{:S(2)}) collective-permute-start(bf16[96,1024]{1,0:T(8,128)(2,1)S(1)} %get-tuple-element.131), channel_id=1, source_target_pairs={{0,4},{4,8},{8,12},{12,0},{1,5},{5,9},{9,13},{13,1},{2,6},{6,10},{... | collective-permute-start | bytes 589832 | tf_op jit(solution)/shard_map/late_rs_1/ppermute | solution.py:718
  128.6 11.8 %collective-permute-start.43 = (bf16[96,1024]{1,0:T(8,128)(2,1)S(1)}, bf16[96,1024]{1,0:T(8,128)(2,1)S(1)}, u32[]{:S(2)}, u32[]{:S(2)}) collective-permute-start(bf16[96,1024]{1,0:T(8,128)(2,1)S(1)} %get-tuple-element.132), channel_id=1, source_target_pairs={{0,8},{4,12},{8,0},{12,4},{1,9},{5,13},{9,1},{13,5},{2,10},{6,14},... | collective-permute-start | bytes 589832 | tf_op jit(solution)/shard_map/late_rs_2/ppermute | solution.py:718
  130.3 24.0 %collective-permute-start.35 = (bf16[256,512]{1,0:T(8,128)(2,1)S(1)}, bf16[256,512]{1,0:T(8,128)(2,1)S(1)}, u32[]{:S(2)}, u32[]{:S(2)}) collective-permute-start(bf16[256,512]{1,0:T(8,128)(2,1)S(1)} %get-tuple-element.112.g1), channel_id=1, source_target_pairs={{0,12},{4,0},{8,4},{12,8},{1,13},{5,1},{9,5},{13,9},{2,14},{6,2},{... | collective-permute-start | bytes 786440 | tf_op jit(solution)/shard_map/gkv_rs_1/ppermute | solution.py:718
  132.4 21.9 %collective-permute-start.36 = (bf16[256,512]{1,0:T(8,128)(2,1)S(1)}, bf16[256,512]{1,0:T(8,128)(2,1)S(1)}, u32[]{:S(2)}, u32[]{:S(2)}) collective-permute-start(bf16[256,512]{1,0:T(8,128)(2,1)S(1)} %get-tuple-element.113.g2), channel_id=1, source_target_pairs={{0,8},{4,12},{8,0},{12,4},{1,9},{5,13},{9,1},{13,5},{2,10},{6,14},... | collective-permute-start | bytes 786440 | tf_op jit(solution)/shard_map/gkv_rs_2/ppermute | solution.py:718
  132.9 21.3 %collective-permute-start.37 = (bf16[256,512]{1,0:T(8,128)(2,1)S(1)}, bf16[256,512]{1,0:T(8,128)(2,1)S(1)}, u32[]{:S(2)}, u32[]{:S(2)}) collective-permute-start(bf16[256,512]{1,0:T(8,128)(2,1)S(1)} %get-tuple-element.114.g3), channel_id=1, source_target_pairs={{0,4},{4,8},{8,12},{12,0},{1,5},{5,9},{9,13},{13,1},{2,6},{6,10},{... | collective-permute-start | bytes 786440 | tf_op jit(solution)/shard_map/gkv_rs_3/ppermute | solution.py:718
  136.7 15.5 %collective-permute-start.44 = (bf16[96,1024]{1,0:T(8,128)(2,1)S(1)}, bf16[96,1024]{1,0:T(8,128)(2,1)S(1)}, u32[]{:S(2)}, u32[]{:S(2)}) collective-permute-start(bf16[96,1024]{1,0:T(8,128)(2,1)S(1)} %get-tuple-element.133), channel_id=1, source_target_pairs={{0,12},{4,0},{8,4},{12,8},{1,13},{5,1},{9,5},{13,9},{2,14},{6,2},{... | collective-permute-start | bytes 589832 | tf_op jit(solution)/shard_map/late_rs_3/ppermute | solution.py:718
  140.4 32.6 %collective-permute-start.52 = (bf16[80,1536]{1,0:T(8,128)(2,1)S(1)}, bf16[80,1536]{1,0:T(8,128)(2,1)S(1)}, u32[]{:S(2)}, u32[]{:S(2)}) collective-permute-start(bf16[80,1536]{1,0:T(8,128)(2,1)S(1)} %get-tuple-element.149), channel_id=1, source_target_pairs={{0,4},{4,8},{8,12},{12,0},{1,5},{5,9},{9,13},{13,1},{2,6},{6,10},{... | collective-permute-start | bytes 737288 | tf_op jit(solution)/shard_map/early_rs_1/ppermute | solution.py:718
  152.4 13.3 %collective-permute-start.47 = (bf16[96,512]{1,0:T(8,128)(2,1)S(1)}, bf16[96,512]{1,0:T(8,128)(2,1)S(1)}, u32[]{:S(2)}, u32[]{:S(2)}) collective-permute-start(bf16[96,512]{1,0:T(8,128)(2,1)S(1)} %get-tuple-element.135.refs_0_), channel_id=1, source_target_pairs={{0,3},{1,0},{2,1},{3,2},{4,7},{5,4},{6,5},{7,6},{8,11},{9,8},{10,9... | collective-permute-start | bytes 294920 | tf_op jit(solution)/shard_map/late_z_3/ppermute | solution.py:718
  155.3 4.8 %collective-permute-start.38 = (bf16[64,640]{1,0:T(8,128)(2,1)S(1)}, bf16[64,640]{1,0:T(8,128)(2,1)S(1)}, u32[]{:S(2)}, u32[]{:S(2)}) collective-permute-start(bf16[64,640]{1,0:T(8,128)(2,1)S(1)} %get-tuple-element.124), channel_id=1, source_target_pairs={{0,3},{1,0},{2,1},{3,2},{4,7},{5,4},{6,5},{7,6},{8,11},{9,8},{10,9... | collective-permute-start | bytes 245768 | tf_op jit(solution)/shard_map/hidden_rs_1/ppermute | solution.py:718
  156.3 11.6 %collective-permute-start.46 = (bf16[96,512]{1,0:T(8,128)(2,1)S(1)}, bf16[96,512]{1,0:T(8,128)(2,1)S(1)}, u32[]{:S(2)}, u32[]{:S(2)}) collective-permute-start(bf16[96,512]{1,0:T(8,128)(2,1)S(1)} %get-tuple-element.135.refs_0_), channel_id=1, source_target_pairs={{0,2},{1,3},{2,0},{3,1},{4,6},{5,7},{6,4},{7,5},{8,10},{9,11},{10,... | collective-permute-start | bytes 294920 | tf_op jit(solution)/shard_map/late_z_2/ppermute | solution.py:718
  157.0 11.4 %collective-permute-start.45 = (bf16[96,512]{1,0:T(8,128)(2,1)S(1)}, bf16[96,512]{1,0:T(8,128)(2,1)S(1)}, u32[]{:S(2)}, u32[]{:S(2)}) collective-permute-start(bf16[96,512]{1,0:T(8,128)(2,1)S(1)} %get-tuple-element.135.refs_0_), channel_id=1, source_target_pairs={{0,1},{1,2},{2,3},{3,0},{4,5},{5,6},{6,7},{7,4},{8,9},{9,10},{10,1... | collective-permute-start | bytes 294920 | tf_op jit(solution)/shard_map/late_z_1/ppermute | solution.py:718
  160.1 10.1 %collective-permute-start.39 = (bf16[64,640]{1,0:T(8,128)(2,1)S(1)}, bf16[64,640]{1,0:T(8,128)(2,1)S(1)}, u32[]{:S(2)}, u32[]{:S(2)}) collective-permute-start(bf16[64,640]{1,0:T(8,128)(2,1)S(1)} %get-tuple-element.125), channel_id=1, source_target_pairs={{0,2},{1,3},{2,0},{3,1},{4,6},{5,7},{6,4},{7,5},{8,10},{9,11},{10,... | collective-permute-start | bytes 245768 | tf_op jit(solution)/shard_map/hidden_rs_2/ppermute | solution.py:718
  165.6 6.8 %collective-permute-start.40 = (bf16[64,640]{1,0:T(8,128)(2,1)S(1)}, bf16[64,640]{1,0:T(8,128)(2,1)S(1)}, u32[]{:S(2)}, u32[]{:S(2)}) collective-permute-start(bf16[64,640]{1,0:T(8,128)(2,1)S(1)} %get-tuple-element.126), channel_id=1, source_target_pairs={{0,1},{1,2},{2,3},{3,0},{4,5},{5,6},{6,7},{7,4},{8,9},{9,10},{10,1... | collective-permute-start | bytes 245768 | tf_op jit(solution)/shard_map/hidden_rs_3/ppermute | solution.py:718
  167.9 9.9 %collective-permute-start.53 = (bf16[80,1536]{1,0:T(8,128)(2,1)S(1)}, bf16[80,1536]{1,0:T(8,128)(2,1)S(1)}, u32[]{:S(2)}, u32[]{:S(2)}) collective-permute-start(bf16[80,1536]{1,0:T(8,128)(2,1)S(1)} %get-tuple-element.150), channel_id=1, source_target_pairs={{0,8},{4,12},{8,0},{12,4},{1,9},{5,13},{9,1},{13,5},{2,10},{6,14},... | collective-permute-start | bytes 737288 | tf_op jit(solution)/shard_map/early_rs_2/ppermute | solution.py:718
  168.4 9.4 %collective-permute-start.54 = (bf16[80,1536]{1,0:T(8,128)(2,1)S(1)}, bf16[80,1536]{1,0:T(8,128)(2,1)S(1)}, u32[]{:S(2)}, u32[]{:S(2)}) collective-permute-start(bf16[80,1536]{1,0:T(8,128)(2,1)S(1)} %get-tuple-element.151), channel_id=1, source_target_pairs={{0,12},{4,0},{8,4},{12,8},{1,13},{5,1},{9,5},{13,9},{2,14},{6,2},{... | collective-permute-start | bytes 737288 | tf_op jit(solution)/shard_map/early_rs_3/ppermute | solution.py:718
  170.2 16.5 %collective-permute-start.50 = (bf16[96,1024]{1,0:T(8,128)(2,1)S(1)}, bf16[96,1024]{1,0:T(8,128)(2,1)S(1)}, u32[]{:S(2)}, u32[]{:S(2)}) collective-permute-start(bf16[96,1024]{1,0:T(8,128)(2,1)S(1)} %shard_map.284.c0), channel_id=1, source_target_pairs={{0,4},{4,8},{8,12},{12,0},{1,5},{5,9},{9,13},{13,1},{2,6},{6,10},{... | collective-permute-start | bytes 589832 | tf_op jit(solution)/shard_map/late_ag_3/ppermute | solution.py:718
  172.5 14.2 %collective-permute-start.49 = (bf16[96,1024]{1,0:T(8,128)(2,1)S(1)}, bf16[96,1024]{1,0:T(8,128)(2,1)S(1)}, u32[]{:S(2)}, u32[]{:S(2)}) collective-permute-start(bf16[96,1024]{1,0:T(8,128)(2,1)S(1)} %shard_map.284.c0), channel_id=1, source_target_pairs={{0,8},{4,12},{8,0},{12,4},{1,9},{5,13},{9,1},{13,5},{2,10},{6,14},... | collective-permute-start | bytes 589832 | tf_op jit(solution)/shard_map/late_ag_2/ppermute | solution.py:718
  173.0 13.7 %collective-permute-start.48 = (bf16[96,1024]{1,0:T(8,128)(2,1)S(1)}, bf16[96,1024]{1,0:T(8,128)(2,1)S(1)}, u32[]{:S(2)}, u32[]{:S(2)}) collective-permute-start(bf16[96,1024]{1,0:T(8,128)(2,1)S(1)} %shard_map.284.c0), channel_id=1, source_target_pairs={{0,12},{4,0},{8,4},{12,8},{1,13},{5,1},{9,5},{13,9},{2,14},{6,2},{... | collective-permute-start | bytes 589832 | tf_op jit(solution)/shard_map/late_ag_1/ppermute | solution.py:718
  177.9 13.3 %collective-permute-start.57 = (bf16[80,1536]{1,0:T(8,128)(2,1)S(1)}, bf16[80,1536]{1,0:T(8,128)(2,1)S(1)}, u32[]{:S(2)}, u32[]{:S(2)}) collective-permute-start(bf16[80,1536]{1,0:T(8,128)(2,1)S(1)} %shard_map.288.c0), channel_id=1, source_target_pairs={{0,4},{4,8},{8,12},{12,0},{1,5},{5,9},{9,13},{13,1},{2,6},{6,10},{... | collective-permute-start | bytes 737288 | tf_op jit(solution)/shard_map/early_ag_3/ppermute | solution.py:718
  184.5 8.7 %collective-permute-start.56 = (bf16[80,1536]{1,0:T(8,128)(2,1)S(1)}, bf16[80,1536]{1,0:T(8,128)(2,1)S(1)}, u32[]{:S(2)}, u32[]{:S(2)}) collective-permute-start(bf16[80,1536]{1,0:T(8,128)(2,1)S(1)} %shard_map.288.c0), channel_id=1, source_target_pairs={{0,8},{4,12},{8,0},{12,4},{1,9},{5,13},{9,1},{13,5},{2,10},{6,14},... | collective-permute-start | bytes 737288 | tf_op jit(solution)/shard_map/early_ag_2/ppermute | solution.py:718
  186.7 6.5 %collective-permute-start.55 = (bf16[80,1536]{1,0:T(8,128)(2,1)S(1)}, bf16[80,1536]{1,0:T(8,128)(2,1)S(1)}, u32[]{:S(2)}, u32[]{:S(2)}) collective-permute-start(bf16[80,1536]{1,0:T(8,128)(2,1)S(1)} %shard_map.288.c0), channel_id=1, source_target_pairs={{0,12},{4,0},{8,4},{12,8},{1,13},{5,1},{9,5},{13,9},{2,14},{6,2},{... | collective-permute-start | bytes 737288 | tf_op jit(solution)/shard_map/early_ag_1/ppermute | solution.py:718
  (48 other events, 254.3 us)
